TPU v7x, 32 devices: a whole 2x2x4 slice. The times are simulated.
32 devices in a mesh: fsdp: 4 (over z), ctx: 2 (over y), tp: 4 (over x, core).
Axes of the slice: x: 2, y: 2, z: 4, core: 2. Of those that a mesh axis runs over, the one named last changes fastest.
Arguments:
- inputs: bfloat16 [6144, 2048], P(('fsdp', 'ctx')), may hold values from -6 to 6
- loss_sensitivity: bfloat16 [6144, 2048], P(('fsdp', 'ctx')), may hold values from -6 to 6
- parent_block: int32 [4, 6], P('fsdp'), may hold values from -1 to 4, as said below
- adapter_of: int32 [8], replicated, may hold values from 0 to 7, each once
- w_qkv: bfloat16 [3, 2048, 2048], P(None, 'fsdp', 'tp'), may hold values from -0.125 to 0.125
- bias_qv: float32 [2, 2048], P(None, 'tp'), may hold values from -3 to 3
- w_o: bfloat16 [2048, 2048], P('tp', 'fsdp'), may hold values from -1 to 1
- exit_offsets: float32 [2, 2048], replicated, may hold values from -3 to 3
- ln_gain: float32 [2, 2048], replicated, may hold values from 0.5 to 1.5
- ln_bias: float32 [2, 2048], replicated, may hold values from -2 to 2
- w_in: bfloat16 [2048, 8192], P('fsdp', 'tp'), may hold values from -0.125 to 0.125
- hidden_offset_frozen: float32 [8192], P('tp'), may hold values from -3 to 3
- w_out: bfloat16 [8192, 2048], P('tp', 'fsdp'), may hold values from -0.0625 to 0.0625
- a_attn: float32 [4, 8, 2048, 16], replicated, may hold values from -0.25 to 0.25
- b_attn: float32 [4, 8, 16, 2048], replicated, may hold values from -1.5 to 1.5
- a_up: float32 [8, 2048, 16], replicated, may hold values from -0.25 to 0.25
- b_up: float32 [8, 16, 8192], P(None, None, 'tp'), may hold values from -1.5 to 1.5
- a_down: float32 [8, 8192, 16], P(None, 'tp'), may hold values from -0.125 to 0.125
- b_down: float32 [8, 16, 2048], replicated, may hold values from -1.5 to 1.5
Outputs:
- layer_out: bfloat16 [6144, 2048], P(('fsdp', 'ctx'))
- grad_inputs: bfloat16 [6144, 2048], P(('fsdp', 'ctx'))
- grad_a_attn: float32 [4, 8, 2048, 16], P(None, None, ('tp', 'fsdp', 'ctx'))
- grad_b_attn: float32 [4, 8, 16, 2048], P(None, None, None, ('tp', 'fsdp', 'ctx'))
- grad_a_up: float32 [8, 2048, 16], P(None, ('tp', 'fsdp', 'ctx'))
- grad_b_up: float32 [8, 16, 8192], P(None, None, ('tp', 'fsdp', 'ctx'))
- grad_a_down: float32 [8, 8192, 16], P(None, ('tp', 'fsdp', 'ctx'))
- grad_b_down: float32 [8, 16, 2048], P(None, None, ('tp', 'fsdp', 'ctx'))
Inputs may be any that keep to these rules, and one draw needn't show every extreme that they name: parent_block[g, b] is -1 where block b is the first block of one of group g's 2 trees, else an earlier block of the same tree; trees are numbered by the order of their first blocks. adapter_of[g * 2 + t] is the adapter set of tree t of group g; the entries are a permutation.
All inputs are finite; a program needn't handle non-finite values.
Results may differ from a plain program's by a relative error of at most 0.025.
Values may be sent and summed in bfloat16 or wider, within the bound.
No kernel may reach another device: no remote copies, remote signals or barrier semaphores. Data moves between devices by JAX's collectives and lax.ppermute only.
A program may use at most 256 MiB of HBM per device.

v0:
```python
from functools import partial

import jax
import jax.numpy as jnp
from jax import lax
from jax.sharding import PartitionSpec as P

HD = 128
RANK = 16
ADAPTERS = 8
TREES_GROUP = 2
BLOCK = 256


layer_eps = 1e-05
adaptive_factor = 0.5
neg_fill = -1e30
highest = lax.Precision.HIGHEST


def layer_norm(vector_rows, gain_row, shift_row):
    centre = vector_rows - jnp.mean(vector_rows, axis=-1, keepdims=True)
    spread = jnp.mean(centre * centre, axis=-1, keepdims=True)
    return centre * lax.rsqrt(spread + layer_eps) * gain_row + shift_row


def ancestry(parents):
    block_total = parents.shape[0]
    position = jnp.arange(block_total, dtype=jnp.int32)

    def extend(block_step, carry):
        reach, current, root_block = carry
        valid = current >= 0
        reach = reach | valid[:, None] & (position[None, :] == current[:, None])
        root_block = jnp.where(valid, current, root_block)
        upward = jnp.take(parents, jnp.maximum(current, 0), axis=0)
        current = jnp.where(valid, upward, -1)
        return (reach, current, root_block)

    start = (jnp.zeros((block_total, block_total), dtype=bool), position, position)
    reach, current, root_block = lax.fori_loop(0, block_total, extend, start)
    root_order = jnp.cumsum((parents < 0).astype(jnp.int32)) - 1
    tree_slot = jnp.take(root_order, root_block, axis=0)
    return (reach.astype(jnp.float32), tree_slot)


def multiplied_result_value(operand, other):
    return jnp.dot(operand, other, preferred_element_type=jnp.float32)


def hidden_entries_lines(operand, other):
    return lax.dot_general(
        operand, other, (((0,), (0,)), ((), ())), preferred_element_type=jnp.float32
    )


def multiplied_flipped(operand, other):
    return lax.dot_general(
        operand, other, (((1,), (1,)), ((), ())), preferred_element_type=jnp.float32
    )


def down_matrix(down_pair):
    return jnp.transpose(down_pair, (1, 0, 2)).reshape(down_pair.shape[1], -1).astype(jnp.bfloat16)


def expanding_factor(up_pair):
    return up_pair.reshape(-1, up_pair.shape[2]).astype(jnp.bfloat16)


def spread_pair(grad_pair, placing):
    return jnp.einsum("ta,t...->a...", placing, grad_pair, precision=highest)


def grad_block(
    query_heads, grad_heads, key_low, value_low, allowed, log_rows, dot_rows, score_scale
):
    key_heads = key_low.reshape(query_heads.shape[0], query_heads.shape[1], query_heads.shape[2])
    value_heads = value_low.reshape(key_heads.shape)
    scores = jnp.where(
        allowed,
        jnp.einsum("qhd,khd->hqk", query_heads, key_heads, preferred_element_type=jnp.float32)
        * score_scale,
        neg_fill,
    )
    probabilities = jnp.where(allowed, jnp.exp(scores - log_rows[:, :, None]), 0.0)
    grad_probs = jnp.einsum(
        "qhd,khd->hqk", grad_heads, value_heads, preferred_element_type=jnp.float32
    )
    grad_scores = (probabilities * (grad_probs - dot_rows[:, :, None])).astype(jnp.bfloat16)
    return (probabilities, grad_scores, key_heads)


def body(
    inputs,
    loss_sensitivity,
    parent_block,
    adapter_of,
    w_qkv,
    bias_qv,
    w_o,
    exit_offsets,
    ln_gain,
    ln_bias,
    w_in,
    hidden_offset_frozen,
    w_out,
    a_attn,
    b_attn,
    a_up,
    b_up,
    a_down,
    b_down,
):
    group_index = lax.axis_index("fsdp")
    context_index = lax.axis_index("ctx")
    tensor_index = lax.axis_index("tp")
    tok_rows = inputs.shape[0]
    local_width = w_qkv.shape[2]
    head_local = local_width // HD
    blocks_here = tok_rows // BLOCK
    score_scale = HD ** (-0.5)
    ancestors, tree_slot = ancestry(parent_block[0])
    first_block = context_index * blocks_here
    slot_here = lax.dynamic_slice_in_dim(tree_slot, first_block, blocks_here)
    slot_tok = jnp.repeat(slot_here, BLOCK, total_repeat_length=tok_rows)
    adapter_pair = lax.dynamic_slice_in_dim(adapter_of, group_index * TREES_GROUP, TREES_GROUP)
    select_tok = (slot_tok[:, None] == jnp.arange(TREES_GROUP, dtype=jnp.int32)[None, :]).astype(
        jnp.float32
    )
    pick_broadened = jnp.repeat(select_tok, RANK, axis=1, total_repeat_length=TREES_GROUP * RANK)
    placing = (adapter_pair[:, None] == jnp.arange(ADAPTERS, dtype=jnp.int32)[None, :]).astype(
        jnp.float32
    )
    reach_rows = lax.dynamic_slice_in_dim(ancestors, first_block, blocks_here, 0)
    query_pos = context_index * tok_rows + jnp.arange(tok_rows, dtype=jnp.int32)

    def local_lanes(matrix):
        return lax.dynamic_slice_in_dim(
            matrix, tensor_index * local_width, local_width, matrix.ndim - 1
        )

    def visible(key_start, key_rows):
        key_pos = key_start + jnp.arange(key_rows, dtype=jnp.int32)
        columns = lax.dynamic_slice_in_dim(reach_rows, key_start // BLOCK, key_rows // BLOCK, 1)
        table = jnp.repeat(
            jnp.repeat(columns, BLOCK, axis=0, total_repeat_length=tok_rows),
            BLOCK,
            axis=1,
            total_repeat_length=key_rows,
        )
        causal = (query_pos[:, None] // BLOCK != key_pos[None, :] // BLOCK) | (
            key_pos[None, :] <= query_pos[:, None]
        )
        return (table > 0.5) & causal

    def head_scores(query_low, key_low):
        return (
            jnp.einsum(
                "qhd,khd->hqk",
                query_low.reshape(tok_rows, head_local, HD),
                key_low.reshape(-1, head_local, HD),
                preferred_element_type=jnp.float32,
            )
            * score_scale
        )

    gathered = (
        lax.all_gather(w_qkv, "fsdp", axis=1, tiled=True),
        lax.all_gather(w_o, "fsdp", axis=1, tiled=True),
        lax.all_gather(w_in, "fsdp", axis=0, tiled=True),
        lax.all_gather(w_out, "fsdp", axis=1, tiled=True),
    )
    wqkv_full, wo_full, hidden_map_entire, wout_full = gathered
    a_qkv_cat = jnp.concatenate(
        [
            down_matrix(a_attn[0][adapter_pair]),
            down_matrix(a_attn[1][adapter_pair]),
            down_matrix(a_attn[2][adapter_pair]),
        ],
        axis=1,
    )
    query_key_offsets = local_lanes(b_attn[:3])[:, adapter_pair]
    a_o_rows = down_matrix(
        lax.dynamic_slice_in_dim(a_attn[3], tensor_index * local_width, local_width, 1)[
            adapter_pair
        ]
    )
    mixing_offset_entire = expanding_factor(b_attn[3][adapter_pair])
    a_up_cat = down_matrix(a_up[adapter_pair])
    expand_offset_lanes = expanding_factor(b_up[adapter_pair])
    a_down_rows = down_matrix(a_down[adapter_pair])
    shrink_factor_entire = expanding_factor(b_down[adapter_pair])
    piece_lines = inputs.astype(jnp.float32)
    normed_f, ln_one_back = jax.vjp(
        partial(layer_norm, gain_row=ln_gain[0], shift_row=ln_bias[0]), piece_lines
    )
    normed_low = normed_f.astype(jnp.bfloat16)
    down_raw = multiplied_result_value(normed_low, a_qkv_cat).reshape(
        tok_rows, 3, TREES_GROUP * RANK
    )
    query_key_reduced = (down_raw * pick_broadened[:, None, :]).astype(jnp.bfloat16)
    queries = (
        multiplied_result_value(normed_low, wqkv_full[0])
        + bias_qv[0]
        + adaptive_factor
        * multiplied_result_value(query_key_reduced[:, 0], expanding_factor(query_key_offsets[0]))
    ).astype(jnp.bfloat16)
    key_vectors = (
        multiplied_result_value(normed_low, wqkv_full[1])
        + adaptive_factor
        * multiplied_result_value(query_key_reduced[:, 1], expanding_factor(query_key_offsets[1]))
    ).astype(jnp.bfloat16)
    values = (
        multiplied_result_value(normed_low, wqkv_full[2])
        + bias_qv[1]
        + adaptive_factor
        * multiplied_result_value(query_key_reduced[:, 2], expanding_factor(query_key_offsets[2]))
    ).astype(jnp.bfloat16)
    start_state = (
        jnp.full((head_local, tok_rows), neg_fill, jnp.float32),
        jnp.zeros((head_local, tok_rows), jnp.float32),
        jnp.zeros((tok_rows, head_local, HD), jnp.float32),
    )
    fetched_keys = lax.all_gather(key_vectors, "ctx", axis=0, tiled=True)
    fetched_values = lax.all_gather(values, "ctx", axis=0, tiled=True)
    block_count = fetched_keys.shape[0] // tok_rows

    def one_step(block_step, running):
        running_max, running_sum, running_out = running
        offset = block_step * tok_rows
        key_low = lax.dynamic_slice_in_dim(fetched_keys, offset, tok_rows, 0)
        value_low = lax.dynamic_slice_in_dim(fetched_values, offset, tok_rows, 0)
        allowed = visible(offset, tok_rows)[None]
        scores = jnp.where(allowed, head_scores(queries, key_low), neg_fill)
        new_max = jnp.maximum(running_max, jnp.max(scores, axis=2))
        weights = jnp.where(allowed, jnp.exp(scores - new_max[:, :, None]), 0.0)
        fade = jnp.exp(running_max - new_max)
        running_sum = running_sum * fade + jnp.sum(weights, axis=2)
        mixed_part = jnp.einsum(
            "hqk,khd->qhd",
            weights.astype(jnp.bfloat16),
            value_low.reshape(tok_rows, head_local, HD),
            preferred_element_type=jnp.float32,
        )
        running_out = running_out * jnp.transpose(fade)[:, :, None] + mixed_part
        return (new_max, running_sum, running_out)

    running_max, running_sum, running_out = lax.fori_loop(0, block_count, one_step, start_state)
    attended_f = (running_out / jnp.transpose(running_sum)[:, :, None]).reshape(
        tok_rows, local_width
    )
    log_total = running_max + jnp.log(running_sum)
    attended_low = attended_f.astype(jnp.bfloat16)
    branch_part = multiplied_result_value(attended_low, wo_full)
    down_o_part = multiplied_result_value(attended_low, a_o_rows)
    residual_addend, down_o_sum = (
        lax.psum(branch_part.astype(jnp.bfloat16), "tp").astype(jnp.float32),
        lax.psum(down_o_part.astype(jnp.bfloat16), "tp").astype(jnp.float32),
    )
    mixing_reduced_cheap = (down_o_sum * pick_broadened).astype(jnp.bfloat16)
    hidden_state = (
        piece_lines
        + residual_addend
        + exit_offsets[0]
        + adaptive_factor * multiplied_result_value(mixing_reduced_cheap, mixing_offset_entire)
    )
    normed_two_f, ln_two_back = jax.vjp(
        partial(layer_norm, gain_row=ln_gain[1], shift_row=ln_bias[1]), hidden_state
    )
    standardized_later_cheap = normed_two_f.astype(jnp.bfloat16)
    expand_reduced_cheap = (
        multiplied_result_value(standardized_later_cheap, a_up_cat) * pick_broadened
    ).astype(jnp.bfloat16)
    pre_act = (
        multiplied_result_value(standardized_later_cheap, hidden_map_entire)
        + hidden_offset_frozen
        + adaptive_factor * multiplied_result_value(expand_reduced_cheap, expand_offset_lanes)
    )
    hidden_f, gelu_back = jax.vjp(partial(jax.nn.gelu, approximate=False), pre_act)
    hidden_low = hidden_f.astype(jnp.bfloat16)
    out_part = multiplied_result_value(hidden_low, wout_full)
    down_down_part = multiplied_result_value(hidden_low, a_down_rows)
    exit_accumulated, down_down_sum = (
        lax.psum(out_part.astype(jnp.bfloat16), "tp").astype(jnp.float32),
        lax.psum(down_down_part.astype(jnp.bfloat16), "tp").astype(jnp.float32),
    )
    shrink_reduced_cheap = (down_down_sum * pick_broadened).astype(jnp.bfloat16)
    returned_value = (
        hidden_state
        + exit_accumulated
        + exit_offsets[1]
        + adaptive_factor * multiplied_result_value(shrink_reduced_cheap, shrink_factor_entire)
    )
    layer_out = returned_value.astype(jnp.bfloat16)
    wqkv_back, wo_back, win_back, wout_back = (
        lax.all_gather(w_qkv, "fsdp", axis=1, tiled=True),
        lax.all_gather(w_o, "fsdp", axis=1, tiled=True),
        lax.all_gather(w_in, "fsdp", axis=0, tiled=True),
        lax.all_gather(w_out, "fsdp", axis=1, tiled=True),
    )
    grad_result = loss_sensitivity.astype(jnp.float32)
    shrink_offset_couple_deriv = adaptive_factor * hidden_entries_lines(
        shrink_reduced_cheap, local_lanes(loss_sensitivity)
    )
    shrink_reduced_deriv = (
        adaptive_factor
        * multiplied_flipped(loss_sensitivity, shrink_factor_entire)
        * pick_broadened
    ).astype(jnp.bfloat16)
    grad_hidden = multiplied_flipped(loss_sensitivity, wout_back) + multiplied_flipped(
        shrink_reduced_deriv, a_down_rows
    )
    grad_a_down_pair = hidden_entries_lines(hidden_low, shrink_reduced_deriv)
    before_gelu_deriv = gelu_back(grad_hidden)[0].astype(jnp.bfloat16)
    expand_offset_couple_deriv = adaptive_factor * hidden_entries_lines(
        expand_reduced_cheap, before_gelu_deriv
    )
    expand_reduced_deriv_piece = adaptive_factor * multiplied_flipped(
        before_gelu_deriv, expand_offset_lanes
    )
    grad_normed_two_part = multiplied_flipped(before_gelu_deriv, win_back)
    grad_normed_two_sum, grad_down_up_sum = (
        lax.psum(grad_normed_two_part.astype(jnp.bfloat16), "tp").astype(jnp.float32),
        lax.psum(expand_reduced_deriv_piece.astype(jnp.bfloat16), "tp").astype(jnp.float32),
    )
    grad_down_up = (grad_down_up_sum * pick_broadened).astype(jnp.bfloat16)
    grad_normed_two = grad_normed_two_sum + multiplied_flipped(grad_down_up, a_up_cat)
    grad_a_up_pair = hidden_entries_lines(local_lanes(standardized_later_cheap), grad_down_up)
    grad_middle = grad_result + ln_two_back(grad_normed_two)[0]
    residual_deriv = grad_middle.astype(jnp.bfloat16)
    mixing_offset_couple_deriv = adaptive_factor * hidden_entries_lines(
        mixing_reduced_cheap, local_lanes(residual_deriv)
    )
    mixing_reduced_deriv = (
        adaptive_factor * multiplied_flipped(residual_deriv, mixing_offset_entire) * pick_broadened
    ).astype(jnp.bfloat16)
    grad_attended = (
        multiplied_flipped(residual_deriv, wo_back)
        + multiplied_flipped(mixing_reduced_deriv, a_o_rows)
    ).astype(jnp.bfloat16)
    grad_a_o_pair = hidden_entries_lines(attended_low, mixing_reduced_deriv)
    grad_attended_heads = grad_attended.reshape(tok_rows, head_local, HD)
    row_dot = jnp.transpose(
        jnp.sum(
            (grad_attended.astype(jnp.float32) * attended_f).reshape(tok_rows, head_local, HD),
            axis=2,
        )
    )
    keys_all, values_all = (
        lax.all_gather(key_vectors, "ctx", axis=0, tiled=True),
        lax.all_gather(values, "ctx", axis=0, tiled=True),
    )
    shard_total = keys_all.shape[0] // tok_rows
    query_heads = queries.reshape(tok_rows, head_local, HD)

    def back_step(grad_query, block_step):
        offset = block_step * tok_rows
        key_low = lax.dynamic_slice_in_dim(keys_all, offset, tok_rows, 0)
        value_low = lax.dynamic_slice_in_dim(values_all, offset, tok_rows, 0)
        allowed = visible(offset, tok_rows)[None]
        probabilities, grad_scores, key_heads = grad_block(
            query_heads,
            grad_attended_heads,
            key_low,
            value_low,
            allowed,
            log_total,
            row_dot,
            score_scale,
        )
        grad_query = (
            grad_query
            + jnp.einsum("hqk,khd->qhd", grad_scores, key_heads, preferred_element_type=jnp.float32)
            * score_scale
        )
        grad_key = (
            jnp.einsum("hqk,qhd->khd", grad_scores, query_heads, preferred_element_type=jnp.float32)
            * score_scale
        )
        grad_value = jnp.einsum(
            "hqk,qhd->khd",
            probabilities.astype(jnp.bfloat16),
            grad_attended_heads,
            preferred_element_type=jnp.float32,
        )
        return (
            grad_query,
            (grad_key.reshape(tok_rows, local_width), grad_value.reshape(tok_rows, local_width)),
        )

    grad_query_sum, (key_terms, value_terms) = lax.scan(
        back_step,
        jnp.zeros((tok_rows, head_local, HD), jnp.float32),
        jnp.arange(shard_total, dtype=jnp.int32),
    )
    key_terms = key_terms.reshape(shard_total * tok_rows, local_width)
    value_terms = value_terms.reshape(shard_total * tok_rows, local_width)
    grad_key_sum, grad_value_sum = (
        lax.psum_scatter(
            key_terms.astype(jnp.bfloat16), "ctx", scatter_dimension=0, tiled=True
        ).astype(jnp.float32),
        lax.psum_scatter(
            value_terms.astype(jnp.bfloat16), "ctx", scatter_dimension=0, tiled=True
        ).astype(jnp.float32),
    )
    query_key_deriv = (
        grad_query_sum.reshape(tok_rows, local_width).astype(jnp.bfloat16),
        grad_key_sum.astype(jnp.bfloat16),
        grad_value_sum.astype(jnp.bfloat16),
    )
    grad_b_qkv_pairs = [
        adaptive_factor
        * hidden_entries_lines(
            query_key_reduced[:, which_linear_map], query_key_deriv[which_linear_map]
        )
        for which_linear_map in range(3)
    ]
    grad_down_qkv_part = jnp.stack(
        [
            adaptive_factor
            * multiplied_flipped(
                query_key_deriv[which_linear_map],
                expanding_factor(query_key_offsets[which_linear_map]),
            )
            for which_linear_map in range(3)
        ],
        axis=1,
    ).reshape(tok_rows, -1)
    grad_normed_part = (
        multiplied_flipped(query_key_deriv[0], wqkv_back[0])
        + multiplied_flipped(query_key_deriv[1], wqkv_back[1])
        + multiplied_flipped(query_key_deriv[2], wqkv_back[2])
    )
    grad_normed_sum, grad_down_qkv_sum = (
        lax.psum(grad_normed_part.astype(jnp.bfloat16), "tp").astype(jnp.float32),
        lax.psum(grad_down_qkv_part.astype(jnp.bfloat16), "tp").astype(jnp.float32),
    )
    grad_down_qkv = (
        (grad_down_qkv_sum.reshape(tok_rows, 3, TREES_GROUP * RANK) * pick_broadened[:, None, :])
        .astype(jnp.bfloat16)
        .reshape(tok_rows, -1)
    )
    grad_normed = grad_normed_sum + multiplied_flipped(grad_down_qkv, a_qkv_cat)
    grad_inputs = (grad_middle + ln_one_back(grad_normed)[0]).astype(jnp.bfloat16)
    grad_a_qkv_pair = hidden_entries_lines(local_lanes(normed_low), grad_down_qkv)
    grad_a_qkv_pair = jnp.transpose(
        grad_a_qkv_pair.reshape(local_width, 3, TREES_GROUP, RANK), (1, 2, 0, 3)
    )
    grad_a_o_term = spread_pair(
        jnp.transpose(grad_a_o_pair.reshape(local_width, TREES_GROUP, RANK), (1, 0, 2)), placing
    )
    grad_a_attn_term = jnp.concatenate(
        [
            jnp.einsum("ta,itdr->iadr", placing, grad_a_qkv_pair, precision=highest),
            grad_a_o_term[None],
        ],
        axis=0,
    )
    grad_b_attn_term = jnp.stack(
        [
            spread_pair(grad_b_qkv_pairs[0].reshape(TREES_GROUP, RANK, local_width), placing),
            spread_pair(grad_b_qkv_pairs[1].reshape(TREES_GROUP, RANK, local_width), placing),
            spread_pair(grad_b_qkv_pairs[2].reshape(TREES_GROUP, RANK, local_width), placing),
            spread_pair(
                mixing_offset_couple_deriv.reshape(TREES_GROUP, RANK, local_width), placing
            ),
        ],
        axis=0,
    )
    grad_a_up_term = spread_pair(
        jnp.transpose(grad_a_up_pair.reshape(local_width, TREES_GROUP, RANK), (1, 0, 2)), placing
    )
    grad_b_up_term = spread_pair(expand_offset_couple_deriv.reshape(TREES_GROUP, RANK, -1), placing)
    grad_a_down_term = spread_pair(
        jnp.transpose(grad_a_down_pair.reshape(-1, TREES_GROUP, RANK), (1, 0, 2)), placing
    )
    grad_b_down_term = spread_pair(
        shrink_offset_couple_deriv.reshape(TREES_GROUP, RANK, local_width), placing
    )
    grad_outputs = (
        lax.psum_scatter(
            grad_a_attn_term.astype(jnp.bfloat16), ("fsdp", "ctx"), scatter_dimension=2, tiled=True
        ).astype(jnp.float32),
        lax.psum_scatter(
            grad_b_attn_term.astype(jnp.bfloat16), ("fsdp", "ctx"), scatter_dimension=3, tiled=True
        ).astype(jnp.float32),
        lax.psum_scatter(
            grad_a_up_term.astype(jnp.bfloat16), ("fsdp", "ctx"), scatter_dimension=1, tiled=True
        ).astype(jnp.float32),
        lax.psum_scatter(
            grad_b_up_term.astype(jnp.bfloat16), ("fsdp", "ctx"), scatter_dimension=2, tiled=True
        ).astype(jnp.float32),
        lax.psum_scatter(
            grad_a_down_term.astype(jnp.bfloat16), ("fsdp", "ctx"), scatter_dimension=1, tiled=True
        ).astype(jnp.float32),
        lax.psum_scatter(
            grad_b_down_term.astype(jnp.bfloat16), ("fsdp", "ctx"), scatter_dimension=2, tiled=True
        ).astype(jnp.float32),
    )
    return (
        layer_out,
        grad_inputs,
        grad_outputs[0],
        grad_outputs[1],
        grad_outputs[2],
        grad_outputs[3],
        grad_outputs[4],
        grad_outputs[5],
    )


def solution(mesh):
    in_specs = (
        P(("fsdp", "ctx"), None),
        P(("fsdp", "ctx"), None),
        P("fsdp", None),
        P(),
        P(None, "fsdp", "tp"),
        P(None, "tp"),
        P("tp", "fsdp"),
        P(),
        P(),
        P(),
        P("fsdp", "tp"),
        P("tp"),
        P("tp", "fsdp"),
        P(),
        P(),
        P(),
        P(None, None, "tp"),
        P(None, "tp", None),
        P(),
    )
    out_specs = (
        P(("fsdp", "ctx"), None),
        P(("fsdp", "ctx"), None),
        P(None, None, ("tp", "fsdp", "ctx"), None),
        P(None, None, None, ("tp", "fsdp", "ctx")),
        P(None, ("tp", "fsdp", "ctx"), None),
        P(None, None, ("tp", "fsdp", "ctx")),
        P(None, ("tp", "fsdp", "ctx"), None),
        P(None, None, ("tp", "fsdp", "ctx")),
    )
    return jax.shard_map(body, mesh=mesh, in_specs=in_specs, out_specs=out_specs, check_vma=False)
```

profile of v0, /device:TPU:9, one launch (start us, length us, event | category | flops | bytes accessed | tf_op | source)
XLA Modules:
  0.0 1418.2 jit_solution(12114626538770693673)
XLA Ops:
  36.2 87.1 %all-gather.7.cloned.1.call-done = bf16[3,2048,512]{2,1,0:T(8,128)(2,1)} async-done(((bf16[3,512,512]{2,1,0:T(8,128)(2,1)}), bf16[3,2048,512]{2,1,0:T(8,128)(2,1)}) %all-gather.7.cloned.1.call-update) | async-done | bytes 6291472 | tf_op jit(solution)/shard_map/all_gather | solution.py:169
  141.4 16.0 %all-gather.11.cloned.1.call-done = bf16[1536,512]{1,0:T(8,128)(2,1)} async-done(((bf16[768,512]{1,0:T(8,128)(2,1)}), bf16[1536,512]{1,0:T(8,128)(2,1)}) %all-gather.11.cloned.1.call-update) | async-done | bytes 1572880 | tf_op jit(solution)/shard_map/all_gather | solution.py:226
  160.1 26.0 %all-gather.9.cloned.1.call-done = bf16[1536,512]{1,0:T(8,128)(2,1)} async-done(((bf16[768,512]{1,0:T(8,128)(2,1)}), bf16[1536,512]{1,0:T(8,128)(2,1)}) %all-gather.9.cloned.1.call-update) | async-done | bytes 1572880 | tf_op jit(solution)/shard_map/all_gather | solution.py:225
  188.8 49.6 %while.67 = (s32[]{:T(128)}, f32[4,768]{1,0:T(4,128)S(1)}, f32[4,768]{1,0:T(4,128)S(1)}, f32[768,4,128]{0,2,1:T(8,128)}, f32[3,6]{1,0:T(4,128)S(1)}, /*index=5*/...) while((s32[]{:T(128)}, f32[4,768]{1,0:T(4,128)S(1)}, ...), condition=%wide.region_8.12_spmd.clone.clone.clone, body=%wide.region_5.11_spmd.clone.clone.clone.sunk | while | flops 1242804736 | bytes 86787112 | solution.py:249
  263.1 12.6 psum.57
  275.6 40.1 %all-reduce.7.cloned.1.call-done = bf16[768,2048]{1,0:T(8,128)(2,1)} async-done(((bf16[768,2048]{1,0:T(8,128)(2,1)}), bf16[768,2048]{1,0:T(8,128)(2,1)}) %all-reduce.7.cloned.1.call-update) | async-done | bytes 3145744 | tf_op jit(solution)/shard_map/psum | solution.py:258
  325.7 138.6 %all-gather.15.cloned.1.call-done = bf16[2048,2048]{1,0:T(8,128)(2,1)} async-done(((bf16[512,2048]{1,0:T(8,128)(2,1)}), bf16[2048,2048]{1,0:T(8,128)(2,1)}) %all-gather.15.cloned.1.call-update) | async-done | bytes 8388624 | tf_op jit(solution)/shard_map/all_gather | solution.py:171
  474.3 16.8 %multiply_convert_fusion = (bf16[768,2048]{1,0:T(8,128)(2,1)}, f32[768,2048]{1,0:T(8,128)}, f32[768,2048]{1,0:T(8,128)}) fusion(bf16[768,32]{0,1:T(8,128)(2,1)S(1)} %fusion.89, bf16[32,2048]{1,0:T(8,128)(2,1)S(1)} %bitcast.460, f32[768,2048]{1,0:T(8,128)S(1)} %fusion.163, f32[2048]{0:T(1024)S(1)} %copy-done.96), kind=kOutput, calls=%fused_computation.145 | convolution fusion | flops 207618048 | bytes 22208512 | tf_op jit(solution)/shard_map/dot_general | solution.py:48
  491.1 122.7 %all-gather.17.cloned.1.call-done = bf16[2048,2048]{1,0:T(8,128)(2,1)} async-done(((bf16[2048,512]{1,0:T(8,128)(2,1)}), bf16[2048,2048]{1,0:T(8,128)(2,1)}) %all-gather.17.cloned.1.call-update) | async-done | bytes 8388624 | tf_op jit(solution)/shard_map/all_gather | solution.py:172
  632.6 12.0 convolution_convert_fusion
  645.8 18.2 %all-reduce.11.cloned.1.call-done = (bf16[768,32]{0,1:T(8,128)(2,1)}, bf16[768,32]{0,1:T(8,128)(2,1)}) async-done(((bf16[768,32]{0,1:T(8,128)(2,1)}, bf16[768,32]{0,1:T(8,128)(2,1)}), (bf16[768,32]{0,1:T(8,128)(2,1)}, bf16[768,32]{0,1:T(8,128)(2,1)})) %all-reduce.11.cloned.1.call-update) | async-done | bytes 98320 | tf_op jit(solution)/shard_map/psum | solution.py:325
  664.0 71.9 %all-reduce.9.cloned.1.call-done = bf16[768,2048]{1,0:T(8,128)(2,1)} async-done(((bf16[768,2048]{1,0:T(8,128)(2,1)}), bf16[768,2048]{1,0:T(8,128)(2,1)}) %all-reduce.9.cloned.1.call-update) | async-done | bytes 3145744 | tf_op jit(solution)/shard_map/psum | solution.py:324
  751.6 64.2 %while.68 = (s32[]{:T(128)}, f32[768,4,128]{0,2,1:T(8,128)}, bf16[2,768,512]{2,1,0:T(8,128)(2,1)}, bf16[2,768,512]{2,1,0:T(8,128)(2,1)}, s32[2]{0:T(128)S(1)}, /...) while((s32[]{:T(128)}, f32[768,4,128]{0,2,1:T(8,128)}, ...), condition=%wide.region_21.25_spmd.clone.clone.clone, body=%wide.region_20.24_spmd.clone.clone.clone.sunk | while | flops 3053152768 | bytes 154458400 | solution.py:392
  838.9 12.2 convolution_convert_fusion.1
  872.5 11.8 copy.146
  884.3 13.6 reshape.1031
  910.0 23.7 %reduce-scatter.29.cloned.1.call-done = bf16[64,128]{1,0:T(8,128)(2,1)} async-done(((bf16[512,128]{1,0:T(8,128)(2,1)}), bf16[64,128]{1,0:T(8,128)(2,1)}) %reduce-scatter.29.cloned.1.call-update) | async-done | bytes 16400
  935.6 62.2 %reduce-scatter.31.cloned.1.call-done = bf16[64,128]{1,0:T(8,128)(2,1)} async-done(((bf16[512,128]{1,0:T(8,128)(2,1)}), bf16[64,128]{1,0:T(8,128)(2,1)}) %reduce-scatter.31.cloned.1.call-update) | async-done | bytes 16400
  999.8 63.1 %reduce-scatter.21.cloned.1.call-done = bf16[8,16,256]{2,0,1:T(8,128)(2,1)} async-done(((bf16[8,16,2048]{2,0,1:T(8,128)(2,1)}), bf16[8,16,256]{2,0,1:T(8,128)(2,1)}) %reduce-scatter.21.cloned.1.call-update) | async-done | bytes 65552 | tf_op jit(solution)/shard_map/reduce_scatter | solution.py:491
  1064.4 63.1 %reduce-scatter.23.cloned.1.call-done = bf16[8,256,16]{1,0,2:T(8,128)(2,1)} async-done(((bf16[8,2048,16]{1,0,2:T(8,128)(2,1)}), bf16[8,256,16]{1,0,2:T(8,128)(2,1)}) %reduce-scatter.23.cloned.1.call-update) | async-done | bytes 65552 | tf_op jit(solution)/shard_map/reduce_scatter | solution.py:494
  1129.7 62.3 %reduce-scatter.27.cloned.1.call-done = bf16[64,512]{1,0:T(8,128)(2,1)} async-done(((bf16[512,512]{1,0:T(8,128)(2,1)}), bf16[64,512]{1,0:T(8,128)(2,1)}) %reduce-scatter.27.cloned.1.call-update) | async-done | bytes 65552
  1196.0 122.4 %all-reduce.13.cloned.1.call-done = (bf16[768,96]{0,1:T(8,128)(2,1)}, bf16[768,2048]{1,0:T(8,128)(2,1)}, bf16[768,2048]{1,0:T(8,128)(2,1)}) async-done(((bf16[768,96]{0,1:T(8,128)(2,1)}, bf16[768,2048]{1,0:T(8,128)(2,1)}, bf16[768,2048]{1,0:T(8,128)(2,1)}), (bf16[768,96]{0,1:T(8,128)(2,1)}, bf16[768,2048]{1,0:T(8,128)(2,1)}, bf16[768,2048]{1,0:T(8,128)(2,1)})) %all-reduce.13.cloned.1.call-update) | async-done | bytes 6438928 | tf_op jit(solution)/shard_map/psum | solution.py:437
  1333.3 13.6 reshape.1029
  1362.2 44.9 %reduce-scatter.25.cloned.1.call-done = bf16[64,512]{1,0:T(8,128)(2,1)} async-done(((bf16[512,512]{1,0:T(8,128)(2,1)}), bf16[64,512]{1,0:T(8,128)(2,1)}) %reduce-scatter.25.cloned.1.call-update) | async-done | bytes 65552
  (531 shorter events, 349.6 us)
Async XLA Ops:
  7.2 246.5 %copy-start = (f32[8,2048,16]{1,2,0:T(8,128)S(1)}, f32[8,2048,16]{1,2,0:T(8,128)}, u32[]{:S(2)}) copy-start(f32[8,2048,16]{1,2,0:T(8,128)} %param.58) | copy-start | bytes 3145732
  7.2 116.1 %all-gather.7.cloned.1.call-start = ((), (), s32[]{:S(2)}) async-start(), calls=%async_computation.8 | async-start | bytes 7864320 | tf_op jit(solution)/shard_map/all_gather | solution.py:169
  7.9 149.4 %all-gather.11.cloned.1.call-start = ((), (), s32[]{:S(2)}) async-start(), calls=%async_computation.10 | async-start | bytes 2359296 | tf_op jit(solution)/shard_map/all_gather | solution.py:226
  25.9 719.9 %copy-start.18 = (f32[32,768]{1,0:T(8,128)}, f32[32,768]{1,0:T(8,128)S(1)}, u32[]{:S(2)}) copy-start(f32[32,768]{1,0:T(8,128)S(1)} %gather_fusion.8) | copy-start | bytes 294916
  129.0 57.2 %all-gather.9.cloned.1.call-start = ((), (), s32[]{:S(2)}) async-start(), calls=%async_computation.9 | async-start | bytes 2359296 | tf_op jit(solution)/shard_map/all_gather | solution.py:225
  134.7 106.7 %all-gather.13.cloned.1.call-start = ((), (), s32[]{:S(2)}) async-start(), calls=%async_computation.11 | async-start | bytes 2621440 | tf_op jit(solution)/shard_map/all_gather | solution.py:170
  135.3 180.5 %all-reduce.7.cloned.1.call-start = ((), (), s32[]{:S(2)}) async-start(), calls=%async_computation.12 | async-start | bytes 6291456 | tf_op jit(solution)/shard_map/psum | solution.py:258
  246.5 217.7 %all-gather.15.cloned.1.call-start = ((), (), s32[]{:S(2)}) async-start(), calls=%async_computation.13 | async-start | bytes 10485760 | tf_op jit(solution)/shard_map/all_gather | solution.py:171
  247.1 366.6 %all-gather.17.cloned.1.call-start = ((), (), s32[]{:S(2)}) async-start(), calls=%async_computation.14 | async-start | bytes 10485760 | tf_op jit(solution)/shard_map/all_gather | solution.py:172
  247.9 416.2 %all-reduce.11.cloned.1.call-start = ((), (), s32[]{:S(2)}) async-start(), calls=%async_computation.24 | async-start | bytes 196608 | tf_op jit(solution)/shard_map/psum | solution.py:325
  261.4 362.5 %copy-start.70 = (bf16[768,32]{0,1:T(8,128)(2,1)}, bf16[768,32]{0,1:T(8,128)(2,1)S(1)}, u32[]{:S(2)}) copy-start(bf16[768,32]{0,1:T(8,128)(2,1)S(1)} %fusion.90) | copy-start | bytes 147460
  325.7 148.6 %copy-start.65 = (bf16[768,32]{0,1:T(8,128)(2,1)}, bf16[768,32]{0,1:T(8,128)(2,1)S(1)}, u32[]{:S(2)}) copy-start(bf16[768,32]{0,1:T(8,128)(2,1)S(1)} %fusion.89) | copy-start | bytes 147460
  632.5 103.4 %all-reduce.9.cloned.1.call-start = ((), (), s32[]{:S(2)}) async-start(), calls=%async_computation.15 | async-start | bytes 6291456 | tf_op jit(solution)/shard_map/psum | solution.py:324
  644.6 215.6 %reduce-scatter.17.cloned.1.call-start = ((), (), s32[]{:S(2)}) async-start(), calls=%async_computation.16 | async-start | bytes 2359296 | tf_op jit(solution)/shard_map/reduce_scatter | solution.py:400
  815.9 54.8 %reduce-scatter.19.cloned.1.call-start = ((), (), s32[]{:S(2)}) async-start(), calls=%async_computation.17 | async-start | bytes 2359296 | tf_op jit(solution)/shard_map/reduce_scatter | solution.py:403
  816.6 117.1 %reduce-scatter.29.cloned.1.call-start = ((), (), s32[]{:S(2)}) async-start(), calls=%async_computation.22 | async-start | bytes 147456
  823.6 174.2 %reduce-scatter.31.cloned.1.call-start = ((), (), s32[]{:S(2)}) async-start(), calls=%async_computation.23 | async-start | bytes 147456
  830.2 232.6 %reduce-scatter.21.cloned.1.call-start = ((), (), s32[]{:S(2)}) async-start(), calls=%async_computation.18 | async-start | bytes 589824 | tf_op jit(solution)/shard_map/reduce_scatter | solution.py:491
  834.6 292.9 %reduce-scatter.23.cloned.1.call-start = ((), (), s32[]{:S(2)}) async-start(), calls=%async_computation.19 | async-start | bytes 589824 | tf_op jit(solution)/shard_map/reduce_scatter | solution.py:494
  838.9 353.2 %reduce-scatter.27.cloned.1.call-start = ((), (), s32[]{:S(2)}) async-start(), calls=%async_computation.21 | async-start | bytes 589824
  897.9 420.6 %all-reduce.13.cloned.1.call-start = ((), (), s32[]{:S(2)}) async-start(), calls=%async_computation.25 | async-start | bytes 12877824 | tf_op jit(solution)/shard_map/psum | solution.py:437
  909.8 219.3 %copy-start.38 = (bf16[768,4,128]{0,2,1:T(8,128)(2,1)S(1)}, bf16[768,4,128]{0,2,1:T(8,128)(2,1)}, u32[]{:S(2)}) copy-start(bf16[768,4,128]{0,2,1:T(8,128)(2,1)} %copy-done.37) | copy-start | bytes 2359300
  909.8 219.3 %copy-start.55 = (bf16[768,32]{0,1:T(8,128)(2,1)S(1)}, bf16[768,32]{0,1:T(8,128)(2,1)}, u32[]{:S(2)}) copy-start(bf16[768,32]{0,1:T(8,128)(2,1)} %copy-done.54) | copy-start | bytes 147460
  909.8 497.4 %reduce-scatter.25.cloned.1.call-start = ((), (), s32[]{:S(2)}) async-start(), calls=%async_computation.20 | async-start | bytes 589824
  (110 other events, 1911.4 us)
Sparse Core Ops, SparseCore 0:
  9.6 113.6 all-gather.6
  129.1 28.2 all-gather.10
  158.9 27.1 all-gather.8
  187.6 44.0 all-gather.12
  246.7 69.0 all-reduce.6
  317.2 147.0 all-gather.14
  465.8 147.8 all-gather.16
  632.6 31.3 all-reduce.10
  666.5 69.3 all-reduce.8
  816.0 26.2 reduce-scatter.16
  844.6 26.0 reduce-scatter.18
  874.8 58.8 reduce-scatter.28
  937.9 59.8 reduce-scatter.30
  1001.4 61.4 reduce-scatter.20
  1066.1 61.4 reduce-scatter.22
  1131.1 60.9 reduce-scatter.26
  1195.0 123.3 all-reduce.12
  1347.0 60.1 reduce-scatter.24
where the time goes:
time: 1430 us; the launch traced here: 1420 us
  waiting for transfers between devices  974 us (68%)
  matrix products  226 us (16%)
  local copies, waits for them, and re-layouts  148 us (10%)
  other arithmetic  37.5 us (3%)
  between operations  16.2 us (1%)
    unnamed x22, waiting for transfers between devices  196 us
    all_gather x1, waiting for transfers between devices, body(): lax.all_gather(w_in, 'fsdp', axis=0, tiled=True)  139 us
    all_gather x1, waiting for transfers between devices, body(): lax.all_gather(w_out, 'fsdp', axis=1, tiled=True)  123 us
    psum x1, waiting for transfers between devices, body(): lax.psum(grad_down_qkv_part.astype(jnp.bfloat16), 'tp').astype(jnp.float32)  122 us
    unnamed x213, local copies, waits for them, and re-layouts  90.9 us
    all_gather x1, waiting for transfers between devices, body(): lax.all_gather(w_qkv, 'fsdp', axis=1, tiled=True)  87.1 us
    dot_general x16, matrix products, multiplied_result_value(): return jnp.dot(operand, other, preferred_element_type=jnp.float32)  72.9 us
    psum x1, waiting for transfers between devices, body(): lax.psum(grad_normed_two_part.astype(jnp.bfloat16), 'tp')  71.9 us
  transfers between devices with their start and end apart: 18, of which 16 were waited for; matrix products, arithmetic and copies ran while one was open for 19% of the time, Pallas kernels for 0%

commit v1 on v0

v1 whole, which is shorter than its diff:
```python
import jax
import jax.numpy as jnp
from jax import lax
from jax.experimental import pallas as pl
from jax.experimental.pallas import tpu as pltpu
from jax.sharding import PartitionSpec as P

HD = 128
RANK = 16
ADAPTERS = 8
SLOTS = 2
PAIR = SLOTS * RANK
BLOCK = 256
AUG = 128

layer_eps = 1e-05
factor = 0.5
neg_fill = -1e30
bf16 = jnp.bfloat16
f32 = jnp.float32

CORE_SWAP = [(0, 1), (1, 0), (2, 3), (3, 2)]
X_SWAP = [(0, 2), (2, 0), (1, 3), (3, 1)]


def dot_nn(a, b):
    return lax.dot_general(a, b, (((1,), (0,)), ((), ())), preferred_element_type=f32)


def dot_nt(a, b):
    return lax.dot_general(a, b, (((1,), (1,)), ((), ())), preferred_element_type=f32)


def dot_tn(a, b):
    return lax.dot_general(a, b, (((0,), (0,)), ((), ())), preferred_element_type=f32)


def round_low(v):
    return lax.reduce_precision(v, 8, 7).astype(bf16)


def standardize(rows):
    centre = rows - jnp.mean(rows, axis=-1, keepdims=True)
    spread = jnp.mean(centre * centre, axis=-1, keepdims=True)
    inverse = lax.rsqrt(spread + layer_eps)
    return centre * inverse, inverse


def norm_back(grad_scaled, unit, inverse):
    first = jnp.mean(grad_scaled, axis=-1, keepdims=True)
    second = jnp.mean(grad_scaled * unit, axis=-1, keepdims=True)
    return inverse * (grad_scaled - first - unit * second)


def ancestry(parents):
    total = parents.shape[0]
    position = jnp.arange(total, dtype=jnp.int32)
    reach = (
        (parents[:, None] == position[None, :]) | (position[:, None] == position[None, :])
    ).astype(f32)
    span = 1
    while span < total:
        reach = jnp.minimum(jnp.sum(reach[:, :, None] * reach[None, :, :], axis=1), 1.0)
        span *= 2
    roots = (parents < 0).astype(f32)
    order = jnp.sum(jnp.where(position[None, :] <= position[:, None], roots[None, :], 0.0), axis=1)
    slot = jnp.sum(reach * (roots * (order - 1.0))[None, :], axis=1)
    return reach, slot


def attend_forward(qkv, far, far_bias, own_bias, heads, scale):
    tokens = qkv.shape[0]
    far_rows = far.shape[0]
    blocks = tokens // BLOCK

    def kernel(q_ref, k_ref, v_ref, fk_ref, fv_ref, fb_ref, ob_ref, o_ref, pf_ref, po_ref):
        far_k = fk_ref[...]
        far_v = fv_ref[...]
        for b in range(blocks):
            rows = slice(b * BLOCK, (b + 1) * BLOCK)
            width = (b + 1) * BLOCK
            q = q_ref[rows, :]
            s_far = dot_nt(q, far_k) * scale + fb_ref[b : b + 1, :]
            s_own = dot_nt(q, k_ref[:width, :]) * scale + ob_ref[b : b + 1, :width]
            q_pos = lax.broadcasted_iota(jnp.int32, (BLOCK, width), 0) + b * BLOCK
            k_pos = lax.broadcasted_iota(jnp.int32, (BLOCK, width), 1)
            s_own = jnp.where(k_pos <= q_pos, s_own, neg_fill)
            top = jnp.maximum(
                jnp.max(s_far, axis=1, keepdims=True), jnp.max(s_own, axis=1, keepdims=True)
            )
            p_far = jnp.exp(s_far - top)
            p_own = jnp.exp(s_own - top)
            total = jnp.sum(p_far, axis=1, keepdims=True) + jnp.sum(p_own, axis=1, keepdims=True)
            inverse = 1.0 / total
            p_far = (p_far * inverse).astype(bf16)
            p_own = (p_own * inverse).astype(bf16)
            pf_ref[0, rows, :] = p_far
            po_ref[0, rows, :width] = p_own
            o_ref[rows, :] = dot_nn(p_far, far_v) + dot_nn(p_own, v_ref[:width, :])

    return pl.pallas_call(
        kernel,
        grid=(heads,),
        in_specs=[
            pl.BlockSpec((tokens, HD), lambda h: (0, h)),
            pl.BlockSpec((tokens, HD), lambda h: (0, heads + h)),
            pl.BlockSpec((tokens, HD), lambda h: (0, 2 * heads + h)),
            pl.BlockSpec((far_rows, HD), lambda h: (0, h)),
            pl.BlockSpec((far_rows, HD), lambda h: (0, heads + h)),
            pl.BlockSpec((blocks, far_rows), lambda h: (0, 0)),
            pl.BlockSpec((blocks, tokens), lambda h: (0, 0)),
        ],
        out_specs=[
            pl.BlockSpec((tokens, HD), lambda h: (0, h)),
            pl.BlockSpec((1, tokens, far_rows), lambda h: (h, 0, 0)),
            pl.BlockSpec((1, tokens, tokens), lambda h: (h, 0, 0)),
        ],
        out_shape=[
            jax.ShapeDtypeStruct((tokens, heads * HD), f32),
            jax.ShapeDtypeStruct((heads, tokens, far_rows), bf16),
            jax.ShapeDtypeStruct((heads, tokens, tokens), bf16),
        ],
        compiler_params=pltpu.CompilerParams(vmem_limit_bytes=56 << 20),
        name="attend_forward",
    )(qkv, qkv, qkv, far, far, far_bias, own_bias)


def attend_backward(qkv, far, grad_attended, attended, probs_far, probs_own, heads, scale):
    tokens = qkv.shape[0]
    far_rows = far.shape[0]
    blocks = tokens // BLOCK

    def kernel(
        q_ref, k_ref, v_ref, fk_ref, fv_ref, g_ref, o_ref, pf_ref, po_ref,
        dq_ref, dk_ref, dv_ref, dfk_ref, dfv_ref,
        dk_acc, dv_acc, dfk_acc, dfv_acc,
    ):
        far_k = fk_ref[...]
        far_v = fv_ref[...]
        for b in reversed(range(blocks)):
            first = b == blocks - 1
            rows = slice(b * BLOCK, (b + 1) * BLOCK)
            width = (b + 1) * BLOCK
            q = q_ref[rows, :]
            g = g_ref[rows, :]
            row_dot = jnp.sum(g.astype(f32) * o_ref[rows, :], axis=1, keepdims=True)
            p_far = pf_ref[0, rows, :]
            p_own = po_ref[0, rows, :width]
            d_far = (p_far.astype(f32) * (dot_nt(g, far_v) - row_dot)).astype(bf16)
            d_own = (p_own.astype(f32) * (dot_nt(g, v_ref[:width, :]) - row_dot)).astype(bf16)
            dq_ref[rows, :] = (
                (dot_nn(d_far, far_k) + dot_nn(d_own, k_ref[:width, :])) * scale
            ).astype(bf16)
            if first:
                dfk_acc[...] = dot_tn(d_far, q)
                dfv_acc[...] = dot_tn(p_far, g)
                dk_acc[...] = dot_tn(d_own, q)
                dv_acc[...] = dot_tn(p_own, g)
            else:
                dfk_acc[...] += dot_tn(d_far, q)
                dfv_acc[...] += dot_tn(p_far, g)
                dk_acc[:width, :] += dot_tn(d_own, q)
                dv_acc[:width, :] += dot_tn(p_own, g)
        dk_ref[...] = (dk_acc[...] * scale).astype(bf16)
        dv_ref[...] = dv_acc[...].astype(bf16)
        dfk_ref[...] = (dfk_acc[...] * scale).astype(bf16)
        dfv_ref[...] = dfv_acc[...].astype(bf16)

    head_spec = pl.BlockSpec((tokens, HD), lambda h: (0, h))
    far_spec = pl.BlockSpec((far_rows, HD), lambda h: (0, h))
    own_shape = jax.ShapeDtypeStruct((tokens, heads * HD), bf16)
    far_shape = jax.ShapeDtypeStruct((far_rows, heads * HD), bf16)
    return pl.pallas_call(
        kernel,
        grid=(heads,),
        in_specs=[
            head_spec,
            pl.BlockSpec((tokens, HD), lambda h: (0, heads + h)),
            pl.BlockSpec((tokens, HD), lambda h: (0, 2 * heads + h)),
            far_spec,
            pl.BlockSpec((far_rows, HD), lambda h: (0, heads + h)),
            head_spec,
            head_spec,
            pl.BlockSpec((1, tokens, far_rows), lambda h: (h, 0, 0)),
            pl.BlockSpec((1, tokens, tokens), lambda h: (h, 0, 0)),
        ],
        out_specs=[head_spec, head_spec, head_spec, far_spec, far_spec],
        out_shape=[own_shape, own_shape, own_shape, far_shape, far_shape],
        scratch_shapes=[
            pltpu.VMEM((tokens, HD), f32),
            pltpu.VMEM((tokens, HD), f32),
            pltpu.VMEM((far_rows, HD), f32),
            pltpu.VMEM((far_rows, HD), f32),
        ],
        compiler_params=pltpu.CompilerParams(vmem_limit_bytes=56 << 20),
        name="attend_backward",
    )(qkv, qkv, qkv, far, far, grad_attended, attended, probs_far, probs_own)


def gate(value, *waits):
    return lax.optimization_barrier((value,) + waits)[0]


def make_body(ctx_size):
    pair_ctx = ctx_size == 2

    def body(
        inputs,
        loss_sensitivity,
        parent_block,
        adapter_of,
        w_qkv,
        bias_qv,
        w_o,
        exit_offsets,
        ln_gain,
        ln_bias,
        w_in,
        hidden_offset_frozen,
        w_out,
        a_attn,
        b_attn,
        a_up,
        b_up,
        a_down,
        b_down,
    ):
        group = lax.axis_index("fsdp")
        context = lax.axis_index("ctx")
        tensor = lax.axis_index("tp")
        core = tensor % 2
        tokens, width = inputs.shape
        half = tokens // 2
        local = w_qkv.shape[2]
        shard = w_qkv.shape[1]
        hidden_local = w_in.shape[1]
        heads = local // HD
        blocks = tokens // BLOCK
        scale = HD ** (-0.5)
        wide = width + AUG

        def on(value, axis, pairs):
            return lax.ppermute(value, axis, pairs)

        def own_rows(matrix):
            return lax.dynamic_slice_in_dim(matrix, core * half, half, 0)

        def other_rows(matrix):
            return lax.dynamic_slice_in_dim(matrix, (1 - core) * half, half, 0)

        def natural(own, other):
            return jnp.concatenate(
                [jnp.where(core == 0, own, other), jnp.where(core == 0, other, own)], axis=0
            )

        def local_lanes(matrix):
            return lax.dynamic_slice_in_dim(matrix, tensor * local, local, matrix.ndim - 1)

        def put(buffer, piece, row, column):
            return lax.dynamic_update_slice(buffer, piece, (row, column))

        swap_y = [(0, 1), (1, 0)]

        def spread_weight(buffer, own, half_axis, row_step, col_step, row_half, col_half, waits):
            size = own.shape[half_axis] // 2
            part = lax.dynamic_slice_in_dim(own, context * size, size, half_axis)
            part = gate(part, *waits) if waits else part
            from_two = on(part, "fsdp", [(0, 2), (2, 0), (1, 3), (3, 1)])
            from_one = on(part, "fsdp", [(0, 1), (1, 0), (2, 3), (3, 2)])
            middle = on(part, "fsdp", [(1, 2), (2, 1)])
            ends = on(from_two, "fsdp", [(2, 3), (1, 0)])
            y_one = on(from_one, "ctx", swap_y)
            y_two = on(from_two, "ctx", swap_y)
            both = ("fsdp", "ctx")
            y_middle = on(middle, both, [(2, 3), (3, 2), (4, 5), (5, 4)])
            y_ends = on(ends, both, [(0, 1), (1, 0), (6, 7), (7, 6)])
            inner = (group == 1) | (group == 2)
            buffer = put(buffer, own, group * row_step, group * col_step)

            def both_halves(buffer, piece, other, source):
                row = source * row_step
                col = source * col_step
                buffer = put(buffer, piece, row + context * row_half, col + context * col_half)
                return put(
                    buffer,
                    other,
                    row + (1 - context) * row_half,
                    col + (1 - context) * col_half,
                )

            buffer = both_halves(buffer, from_one, y_one, group ^ 1)
            buffer = both_halves(buffer, from_two, y_two, group ^ 2)
            buffer = both_halves(
                buffer,
                jnp.where(inner, middle, ends),
                jnp.where(inner, y_middle, y_ends),
                group ^ 3,
            )
            return buffer, (from_one, from_two)

        def sum_tp(other_low, own_full):
            got = on(other_low, "tp", CORE_SWAP)
            mine = round_low(own_full + got.astype(f32))
            far = on(mine, "tp", X_SWAP)
            return mine.astype(f32) + far.astype(f32)

        pair = lax.dynamic_slice_in_dim(adapter_of, group * SLOTS, SLOTS)

        def pick_pair(array, axis):
            return jnp.concatenate(
                [lax.dynamic_slice_in_dim(array, pair[s], 1, axis) for s in range(SLOTS)], axis
            )

        a_pair = jnp.swapaxes(pick_pair(a_attn, 1), 2, 3)
        a_qkv_rows = a_pair[:3].reshape(3 * PAIR, width).astype(bf16)
        a_o_rows = local_lanes(a_pair[3].reshape(PAIR, width)).astype(bf16)
        b_pair = pick_pair(b_attn, 1)
        b_qkv_rows = local_lanes(b_pair[:3]).reshape(3, PAIR, local).astype(bf16)
        b_o_rows = b_pair[3].reshape(PAIR, width).astype(bf16)
        a_up_rows = jnp.swapaxes(pick_pair(a_up, 0), 1, 2).reshape(PAIR, width).astype(bf16)
        b_up_rows = pick_pair(b_up, 0).reshape(PAIR, hidden_local).astype(bf16)
        a_down_rows = (
            jnp.swapaxes(pick_pair(a_down, 0), 1, 2).reshape(PAIR, hidden_local).astype(bf16)
        )
        b_down_rows = pick_pair(b_down, 0).reshape(PAIR, width).astype(bf16)

        q_aug = jnp.concatenate(
            [jnp.pad(b_qkv_rows[i], ((0, 0), (i * local, (2 - i) * local))) for i in range(3)]
            + [jnp.zeros((AUG - 3 * PAIR, 3 * local), bf16)],
            axis=0,
        )
        q_start = jnp.concatenate([jnp.zeros((width, 3 * local), bf16), q_aug], axis=0)
        o_aug = jnp.pad(a_o_rows.T, ((0, 0), (0, AUG - PAIR)))
        o_start = jnp.concatenate([jnp.zeros((local, width), bf16), o_aug], axis=1)
        in_aug = jnp.pad(b_up_rows, ((0, AUG - PAIR), (0, 0)))
        in_start = jnp.concatenate([jnp.zeros((width, hidden_local), bf16), in_aug], axis=0)
        out_aug = jnp.pad(a_down_rows.T, ((0, 0), (0, AUG - PAIR)))
        out_start = jnp.concatenate([jnp.zeros((hidden_local, width), bf16), out_aug], axis=1)
        own_q = jnp.transpose(w_qkv, (1, 0, 2)).reshape(shard, 3 * local)
        if pair_ctx:
            quarter = tokens // 4
            sent = lax.dynamic_slice_in_dim(inputs, tensor * quarter, quarter, 0)
            far_quarter = on(sent, "ctx", [(0, 1)])
            far_x = on(far_quarter, "tp", X_SWAP)
            far_core = on(far_quarter, "tp", CORE_SWAP)
            far_both = on(far_x, "tp", CORE_SWAP)
            far_inputs = jnp.zeros((tokens, width), bf16)
            for piece, place in (
                (far_quarter, tensor),
                (far_x, tensor ^ 2),
                (far_core, tensor ^ 1),
                (far_both, tensor ^ 3),
            ):
                far_inputs = put(far_inputs, piece, place * quarter, 0)
            q_full, q_done = spread_weight(q_start, own_q, 0, shard, 0, shard // 2, 0, ())
            o_full, o_done = spread_weight(o_start, w_o, 0, 0, shard, local // 2, 0, q_done)
            in_full, in_done = spread_weight(in_start, w_in, 0, shard, 0, shard // 2, 0, o_done)
            out_full, _ = spread_weight(out_start, w_out, 0, 0, shard, hidden_local // 2, 0, in_done)
        else:
            q_full = put(q_start, lax.all_gather(own_q, "fsdp", axis=0, tiled=True), 0, 0)
            o_full = put(o_start, lax.all_gather(w_o, "fsdp", axis=1, tiled=True), 0, 0)
            in_full = put(in_start, lax.all_gather(w_in, "fsdp", axis=0, tiled=True), 0, 0)
            out_full = put(out_start, lax.all_gather(w_out, "fsdp", axis=1, tiled=True), 0, 0)

        reach, slot = ancestry(parent_block[0])
        all_blocks = reach.shape[0]
        first_block = context * blocks
        far_blocks = blocks if pair_ctx else all_blocks
        reach_rows = lax.dynamic_slice_in_dim(reach, first_block, blocks, 0)
        block_ids = jnp.arange(far_blocks, dtype=jnp.int32)
        far_open = (reach_rows[:, :far_blocks] > 0.5) & (block_ids[None, :] < first_block)
        own_open = lax.dynamic_slice_in_dim(reach_rows, first_block, blocks, 1) > 0.5
        far_bias = jnp.repeat(jnp.where(far_open, 0.0, neg_fill).astype(f32), BLOCK, axis=1)
        own_bias = jnp.repeat(jnp.where(own_open, 0.0, neg_fill).astype(f32), BLOCK, axis=1)

        def picks(slots):
            select = (slots[:, None] == jnp.arange(SLOTS, dtype=f32)[None, :]).astype(f32)
            return jnp.repeat(jnp.repeat(select, RANK, axis=1), BLOCK, axis=0)

        pick = picks(lax.dynamic_slice_in_dim(slot, first_block, blocks))
        pick_own = own_rows(pick)

        gain_one, shift_one = ln_gain[0][None, :], ln_bias[0][None, :]
        gain_two, shift_two = ln_gain[1][None, :], ln_bias[1][None, :]

        def widen(low, *extra):
            spare = AUG - sum(e.shape[1] for e in extra)
            tail = [jnp.zeros((low.shape[0], spare), bf16)] if spare else []
            return jnp.concatenate([low, *extra, *tail], axis=1)

        def first_norm(rows, pick_rows):
            low = (standardize(rows.astype(f32))[0] * gain_one + shift_one).astype(bf16)
            reduced = (dot_nt(low, a_qkv_rows) * jnp.tile(pick_rows, (1, 3))).astype(bf16)
            return low, widen(low, factor * reduced)

        normed, normed_wide = first_norm(inputs, pick)
        zero_bias = jnp.zeros((local,), f32)
        q_bias = jnp.concatenate([bias_qv[0], zero_bias, bias_qv[1]])[None, :]
        qkv = (dot_nn(normed_wide, q_full) + q_bias).astype(bf16)
        if pair_ctx:
            _, far_wide = first_norm(far_inputs, picks(slot[:blocks]))
            far_kv = (dot_nn(far_wide, q_full[:, local:]) + q_bias[:, local:]).astype(bf16)
        else:
            far_kv = lax.all_gather(qkv[:, local:], "ctx", axis=0, tiled=True)

        attended_f, probs_far, probs_own = attend_forward(
            qkv, far_kv, far_bias, own_bias, heads, scale
        )
        attended = attended_f.astype(bf16)
        attended_own = own_rows(attended)
        attended_other = other_rows(attended)
        branch = sum_tp(
            dot_nn(attended_other, o_full).astype(bf16), dot_nn(attended_own, o_full)
        )
        down_o = factor * (branch[:, width : width + PAIR] * pick_own).astype(bf16)
        middle = (
            own_rows(inputs).astype(f32)
            + branch[:, :width]
            + exit_offsets[0][None, :]
            + dot_nn(down_o, b_o_rows)
        )
        unit_two, inverse_two = standardize(middle)
        normed_two = (unit_two * gain_two + shift_two).astype(bf16)
        down_up = factor * (dot_nt(normed_two, a_up_rows) * pick_own).astype(bf16)
        two_own = widen(normed_two, down_up, down_o)
        two_other = on(two_own, "tp", CORE_SWAP)
        two_wide = jnp.concatenate([two_own, two_other], axis=0)

        pre_act = dot_nn(two_wide, in_full) + hidden_offset_frozen[None, :]
        phi = 0.5 * (1.0 + lax.erf(pre_act * (2.0 ** -0.5)))
        hidden = (pre_act * phi).astype(bf16)
        slope = (
            phi + pre_act * jnp.exp(-0.5 * pre_act * pre_act) * (0.5 / jnp.pi) ** 0.5
        ).astype(bf16)

        loss_own = own_rows(loss_sensitivity)
        loss_rel = jnp.concatenate([loss_own, other_rows(loss_sensitivity)], axis=0)
        pick_rel = jnp.concatenate([pick_own, other_rows(pick)], axis=0)
        grad_down_down = (factor * dot_nt(loss_rel, b_down_rows) * pick_rel).astype(bf16)
        loss_wide = widen(loss_rel, grad_down_down)
        grad_pre = (dot_nt(loss_wide, out_full) * slope.astype(f32)).astype(bf16)
        grad_two = sum_tp(
            dot_nt(grad_pre[half:], in_full).astype(bf16), dot_nt(grad_pre[:half], in_full)
        )
        grad_down_up = (factor * grad_two[:, width : width + PAIR] * pick_own).astype(bf16)
        grad_normed_two = grad_two[:, :width] + dot_nn(grad_down_up, a_up_rows)
        grad_middle = loss_own.astype(f32) + norm_back(
            grad_normed_two * gain_two, unit_two, inverse_two
        )
        grad_branch = grad_middle.astype(bf16)
        grad_down_o = (factor * dot_nt(grad_branch, b_o_rows) * pick_own).astype(bf16)
        back_own = widen(grad_branch, grad_down_o, grad_down_up)
        back_other = on(back_own, "tp", CORE_SWAP)
        grad_attended = natural(
            dot_nt(back_own, o_full).astype(bf16), dot_nt(back_other, o_full).astype(bf16)
        )

        exit_part = sum_tp(
            dot_nn(hidden[half:], out_full).astype(bf16), dot_nn(hidden[:half], out_full)
        )
        down_down = factor * (exit_part[:, width : width + PAIR] * pick_own).astype(bf16)
        layer_own = (
            middle
            + exit_part[:, :width]
            + exit_offsets[1][None, :]
            + dot_nn(down_down, b_down_rows)
        ).astype(bf16)
        layer_wide = widen(layer_own, down_down)
        layer_other = on(layer_wide, "tp", CORE_SWAP)
        layer_out = natural(layer_own, layer_other[:, :width])
        down_down_rel = jnp.concatenate([down_down, layer_other[:, width : width + PAIR]], axis=0)

        grad_q, grad_k, grad_v, far_grad_k, far_grad_v = attend_backward(
            qkv, far_kv, grad_attended, attended_f, probs_far, probs_own, heads, scale
        )
        if pair_ctx:
            more_k = on(far_grad_k, "ctx", [(1, 0)])
            more_v = on(far_grad_v, "ctx", [(1, 0)])
        else:
            more_k = lax.psum_scatter(far_grad_k, "ctx", scatter_dimension=0, tiled=True)
            more_v = lax.psum_scatter(far_grad_v, "ctx", scatter_dimension=0, tiled=True)
        grad_qkv = jnp.concatenate(
            [
                grad_q,
                (grad_k.astype(f32) + more_k.astype(f32)).astype(bf16),
                (grad_v.astype(f32) + more_v.astype(f32)).astype(bf16),
            ],
            axis=1,
        )
        grad_one = sum_tp(
            dot_nt(other_rows(grad_qkv), q_full).astype(bf16), dot_nt(own_rows(grad_qkv), q_full)
        )
        grad_down_qkv = (
            factor * grad_one[:, width : width + 3 * PAIR] * jnp.tile(pick_own, (1, 3))
        ).astype(bf16)
        other_down_qkv = on(grad_down_qkv, "tp", CORE_SWAP)
        grad_normed = grad_one[:, :width] + dot_nn(grad_down_qkv, a_qkv_rows)
        unit_one, inverse_one = standardize(own_rows(inputs).astype(f32))
        grad_own = (
            grad_middle + norm_back(grad_normed * gain_one, unit_one, inverse_one)
        ).astype(bf16)
        grad_other = on(grad_own, "tp", CORE_SWAP)
        grad_inputs = natural(grad_own, grad_other)

        attended_rel = jnp.concatenate([attended_own, attended_other], axis=0)
        back_rel = jnp.concatenate([back_own, back_other], axis=0)
        term_a_o = dot_tn(back_rel[:, width : width + PAIR], attended_rel)
        term_b_o = dot_tn(two_wide[:, width + PAIR : width + 2 * PAIR], local_lanes(back_rel[:, :width]))
        term_a_up = dot_tn(
            back_rel[:, width + PAIR : width + 2 * PAIR], local_lanes(two_wide[:, :width])
        )
        term_b_up = dot_tn(two_wide[:, width : width + PAIR], grad_pre)
        term_a_down = dot_tn(grad_down_down, hidden)
        term_b_down = dot_tn(down_down_rel, local_lanes(loss_rel))
        reduced_qkv = normed_wide[:, width : width + 3 * PAIR]
        term_b_qkv = [
            dot_tn(
                reduced_qkv[:, i * PAIR : (i + 1) * PAIR],
                grad_qkv[:, i * local : (i + 1) * local],
            )
            for i in range(3)
        ]
        natural_down = natural(grad_down_qkv, other_down_qkv)
        term_a_qkv = dot_tn(natural_down, local_lanes(normed))

        holder = jnp.stack([group ^ k for k in range(4)])
        owner = adapter_of.reshape(4, SLOTS)[holder].reshape(4 * SLOTS)
        place = (jnp.arange(ADAPTERS, dtype=jnp.int32)[:, None] == owner[None, :]).astype(f32)

        def deliver(terms):
            lanes = []
            for term in terms:
                cut = term.shape[1] // 4
                lanes.append(term.astype(bf16).reshape(term.shape[0], 4, cut // AUG, AUG))
            received = []
            for k in range(4):
                target = group ^ k
                piece = jnp.concatenate(
                    [
                        lax.dynamic_slice_in_dim(lane, target, 1, 1).reshape(-1, AUG)
                        for lane in lanes
                    ],
                    axis=0,
                )
                if k:
                    piece = on(piece, "fsdp", [(i, i ^ k) for i in range(4)])
                received.append(piece)
            stacked = jnp.stack(received)
            if pair_ctx:
                stacked = stacked.astype(f32) + on(stacked, "ctx", swap_y).astype(f32)
            else:
                stacked = lax.psum(stacked.astype(f32), "ctx")
            results = []
            start = 0
            for lane in lanes:
                rows, _, tiles, _ = lane.shape
                items = rows // PAIR
                count = rows * tiles
                part = stacked[:, start : start + count].reshape(
                    4, items, SLOTS, RANK, tiles * AUG
                )
                start += count
                part = jnp.transpose(part, (0, 2, 1, 3, 4)).reshape(
                    4 * SLOTS, items, RANK, tiles * AUG
                )
                spread = jnp.sum(place[:, :, None, None, None] * part[None], axis=1)
                size = tiles * AUG // ctx_size
                results.append(
                    jnp.swapaxes(
                        lax.dynamic_slice_in_dim(spread, context * size, size, 3), 0, 1
                    )
                )
            return results

        out_a_o, out_b_o, out_a_up, out_b_down, out_b_up, out_a_down = deliver(
            [term_a_o, term_b_o, term_a_up, term_b_down, term_b_up, term_a_down]
        )
        (out_b_qkv,) = deliver([jnp.concatenate(term_b_qkv, axis=0)])
        (out_a_qkv,) = deliver([term_a_qkv])
        grad_a_attn = jnp.swapaxes(jnp.concatenate([out_a_qkv, out_a_o], axis=0), 2, 3)
        grad_b_attn = jnp.concatenate([out_b_qkv, out_b_o], axis=0)
        return (
            layer_out,
            grad_inputs,
            grad_a_attn,
            grad_b_attn,
            jnp.swapaxes(out_a_up[0], 1, 2),
            out_b_up[0],
            jnp.swapaxes(out_a_down[0], 1, 2),
            out_b_down[0],
        )

    return body


def solution(mesh):
    in_specs = (
        P(("fsdp", "ctx"), None),
        P(("fsdp", "ctx"), None),
        P("fsdp", None),
        P(),
        P(None, "fsdp", "tp"),
        P(None, "tp"),
        P("tp", "fsdp"),
        P(),
        P(),
        P(),
        P("fsdp", "tp"),
        P("tp"),
        P("tp", "fsdp"),
        P(),
        P(),
        P(),
        P(None, None, "tp"),
        P(None, "tp", None),
        P(),
    )
    out_specs = (
        P(("fsdp", "ctx"), None),
        P(("fsdp", "ctx"), None),
        P(None, None, ("tp", "fsdp", "ctx"), None),
        P(None, None, None, ("tp", "fsdp", "ctx")),
        P(None, ("tp", "fsdp", "ctx"), None),
        P(None, None, ("tp", "fsdp", "ctx")),
        P(None, ("tp", "fsdp", "ctx"), None),
        P(None, None, ("tp", "fsdp", "ctx")),
    )
    return jax.shard_map(
        make_body(mesh.shape["ctx"]),
        mesh=mesh,
        in_specs=in_specs,
        out_specs=out_specs,
        check_vma=False,
    )
```

time: 1430 us -> 858 us (0.60)
  waiting for transfers between devices: 974 us -> 201 us
  local copies, waits for them, and re-layouts: 148 us -> 282 us
  starting transfers between devices: 1.35 us -> 101 us
  matrix products: 226 us -> 138 us
  other arithmetic: 37.5 us -> 78.3 us
  Pallas kernels: 0 us -> 34.7 us
    all_gather x6 -> x0, waiting for transfers between devices: 390 us -> none  [the longest x1 139 us: body(): lax.all_gather(w_in, 'fsdp', axis=0, tiled=True)]
    psum x4 -> x0, waiting for transfers between devices: 253 us -> none  [the longest x1 122 us: body(): lax.psum(grad_down_qkv_part.astype(jnp.bfloat16), 'tp').astype(jnp.float32)]
    ppermute x0 -> x63, waiting for transfers between devices: none -> 201 us  [on(): return lax.ppermute(value, axis, pairs)]
    unnamed x22 -> x0, waiting for transfers between devices: 196 us -> none
    reduce_scatter x4 -> x0, waiting for transfers between devices: 135 us -> none  [the longest x1 63.1 us: body(): lax.psum_scatter(grad_a_down_term.astype(jnp.bfloat16), ('fsdp', 'ctx'),...]
    dynamic_update_slice x8 -> x28, local copies, waits for them, and re-layouts: 7.19 us -> 120 us  [put(): return lax.dynamic_update_slice(buffer, piece, (row, column))]
    ppermute x0 -> x63, starting transfers between devices: none -> 101 us  [on(): return lax.ppermute(value, axis, pairs)]
    dot_general x66 -> x33, matrix products: 226 us -> 138 us  [the longest x11 63.1 us: dot_nn(): lax.dot_general(a, b, (((1,), (0,)), ((), ())), preferred_element_type=f32)]
  transfers between devices with their start and end apart: 18 -> 63, of which waited for: 16 -> 22; matrix products, arithmetic and copies ran while one was open for 19% -> 44% of each run, Pallas kernels for 0% -> 0%
where the time goes in v1:
time: 858 us; the launch traced here: 841 us
  local copies, waits for them, and re-layouts  282 us (33%)
  waiting for transfers between devices  201 us (23%)
  matrix products  138 us (16%)
  starting transfers between devices  101 us (12%)
  other arithmetic  78.3 us (9%)
  Pallas kernels  34.7 us (4%)
    ppermute x63, waiting for transfers between devices, on(): return lax.ppermute(value, axis, pairs)  201 us
    dynamic_update_slice x28, local copies, waits for them, and re-layouts, put(): return lax.dynamic_update_slice(buffer, piece, (row, column))  120 us
    ppermute x63, starting transfers between devices, on(): return lax.ppermute(value, axis, pairs)  101 us
    dot_general x11, matrix products, dot_nn(): lax.dot_general(a, b, (((1,), (0,)), ((), ())), preferred_element_type=f32)  63.1 us
    dot_general x12, matrix products, dot_nt(): lax.dot_general(a, b, (((1,), (1,)), ((), ())), preferred_element_type=f32)  59.5 us
    unnamed x296, local copies, waits for them, and re-layouts  51.4 us
    pallas_call x1, Pallas kernels, attend_forward(): pl.pallas_call(kernel, grid=(heads,), in_specs=[pl.BlockSpec((tokens, HD)...  21.7 us
  transfers between devices with their start and end apart: 63, of which 22 were waited for; matrix products, arithmetic and copies ran while one was open for 44% of the time, Pallas kernels for 0%

profile of v1, /device:TPU:9, one launch (start us, length us, event | category | flops | bytes accessed | tf_op | source)
XLA Modules:
  0.0 841.1 jit_solution(4117178311801071782)
XLA Ops:
  38.4 11.3 %concatenate.145 = bf16[2176,1536]{0,1:T(8,128)(2,1)} concatenate(bf16[2048,1536]{0,1:T(8,128)(2,1)} %broadcast_in_dim.59, bf16[32,1536]{0,1:T(8,128)(2,1)S(1)} %pad.27, bf16[32,1536]{0,1:T(8,128)(2,1)S(1)} %pad.28, bf16[32,1536]{0,1:T(8,128)(2,1)S(1)} %pad.29, bf16[32,1536]{0,1:T(8,128)(2,1)} %broadcast_in_dim.60), dimensions={0} | concatenate | bytes 13369344 | tf_op jit(solution)/shard_map/concatenate | solution.py:332
  194.6 10.0 %add_convert_fusion.q_ref.k_ref.v_ref = bf16[768,1536]{1,0:T(8,128)(2,1)} fusion(bf16[768,2176]{1,0:T(8,128)(2,1)} %concatenate.143, bf16[2176,1536]{0,1:T(8,128)(2,1)} %select_dynamic-update-slice_fusion.2, f32[1536]{0:T(1024)S(1)} %copy-done.100), kind=kOutput, calls=%fused_computation.29 | convolution fusion | flops 5136187392 | bytes 12392448 | tf_op jit(solution)/shard_map/dot_general | solution.py:27
  209.7 21.7 %attend_forward.1 = (f32[768,512]{1,0:T(8,128)}, bf16[4,768,768]{2,1,0:T(8,128)(2,1)}, bf16[4,768,768]{2,1,0:T(8,128)(2,1)}) custom-call(bf16[768,1536]{1,0:T(8,128)(2,1)} %add_convert_fusion.q_ref.k_ref.v_ref, bf16[768,1536]{1,0:T(8,128)(2,1)} %add_convert_fusion.q_ref.k_ref.v_ref, bf16[768,1536]{1,0:T(8,128)(2,1)} %add_convert_fusion.q_ref.k_ref.v_ref, ...), custom_call_target="tpu_custom_call" | custom-call | tf_op jit(solution)/shard_map/attend_forward/pallas_call | solution.py:101
  244.9 38.1 %collective-permute-done.23 = bf16[256,2048]{1,0:T(8,128)(2,1)} collective-permute-done((bf16[256,2048]{1,0:T(8,128)(2,1)}, bf16[256,2048]{1,0:T(8,128)(2,1)}, u32[]{:S(2)}, u32[]{:S(2)}) %collective-permute-start.23) | collective-permute-done | bytes 1048608 | tf_op jit(solution)/shard_map/ppermute | solution.py:243
  314.3 15.7 %collective-permute-done.26 = bf16[256,2048]{1,0:T(8,128)(2,1)} collective-permute-done((bf16[256,2048]{1,0:T(8,128)(2,1)}, bf16[256,2048]{1,0:T(8,128)(2,1)}, u32[]{:S(2)}, u32[]{:S(2)}) %collective-permute-start.26) | collective-permute-done | bytes 1048608 | tf_op jit(solution)/shard_map/ppermute | solution.py:243
  350.4 13.3 %collective-permute-done.27 = bf16[256,2048]{1,0:T(8,128)(2,1)} collective-permute-done((bf16[256,2048]{1,0:T(8,128)(2,1)}, bf16[256,2048]{1,0:T(8,128)(2,1)}, u32[]{:S(2)}, u32[]{:S(2)}) %collective-permute-start.27) | collective-permute-done | bytes 1048608 | tf_op jit(solution)/shard_map/ppermute | solution.py:243
  407.2 11.6 %dynamic_update_slice.122 = bf16[2048,2176]{0,1:T(8,128)(2,1)} dynamic-update-slice(bf16[2048,2176]{0,1:T(8,128)(2,1)} %constant_dynamic-update-slice_fusion.27, bf16[1024,512]{0,1:T(8,128)(2,1)} %copy.299, s32[]{:T(128)S(6)} %select_n.341, s32[]{:T(128)S(6)} %select_n.330) | dynamic-update-slice | bytes 2097156 | tf_op jit(solution)/shard_map/dynamic_update_slice | solution.py:260
  427.9 10.8 %dynamic_update_slice.123 = bf16[2048,2176]{0,1:T(8,128)(2,1)} dynamic-update-slice(bf16[2048,2176]{0,1:T(8,128)(2,1)} %dynamic_update_slice.122, bf16[1024,512]{0,1:T(8,128)(2,1)} %copy.300, s32[]{:T(128)S(6)} %select_n.342, s32[]{:T(128)S(6)} %select_n.330) | dynamic-update-slice | bytes 2097156 | tf_op jit(solution)/shard_map/dynamic_update_slice | solution.py:260
  438.8 11.6 %dynamic_update_slice.124 = bf16[2048,2176]{0,1:T(8,128)(2,1)} dynamic-update-slice(bf16[2048,2176]{0,1:T(8,128)(2,1)} %dynamic_update_slice.123, bf16[1024,512]{0,1:T(8,128)(2,1)} %copy.301, s32[]{:T(128)S(6)} %select_n.341, s32[]{:T(128)S(6)} %select_n.332) | dynamic-update-slice | bytes 2097156 | tf_op jit(solution)/shard_map/dynamic_update_slice | solution.py:260
  452.7 10.8 %dynamic_update_slice.125 = bf16[2048,2176]{0,1:T(8,128)(2,1)} dynamic-update-slice(bf16[2048,2176]{0,1:T(8,128)(2,1)} %dynamic_update_slice.124, bf16[1024,512]{0,1:T(8,128)(2,1)} %copy.302, s32[]{:T(128)S(6)} %select_n.342, s32[]{:T(128)S(6)} %select_n.332) | dynamic-update-slice | bytes 2097156 | tf_op jit(solution)/shard_map/dynamic_update_slice | solution.py:260
  463.5 11.6 %dynamic_update_slice.126 = bf16[2048,2176]{0,1:T(8,128)(2,1)} dynamic-update-slice(bf16[2048,2176]{0,1:T(8,128)(2,1)} %dynamic_update_slice.125, bf16[1024,512]{0,1:T(8,128)(2,1)} %copy.303, s32[]{:T(128)S(6)} %select_n.341, s32[]{:T(128)S(6)} %select_n.335) | dynamic-update-slice | bytes 2097156 | tf_op jit(solution)/shard_map/dynamic_update_slice | solution.py:260
  482.3 11.2 %dynamic_update_slice.127 = bf16[2048,2176]{0,1:T(8,128)(2,1)} dynamic-update-slice(bf16[2048,2176]{0,1:T(8,128)(2,1)} %dynamic_update_slice.126, bf16[1024,512]{0,1:T(8,128)(2,1)} %copy.304, s32[]{:T(128)S(6)} %select_n.342, s32[]{:T(128)S(6)} %select_n.335) | dynamic-update-slice | bytes 2097156 | tf_op jit(solution)/shard_map/dynamic_update_slice | solution.py:260
  496.2 14.6 %multiply_convert_fusion.1 = (bf16[768,2048]{1,0:T(8,128)(2,1)}, f32[768,2048]{1,0:T(8,128)S(1)}) fusion(f32[2048]{0:T(1024)S(1)} %copy-done.123, bf16[2176,2048]{1,0:T(8,128)(2,1)} %select_dynamic-update-slice_fusion, bf16[384,64]{0,1:T(8,128)(2,1)S(1)} %broadcast.374, bf16[384,2176]{0,1:T(8,128)(2,1)} %collective-permute-done.22, ...), kind=kOutput, calls=%fused_computation.24 | convolution fusion | flops 6871252992 | bytes 21700608 | tf_op jit(solution)/shard_map/dot_general | solution.py:27
  510.9 14.1 %multiply_convert_fusion = bf16[768,2048]{1,0:T(8,128)(2,1)S(1)} fusion(bf16[2048,2176]{0,1:T(8,128)(2,1)} %dynamic_update_slice.127, bf16[768,32]{0,1:T(8,128)(2,1)S(1)} %fusion.68, bf16[384,2048]{0,1:T(8,128)(2,1)S(1)} %copy-done.30, bf16[384,2048]{0,1:T(8,128)(2,1)S(1)} %copy-done.14, f32[768,2048]{1,0:T(8,128)S(1)} %get-tuple-element.159, ...), kind=kOutput, calls=%fused_computation.23 | convolution fusion | flops 6878920704 | bytes 21557504 | tf_op jit(solution)/shard_map/dot_general | solution.py:31
  525.0 9.9 %convolution_convert_fusion.1 = bf16[384,2176]{0,1:T(8,128)(2,1)} fusion(bf16[2176,2048]{1,0:T(8,128)(2,1)} %select_dynamic-update-slice_fusion, bf16[768,2048]{1,0:T(8,128)(2,1)S(1)} %multiply_convert_fusion), kind=kOutput, calls=%fused_computation.46 | convolution fusion | flops 3423387648 | bytes 12156928 | tf_op jit(solution)/shard_map/dot_general | solution.py:31
  535.8 9.0 %convolution_convert_fusion.2 = bf16[384,2176]{0,1:T(8,128)(2,1)S(1)} fusion(bf16[2048,2176]{0,1:T(8,128)(2,1)} %dynamic_update_slice.127, bf16[768,2048]{1,0:T(8,128)(2,1)} %get-tuple-element.158), kind=kOutput, calls=%fused_computation.47 | convolution fusion | flops 3423387648 | bytes 12156928 | tf_op jit(solution)/shard_map/dot_general | solution.py:27
  545.4 9.1 %fusion.24 = bf16[384,2176]{0,1:T(8,128)(2,1)S(1)} fusion(bf16[2176,2048]{1,0:T(8,128)(2,1)} %select_dynamic-update-slice_fusion, bf16[384,2176]{0,1:T(8,128)(2,1)} %collective-permute-done.42, bf16[768,2048]{1,0:T(8,128)(2,1)S(1)} %copy-done.36), kind=kOutput, calls=%fused_computation.43 | convolution fusion | flops 3425894400 | bytes 13828096 | tf_op jit(solution)/shard_map/dot_general | solution.py:31
  556.0 10.1 %fusion.23 = bf16[384,2176]{0,1:T(8,128)(2,1)} fusion(bf16[2048,2176]{0,1:T(8,128)(2,1)} %dynamic_update_slice.127, bf16[384,2176]{0,1:T(8,128)(2,1)S(1)} %collective-permute-done.39, bf16[768,2048]{1,0:T(8,128)(2,1)S(1)} %copy-done.38), kind=kOutput, calls=%fused_computation.42 | convolution fusion | flops 3425894400 | bytes 13828096 | tf_op jit(solution)/shard_map/dot_general | solution.py:27
  567.3 25.5 %collective-permute-done.43 = bf16[384,2176]{0,1:T(8,128)(2,1)S(1)} collective-permute-done((bf16[384,2176]{0,1:T(8,128)(2,1)S(1)}, bf16[384,2176]{0,1:T(8,128)(2,1)S(1)}, u32[]{:S(2)}, u32[]{:S(2)}) %collective-permute-start.43) | collective-permute-done | bytes 1671200 | tf_op jit(solution)/shard_map/ppermute | solution.py:243
  601.2 27.5 %collective-permute-done.40 = bf16[384,2176]{0,1:T(8,128)(2,1)} collective-permute-done((bf16[384,2176]{0,1:T(8,128)(2,1)}, bf16[384,2176]{0,1:T(8,128)(2,1)}, u32[]{:S(2)}, u32[]{:S(2)}) %collective-permute-start.40) | collective-permute-done | bytes 1671200 | tf_op jit(solution)/shard_map/ppermute | solution.py:243
  635.2 11.5 %fusion.31 = (bf16[768,2176]{0,1:T(8,128)(2,1)S(1)}, bf16[768,2176]{0,1:T(8,128)(2,1)S(1)}) fusion(bf16[384,64]{0,1:T(8,128)(2,1)S(1)} %broadcast.374, bf16[384,2176]{0,1:T(8,128)(2,1)} %collective-permute-done.22, bf16[384,32]{0,1:T(8,128)(2,1)S(1)} %copy-done.62, bf16[384,32]{0,1:T(8,128)(2,1)S(1)} %copy-done.70, bf16[384,2048]{0,1:T(8,128)(2,1)S(1)} %copy-done.11, ...), kind=kLoop, calls=%fused_computation.57 | loop fusion | flops 31752192 | bytes 13320192 | tf_op jit(solution)/shard_map/concatenate | solution.py:427
  661.5 13.0 %attend_backward.1 = (bf16[768,512]{1,0:T(8,128)(2,1)}, bf16[768,512]{1,0:T(8,128)(2,1)}, bf16[768,512]{1,0:T(8,128)(2,1)}, bf16[768,512]{1,0:T(8,128)(2,1)}, bf16[768,512]{1,0:T(8,128)(2,1)}) custom-call(bf16[768,1536]{1,0:T(8,128)(2,1)} %add_convert_fusion.q_ref.k_ref.v_ref, bf16[768,1536]{1,0:T(8,128)(2,1)} %add_convert_fusion.q_ref.k_ref.v_ref, ...), custom_call_target="tpu_custom_call" | custom-call | tf_op jit(solution)/shard_map/attend_backward/pallas_call | solution.py:173
  696.9 15.3 %collective-permute-done.45 = bf16[768,512]{1,0:T(8,128)(2,1)} collective-permute-done((bf16[768,512]{1,0:T(8,128)(2,1)}, bf16[768,512]{1,0:T(8,128)(2,1)}, u32[]{:S(2)}, u32[]{:S(2)}) %collective-permute-start.45) | collective-permute-done | bytes 786464 | tf_op jit(solution)/shard_map/ppermute | solution.py:243
  749.5 20.7 %collective-permute-done.48 = bf16[384,2176]{0,1:T(8,128)(2,1)} collective-permute-done((bf16[384,2176]{0,1:T(8,128)(2,1)}, bf16[384,2176]{0,1:T(8,128)(2,1)}, u32[]{:S(2)}, u32[]{:S(2)}) %collective-permute-start.48) | collective-permute-done | bytes 1671200 | tf_op jit(solution)/shard_map/ppermute | solution.py:243
  (662 shorter events, 476.3 us)
Async XLA Ops:
  5.5 47.2 %collective-permute-start = (bf16[256,1536]{0,1:T(8,128)(2,1)}, bf16[256,1536]{0,1:T(8,128)(2,1)}, u32[]{:S(2)}, u32[]{:S(2)}) collective-permute-start(bf16[256,1536]{0,1:T(8,128)(2,1)} %constant_dynamic-slice_fusion.41), channel_id=1, source_target_pairs={{0,8},{8,0},{16,24},{24,16},{1,9},{9,1},{17,25},{25,17},{2,10},{10... | collective-permute-start | bytes 2359304 | tf_op jit(solution)/shard_map/ppermute | solution.py:243
  5.5 47.2 %collective-permute-start.2 = (bf16[256,1536]{0,1:T(8,128)(2,1)}, bf16[256,1536]{0,1:T(8,128)(2,1)}, u32[]{:S(2)}, u32[]{:S(2)}) collective-permute-start(bf16[256,1536]{0,1:T(8,128)(2,1)} %constant_dynamic-slice_fusion.41), channel_id=1, source_target_pairs={{0,16},{16,0},{8,24},{24,8},{1,17},{17,1},{9,25},{25,9},{2,18},{18... | collective-permute-start | bytes 2359304 | tf_op jit(solution)/shard_map/ppermute | solution.py:243
  8.9 81.2 %collective-permute-start.8 = (bf16[192,2048]{1,0:T(8,128)(2,1)}, bf16[192,2048]{1,0:T(8,128)(2,1)}, u32[]{:S(2)}, u32[]{:S(2)}) collective-permute-start(bf16[192,2048]{1,0:T(8,128)(2,1)} %constant_dynamic-slice_fusion.40), channel_id=1, source_target_pairs={{0,4},{1,5},{2,6},{3,7},{8,12},{9,13},{10,14},{11,15},{16,20},{17,... | collective-permute-start | bytes 2359304 | tf_op jit(solution)/shard_map/ppermute | solution.py:243
  90.1 51.2 %collective-permute-start.4 = (bf16[256,1536]{0,1:T(8,128)(2,1)}, bf16[256,1536]{0,1:T(8,128)(2,1)}, u32[]{:S(2)}, u32[]{:S(2)}) collective-permute-start(bf16[256,1536]{0,1:T(8,128)(2,1)} %constant_dynamic-slice_fusion.41), channel_id=1, source_target_pairs={{8,16},{16,8},{9,17},{17,9},{10,18},{18,10},{11,19},{19,11},{12,20... | collective-permute-start | bytes 2359304 | tf_op jit(solution)/shard_map/ppermute | solution.py:243
  92.0 50.3 %collective-permute-start.9 = (bf16[192,2048]{1,0:T(8,128)(2,1)}, bf16[192,2048]{1,0:T(8,128)(2,1)}, u32[]{:S(2)}, u32[]{:S(2)}) collective-permute-start(bf16[192,2048]{1,0:T(8,128)(2,1)} %collective-permute-done.8), channel_id=1, source_target_pairs={{0,2},{2,0},{1,3},{3,1},{4,6},{6,4},{5,7},{7,5},{8,10},{10,8},{9,1... | collective-permute-start | bytes 2359304 | tf_op jit(solution)/shard_map/ppermute | solution.py:243
  95.5 56.2 %collective-permute-start.1 = (bf16[256,1536]{0,1:T(8,128)(2,1)}, bf16[256,1536]{0,1:T(8,128)(2,1)}, u32[]{:S(2)}, u32[]{:S(2)}) collective-permute-start(bf16[256,1536]{0,1:T(8,128)(2,1)} %collective-permute-done), channel_id=1, source_target_pairs={{0,4},{4,0},{1,5},{5,1},{2,6},{6,2},{3,7},{7,3},{8,12},{12,8},{9,1... | collective-permute-start | bytes 2359304 | tf_op jit(solution)/shard_map/ppermute | solution.py:243
  96.9 55.3 %collective-permute-start.5 = (bf16[256,1536]{0,1:T(8,128)(2,1)}, bf16[256,1536]{0,1:T(8,128)(2,1)}, u32[]{:S(2)}, u32[]{:S(2)}) collective-permute-start(bf16[256,1536]{0,1:T(8,128)(2,1)} %collective-permute-done.2), channel_id=1, source_target_pairs={{16,24},{8,0},{17,25},{9,1},{18,26},{10,2},{19,27},{11,3},{20,28},... | collective-permute-start | bytes 2359304 | tf_op jit(solution)/shard_map/ppermute | solution.py:243
  142.3 49.9 %collective-permute-start.6 = (bf16[256,1536]{0,1:T(8,128)(2,1)}, bf16[256,1536]{0,1:T(8,128)(2,1)}, u32[]{:S(2)}, u32[]{:S(2)}) collective-permute-start(bf16[256,1536]{0,1:T(8,128)(2,1)} %collective-permute-done.4), channel_id=1, source_target_pairs={{8,12},{12,8},{16,20},{20,16},{9,13},{13,9},{17,21},{21,17},{10,14... | collective-permute-start | bytes 2359304 | tf_op jit(solution)/shard_map/ppermute | solution.py:243
  236.3 47.8 %collective-permute-start.20 = (bf16[384,2176]{0,1:T(8,128)(2,1)S(1)}, bf16[384,2176]{0,1:T(8,128)(2,1)S(1)}, u32[]{:S(2)}, u32[]{:S(2)}) collective-permute-start(bf16[384,2176]{0,1:T(8,128)(2,1)S(1)} %convolution_convert_fusion.3), channel_id=1, source_target_pairs={{0,1},{1,0},{2,3},{3,2},{4,5},{5,4},{6,7},{7,6},{8,9},{9,8},{10,11... | collective-permute-start | bytes 5013512 | tf_op jit(solution)/shard_map/ppermute | solution.py:243
  240.2 42.9 %collective-permute-start.23 = (bf16[256,2048]{1,0:T(8,128)(2,1)}, bf16[256,2048]{1,0:T(8,128)(2,1)}, u32[]{:S(2)}, u32[]{:S(2)}) collective-permute-start(bf16[256,2048]{1,0:T(8,128)(2,1)} %constant_dynamic-slice_fusion.34), channel_id=1, source_target_pairs={{0,8},{8,0},{16,24},{24,16},{1,9},{9,1},{17,25},{25,17},{2,10},{10... | collective-permute-start | bytes 3145736 | tf_op jit(solution)/shard_map/ppermute | solution.py:243
  243.1 46.9 %collective-permute-start.25 = (bf16[256,2048]{1,0:T(8,128)(2,1)}, bf16[256,2048]{1,0:T(8,128)(2,1)}, u32[]{:S(2)}, u32[]{:S(2)}) collective-permute-start(bf16[256,2048]{1,0:T(8,128)(2,1)} %constant_dynamic-slice_fusion.34), channel_id=1, source_target_pairs={{0,16},{16,0},{8,24},{24,8},{1,17},{17,1},{9,25},{25,9},{2,18},{18... | collective-permute-start | bytes 3145736 | tf_op jit(solution)/shard_map/ppermute | solution.py:243
  288.4 56.8 %collective-permute-start.21 = (bf16[384,2176]{0,1:T(8,128)(2,1)}, bf16[384,2176]{0,1:T(8,128)(2,1)}, u32[]{:S(2)}, u32[]{:S(2)}) collective-permute-start(bf16[384,2176]{0,1:T(8,128)(2,1)} %fusion.25), channel_id=1, source_target_pairs={{0,2},{2,0},{1,3},{3,1},{4,6},{6,4},{5,7},{7,5},{8,10},{10,8},{9,1... | collective-permute-start | bytes 5013512 | tf_op jit(solution)/shard_map/ppermute | solution.py:243
  291.6 47.7 %collective-permute-start.33 = (bf16[1024,512]{1,0:T(8,128)(2,1)}, bf16[1024,512]{1,0:T(8,128)(2,1)}, u32[]{:S(2)}, u32[]{:S(2)}) collective-permute-start(bf16[1024,512]{1,0:T(8,128)(2,1)} %constant_dynamic-slice_fusion.33), channel_id=1, source_target_pairs={{0,16},{16,0},{8,24},{24,8},{1,17},{17,1},{9,25},{25,9},{2,18},{18... | collective-permute-start | bytes 3145736 | tf_op jit(solution)/shard_map/ppermute | solution.py:243
  299.1 64.5 %collective-permute-start.27 = (bf16[256,2048]{1,0:T(8,128)(2,1)}, bf16[256,2048]{1,0:T(8,128)(2,1)}, u32[]{:S(2)}, u32[]{:S(2)}) collective-permute-start(bf16[256,2048]{1,0:T(8,128)(2,1)} %constant_dynamic-slice_fusion.34), channel_id=1, source_target_pairs={{8,16},{16,8},{9,17},{17,9},{10,18},{18,10},{11,19},{19,11},{12,20... | collective-permute-start | bytes 3145736 | tf_op jit(solution)/shard_map/ppermute | solution.py:243
  307.5 58.4 %collective-permute-start.31 = (bf16[1024,512]{1,0:T(8,128)(2,1)}, bf16[1024,512]{1,0:T(8,128)(2,1)S(1)}, u32[]{:S(2)}, u32[]{:S(2)}) collective-permute-start(bf16[1024,512]{1,0:T(8,128)(2,1)} %constant_dynamic-slice_fusion.33), channel_id=1, source_target_pairs={{0,8},{8,0},{16,24},{24,16},{1,9},{9,1},{17,25},{25,17},{2,10},{10... | collective-permute-start | bytes 3145736 | tf_op jit(solution)/shard_map/ppermute | solution.py:243
  330.0 56.1 %collective-permute-start.35 = (bf16[1024,512]{1,0:T(8,128)(2,1)}, bf16[1024,512]{1,0:T(8,128)(2,1)}, u32[]{:S(2)}, u32[]{:S(2)}) collective-permute-start(bf16[1024,512]{1,0:T(8,128)(2,1)} %constant_dynamic-slice_fusion.33), channel_id=1, source_target_pairs={{8,16},{16,8},{9,17},{17,9},{10,18},{18,10},{11,19},{19,11},{12,20... | collective-permute-start | bytes 3145736 | tf_op jit(solution)/shard_map/ppermute | solution.py:243
  345.2 53.7 %collective-permute-start.34 = (bf16[1024,512]{1,0:T(8,128)(2,1)}, bf16[1024,512]{1,0:T(8,128)(2,1)}, u32[]{:S(2)}, u32[]{:S(2)}) collective-permute-start(bf16[1024,512]{1,0:T(8,128)(2,1)} %collective-permute-done.33), channel_id=1, source_target_pairs={{0,4},{4,0},{1,5},{5,1},{2,6},{6,2},{3,7},{7,3},{8,12},{12,8},{9,1... | collective-permute-start | bytes 3145736 | tf_op jit(solution)/shard_map/ppermute | solution.py:243
  374.7 100.4 %collective-permute-start.29 = (bf16[256,2048]{1,0:T(8,128)(2,1)}, bf16[256,2048]{1,0:T(8,128)(2,1)}, u32[]{:S(2)}, u32[]{:S(2)}) collective-permute-start(bf16[256,2048]{1,0:T(8,128)(2,1)} %collective-permute-done.27), channel_id=1, source_target_pairs={{8,12},{12,8},{16,20},{20,16},{9,13},{13,9},{17,21},{21,17},{10,14... | collective-permute-start | bytes 3145736 | tf_op jit(solution)/shard_map/ppermute | solution.py:243
  386.1 89.0 %collective-permute-start.30 = (bf16[256,2048]{1,0:T(8,128)(2,1)}, bf16[256,2048]{1,0:T(8,128)(2,1)}, u32[]{:S(2)}, u32[]{:S(2)}) collective-permute-start(bf16[256,2048]{1,0:T(8,128)(2,1)} %collective-permute-done.28), channel_id=1, source_target_pairs={{0,4},{4,0},{24,28},{28,24},{1,5},{5,1},{25,29},{29,25},{2,6},{6,2... | collective-permute-start | bytes 3145736 | tf_op jit(solution)/shard_map/ppermute | solution.py:243
  392.7 85.1 %collective-permute-start.37 = (bf16[1024,512]{1,0:T(8,128)(2,1)}, bf16[1024,512]{1,0:T(8,128)(2,1)}, u32[]{:S(2)}, u32[]{:S(2)}) collective-permute-start(bf16[1024,512]{1,0:T(8,128)(2,1)} %collective-permute-done.35), channel_id=1, source_target_pairs={{8,12},{12,8},{16,20},{20,16},{9,13},{13,9},{17,21},{21,17},{10,14... | collective-permute-start | bytes 3145736 | tf_op jit(solution)/shard_map/ppermute | solution.py:243
  397.2 80.5 %collective-permute-start.38 = (bf16[1024,512]{1,0:T(8,128)(2,1)}, bf16[1024,512]{1,0:T(8,128)(2,1)}, u32[]{:S(2)}, u32[]{:S(2)}) collective-permute-start(bf16[1024,512]{1,0:T(8,128)(2,1)} %collective-permute-done.36), channel_id=1, source_target_pairs={{0,4},{4,0},{24,28},{28,24},{1,5},{5,1},{25,29},{29,25},{2,6},{6,2... | collective-permute-start | bytes 3145736 | tf_op jit(solution)/shard_map/ppermute | solution.py:243
  398.9 97.3 %collective-permute-start.22 = (bf16[384,2176]{0,1:T(8,128)(2,1)}, bf16[384,2176]{0,1:T(8,128)(2,1)}, u32[]{:S(2)}, u32[]{:S(2)}) collective-permute-start(bf16[384,2176]{0,1:T(8,128)(2,1)} %pad_maximum_fusion.8), channel_id=1, source_target_pairs={{0,1},{1,0},{2,3},{3,2},{4,5},{5,4},{6,7},{7,6},{8,9},{9,8},{10,11... | collective-permute-start | bytes 5013512 | tf_op jit(solution)/shard_map/ppermute | solution.py:243
  566.1 62.6 %collective-permute-start.40 = (bf16[384,2176]{0,1:T(8,128)(2,1)}, bf16[384,2176]{0,1:T(8,128)(2,1)}, u32[]{:S(2)}, u32[]{:S(2)}) collective-permute-start(bf16[384,2176]{0,1:T(8,128)(2,1)} %fusion.23), channel_id=1, source_target_pairs={{0,2},{2,0},{1,3},{3,1},{4,6},{6,4},{5,7},{7,5},{8,10},{10,8},{9,1... | collective-permute-start | bytes 5013512 | tf_op jit(solution)/shard_map/ppermute | solution.py:243
  749.4 41.6 %collective-permute-start.62 = (bf16[4,96,128]{2,1,0:T(8,128)(2,1)}, bf16[4,96,128]{2,1,0:T(8,128)(2,1)}, u32[]{:S(2)}, u32[]{:S(2)}) collective-permute-start(bf16[4,96,128]{2,1,0:T(8,128)(2,1)} %pad_maximum_fusion.24), channel_id=1, source_target_pairs={{0,4},{4,0},{1,5},{5,1},{2,6},{6,2},{3,7},{7,3},{8,12},{12,8},{9,1... | collective-permute-start | bytes 294920 | tf_op jit(solution)/shard_map/ppermute | solution.py:243
  (166 other events, 2511.7 us)

commit v2 on v1

v2 whole, which is shorter than its diff:
```python
import jax
import jax.numpy as jnp
from jax import lax
from jax.experimental import pallas as pl
from jax.experimental.pallas import tpu as pltpu
from jax.sharding import PartitionSpec as P

HD = 128
RANK = 16
ADAPTERS = 8
SLOTS = 2
PAIR = SLOTS * RANK
BLOCK = 256
AUG = 128
ROW_CHUNK = 128

layer_eps = 1e-05
factor = 0.5
neg_fill = -1e30
bf16 = jnp.bfloat16
f32 = jnp.float32

CORE_SWAP = [(0, 1), (1, 0), (2, 3), (3, 2)]
X_SWAP = [(0, 2), (2, 0), (1, 3), (3, 1)]


def dot_nn(a, b):
    return lax.dot_general(a, b, (((1,), (0,)), ((), ())), preferred_element_type=f32)


def dot_nt(a, b):
    return lax.dot_general(a, b, (((1,), (1,)), ((), ())), preferred_element_type=f32)


def dot_tn(a, b):
    return lax.dot_general(a, b, (((0,), (0,)), ((), ())), preferred_element_type=f32)


def round_low(v):
    return lax.reduce_precision(v, 8, 7).astype(bf16)


def standardize(rows):
    centre = rows - jnp.mean(rows, axis=-1, keepdims=True)
    spread = jnp.mean(centre * centre, axis=-1, keepdims=True)
    inverse = lax.rsqrt(spread + layer_eps)
    return centre * inverse, inverse


def norm_back(grad_scaled, unit, inverse):
    first = jnp.mean(grad_scaled, axis=-1, keepdims=True)
    second = jnp.mean(grad_scaled * unit, axis=-1, keepdims=True)
    return inverse * (grad_scaled - first - unit * second)


def ancestry(parents):
    total = parents.shape[0]
    position = jnp.arange(total, dtype=jnp.int32)
    reach = (
        (parents[:, None] == position[None, :]) | (position[:, None] == position[None, :])
    ).astype(f32)
    span = 1
    while span < total:
        reach = jnp.minimum(jnp.sum(reach[:, :, None] * reach[None, :, :], axis=1), 1.0)
        span *= 2
    roots = (parents < 0).astype(f32)
    order = jnp.sum(jnp.where(position[None, :] <= position[:, None], roots[None, :], 0.0), axis=1)
    slot = jnp.sum(reach * (roots * (order - 1.0))[None, :], axis=1)
    return reach, slot


def attend_forward(qkv, far, far_bias, own_bias, heads, scale):
    tokens = qkv.shape[0]
    far_rows = far.shape[0]
    blocks = tokens // BLOCK

    def kernel(q_ref, k_ref, v_ref, fk_ref, fv_ref, fb_ref, ob_ref, o_ref, pf_ref, po_ref):
        far_k = fk_ref[...]
        far_v = fv_ref[...]
        for b in range(blocks):
            rows = slice(b * BLOCK, (b + 1) * BLOCK)
            width = (b + 1) * BLOCK
            q = q_ref[rows, :]
            s_far = dot_nt(q, far_k) * scale + fb_ref[b : b + 1, :]
            s_own = dot_nt(q, k_ref[:width, :]) * scale + ob_ref[b : b + 1, :width]
            q_pos = lax.broadcasted_iota(jnp.int32, (BLOCK, width), 0) + b * BLOCK
            k_pos = lax.broadcasted_iota(jnp.int32, (BLOCK, width), 1)
            s_own = jnp.where(k_pos <= q_pos, s_own, neg_fill)
            top = jnp.maximum(
                jnp.max(s_far, axis=1, keepdims=True), jnp.max(s_own, axis=1, keepdims=True)
            )
            p_far = jnp.exp(s_far - top)
            p_own = jnp.exp(s_own - top)
            total = jnp.sum(p_far, axis=1, keepdims=True) + jnp.sum(p_own, axis=1, keepdims=True)
            inverse = 1.0 / total
            p_far = (p_far * inverse).astype(bf16)
            p_own = (p_own * inverse).astype(bf16)
            pf_ref[0, rows, :] = p_far
            po_ref[0, rows, :width] = p_own
            o_ref[rows, :] = dot_nn(p_far, far_v) + dot_nn(p_own, v_ref[:width, :])

    return pl.pallas_call(
        kernel,
        grid=(heads,),
        in_specs=[
            pl.BlockSpec((tokens, HD), lambda h: (0, h)),
            pl.BlockSpec((tokens, HD), lambda h: (0, heads + h)),
            pl.BlockSpec((tokens, HD), lambda h: (0, 2 * heads + h)),
            pl.BlockSpec((far_rows, HD), lambda h: (0, h)),
            pl.BlockSpec((far_rows, HD), lambda h: (0, heads + h)),
            pl.BlockSpec((blocks, far_rows), lambda h: (0, 0)),
            pl.BlockSpec((blocks, tokens), lambda h: (0, 0)),
        ],
        out_specs=[
            pl.BlockSpec((tokens, HD), lambda h: (0, h)),
            pl.BlockSpec((1, tokens, far_rows), lambda h: (h, 0, 0)),
            pl.BlockSpec((1, tokens, tokens), lambda h: (h, 0, 0)),
        ],
        out_shape=[
            jax.ShapeDtypeStruct((tokens, heads * HD), f32),
            jax.ShapeDtypeStruct((heads, tokens, far_rows), bf16),
            jax.ShapeDtypeStruct((heads, tokens, tokens), bf16),
        ],
        compiler_params=pltpu.CompilerParams(vmem_limit_bytes=56 << 20),
        name="attend_forward",
    )(qkv, qkv, qkv, far, far, far_bias, own_bias)


def attend_backward(qkv, far, grad_attended, attended, probs_far, probs_own, heads, scale):
    tokens = qkv.shape[0]
    far_rows = far.shape[0]
    blocks = tokens // BLOCK

    def kernel(
        q_ref, k_ref, v_ref, fk_ref, fv_ref, g_ref, o_ref, pf_ref, po_ref,
        dq_ref, dk_ref, dv_ref, dfk_ref, dfv_ref,
        dk_acc, dv_acc, dfk_acc, dfv_acc,
    ):
        far_k = fk_ref[...]
        far_v = fv_ref[...]
        for b in reversed(range(blocks)):
            first = b == blocks - 1
            rows = slice(b * BLOCK, (b + 1) * BLOCK)
            width = (b + 1) * BLOCK
            q = q_ref[rows, :]
            g = g_ref[rows, :]
            row_dot = jnp.sum(g.astype(f32) * o_ref[rows, :], axis=1, keepdims=True)
            p_far = pf_ref[0, rows, :]
            p_own = po_ref[0, rows, :width]
            d_far = (p_far.astype(f32) * (dot_nt(g, far_v) - row_dot)).astype(bf16)
            d_own = (p_own.astype(f32) * (dot_nt(g, v_ref[:width, :]) - row_dot)).astype(bf16)
            dq_ref[rows, :] = (
                (dot_nn(d_far, far_k) + dot_nn(d_own, k_ref[:width, :])) * scale
            ).astype(bf16)
            if first:
                dfk_acc[...] = dot_tn(d_far, q)
                dfv_acc[...] = dot_tn(p_far, g)
                dk_acc[...] = dot_tn(d_own, q)
                dv_acc[...] = dot_tn(p_own, g)
            else:
                dfk_acc[...] += dot_tn(d_far, q)
                dfv_acc[...] += dot_tn(p_far, g)
                dk_acc[:width, :] += dot_tn(d_own, q)
                dv_acc[:width, :] += dot_tn(p_own, g)
        dk_ref[...] = (dk_acc[...] * scale).astype(bf16)
        dv_ref[...] = dv_acc[...].astype(bf16)
        dfk_ref[...] = (dfk_acc[...] * scale).astype(bf16)
        dfv_ref[...] = dfv_acc[...].astype(bf16)

    head_spec = pl.BlockSpec((tokens, HD), lambda h: (0, h))
    far_spec = pl.BlockSpec((far_rows, HD), lambda h: (0, h))
    own_shape = jax.ShapeDtypeStruct((tokens, heads * HD), bf16)
    far_shape = jax.ShapeDtypeStruct((far_rows, heads * HD), bf16)
    return pl.pallas_call(
        kernel,
        grid=(heads,),
        in_specs=[
            head_spec,
            pl.BlockSpec((tokens, HD), lambda h: (0, heads + h)),
            pl.BlockSpec((tokens, HD), lambda h: (0, 2 * heads + h)),
            far_spec,
            pl.BlockSpec((far_rows, HD), lambda h: (0, heads + h)),
            head_spec,
            head_spec,
            pl.BlockSpec((1, tokens, far_rows), lambda h: (h, 0, 0)),
            pl.BlockSpec((1, tokens, tokens), lambda h: (h, 0, 0)),
        ],
        out_specs=[head_spec, head_spec, head_spec, far_spec, far_spec],
        out_shape=[own_shape, own_shape, own_shape, far_shape, far_shape],
        scratch_shapes=[
            pltpu.VMEM((tokens, HD), f32),
            pltpu.VMEM((tokens, HD), f32),
            pltpu.VMEM((far_rows, HD), f32),
            pltpu.VMEM((far_rows, HD), f32),
        ],
        compiler_params=pltpu.CompilerParams(vmem_limit_bytes=56 << 20),
        name="attend_backward",
    )(qkv, qkv, qkv, far, far, grad_attended, attended, probs_far, probs_own)


def assemble(spot, pieces, tail, rows, columns, step, parts):
    direction, shard, half_rows = step
    count = max(parts, 1)
    part_columns = columns // count if parts else columns
    tail_rows, tail_columns = tail.shape

    def kernel(spot_ref, *refs):
        own, one, y_one = refs[:3]
        in_two, y_in_two, out_two, y_out_two, in_far, y_in_far, out_far, y_out_far = refs[3:11]
        tail_ref, out, sem = refs[11:]
        group = spot_ref[0]
        context = spot_ref[1]
        inner = (group == 1) | (group == 2)

        def moves(piece, source, which, first):
            made = []
            for i in range(count):
                src = piece.at[i] if parts else piece
                n, m = src.shape
                if direction == "rows":
                    row = pl.multiple_of(source * shard + which * half_rows, half_rows)
                    dst = out.at[pl.ds(row, n), pl.ds(i * part_columns, m)]
                else:
                    row = pl.multiple_of(which * half_rows, half_rows)
                    col = pl.multiple_of(source * shard, shard)
                    dst = out.at[pl.ds(row, n), pl.ds(col, m)]
                made.append(pltpu.make_async_copy(src, dst, sem.at[first + i]))
            return made

        fixed = moves(own, group, 0, 0)
        fixed += moves(one, group ^ 1, context, count)
        fixed += moves(y_one, group ^ 1, 1 - context, 2 * count)
        row0 = rows - tail_rows if direction == "rows" else 0
        col0 = 0 if direction == "rows" else columns - tail_columns
        fixed.append(
            pltpu.make_async_copy(
                tail_ref,
                out.at[pl.ds(row0, tail_rows), pl.ds(col0, tail_columns)],
                sem.at[7 * count],
            )
        )
        inside = moves(in_two, group ^ 2, context, 3 * count)
        inside += moves(y_in_two, group ^ 2, 1 - context, 4 * count)
        inside += moves(in_far, group ^ 3, context, 5 * count)
        inside += moves(y_in_far, group ^ 3, 1 - context, 6 * count)
        outside = moves(out_two, group ^ 2, context, 3 * count)
        outside += moves(y_out_two, group ^ 2, 1 - context, 4 * count)
        outside += moves(out_far, group ^ 3, context, 5 * count)
        outside += moves(y_out_far, group ^ 3, 1 - context, 6 * count)
        for move in fixed:
            move.start()

        @pl.when(inner)
        def _():
            for move in inside:
                move.start()
            for move in inside:
                move.wait()

        @pl.when(jnp.logical_not(inner))
        def _():
            for move in outside:
                move.start()
            for move in outside:
                move.wait()

        for move in fixed:
            move.wait()

    return pl.pallas_call(
        kernel,
        grid_spec=pltpu.PrefetchScalarGridSpec(
            num_scalar_prefetch=1,
            grid=(),
            in_specs=[pl.BlockSpec(memory_space=pl.ANY)] * 12,
            out_specs=pl.BlockSpec(memory_space=pltpu.VMEM),
            scratch_shapes=[pltpu.SemaphoreType.DMA((7 * count + 1,))],
        ),
        out_shape=jax.ShapeDtypeStruct((rows, columns), bf16),
        compiler_params=pltpu.CompilerParams(vmem_limit_bytes=24 << 20),
        name="assemble",
    )(spot, *pieces, tail)


def assemble_gathered(spot, own, gathered, swapped, tail, rows, columns, direction):
    shard_rows, shard_columns = own.shape
    shard = shard_rows if direction == "rows" else shard_columns
    half = shard_rows // 2
    chunks = len(gathered)
    size = half // chunks
    tail_rows, tail_columns = tail.shape
    copies = 7 * chunks + 2

    def kernel(spot_ref, *refs):
        own_ref = refs[0]
        near = refs[1 : 1 + chunks]
        cross = refs[1 + chunks : 1 + 2 * chunks]
        tail_ref, out, sem = refs[1 + 2 * chunks :]
        group = spot_ref[0]
        context = spot_ref[1]
        moves = []

        def move(src, source, which, chunk_row):
            count, width = src.shape
            row = which * half + chunk_row
            if direction == "rows":
                dst = out.at[
                    pl.ds(pl.multiple_of(source * shard + row, size), count), pl.ds(0, width)
                ]
            else:
                dst = out.at[
                    pl.ds(pl.multiple_of(row, size), count),
                    pl.ds(pl.multiple_of(source * shard, shard), width),
                ]
            moves.append(pltpu.make_async_copy(src, dst, sem.at[len(moves)]))

        for j in range(chunks):
            for g in range(4):
                move(near[j].at[pl.ds(g * size, size)], g, context, j * size)
            for i in range(3):
                move(
                    cross[j].at[pl.ds(i * size, size)], group ^ (i + 1), 1 - context, j * size
                )
        move(
            own_ref.at[pl.ds(pl.multiple_of((1 - context) * half, half), half)],
            group,
            1 - context,
            0,
        )
        row0 = rows - tail_rows if direction == "rows" else 0
        col0 = 0 if direction == "rows" else columns - tail_columns
        moves.append(
            pltpu.make_async_copy(
                tail_ref,
                out.at[pl.ds(row0, tail_rows), pl.ds(col0, tail_columns)],
                sem.at[len(moves)],
            )
        )
        for m in moves:
            m.start()
        for m in moves:
            m.wait()

    return pl.pallas_call(
        kernel,
        grid_spec=pltpu.PrefetchScalarGridSpec(
            num_scalar_prefetch=1,
            grid=(),
            in_specs=[pl.BlockSpec(memory_space=pl.ANY)] * (2 + 2 * chunks),
            out_specs=pl.BlockSpec(memory_space=pltpu.VMEM),
            scratch_shapes=[pltpu.SemaphoreType.DMA((copies,))],
        ),
        out_shape=jax.ShapeDtypeStruct((rows, columns), bf16),
        compiler_params=pltpu.CompilerParams(vmem_limit_bytes=24 << 20),
        name="assemble_gathered",
    )(spot, own, *gathered, *swapped, tail)


def norm_wide(pieces, places, slots, down_rows, gain, shift, tokens):
    width = gain.shape[1]
    blocks = tokens // BLOCK
    count = len(pieces)
    quarter = tokens // 4
    steps = 4 // count

    def kernel(place_ref, slot_ref, *refs):
        down_ref, gain_ref, shift_ref, out_ref = refs[count:]
        for i in range(4):
            x_ref = refs[i // steps]
            first = (i % steps) * quarter
            rows = x_ref[first : first + quarter, :].astype(f32)
            start = pl.multiple_of(place_ref[i] * quarter, quarter)
            unit, _ = standardize(rows)
            low = (unit * gain_ref[...] + shift_ref[...]).astype(bf16)
            block = (lax.broadcasted_iota(jnp.int32, (quarter, AUG), 0) + start) // BLOCK
            lane_slot = (lax.broadcasted_iota(jnp.int32, (quarter, AUG), 1) // RANK) % SLOTS
            slot = jnp.zeros((quarter, AUG), jnp.int32)
            for b in range(blocks):
                slot = jnp.where(block == b, slot_ref[b], slot)
            down = jnp.where(slot == lane_slot, dot_nt(low, down_ref[...]), 0.0)
            out_ref[pl.ds(start, quarter), :width] = low
            out_ref[pl.ds(start, quarter), width:] = factor * down.astype(bf16)

    whole = pl.BlockSpec(memory_space=pltpu.VMEM)
    return pl.pallas_call(
        kernel,
        grid_spec=pltpu.PrefetchScalarGridSpec(
            num_scalar_prefetch=2,
            grid=(),
            in_specs=[whole] * (count + 3),
            out_specs=whole,
        ),
        out_shape=jax.ShapeDtypeStruct((tokens, width + AUG), bf16),
        compiler_params=pltpu.CompilerParams(vmem_limit_bytes=32 << 20),
        name="norm_wide",
    )(places, slots, *pieces, down_rows, gain, shift)


def own_pick(first_row, count, slot_ref, blocks):
    block = (lax.broadcasted_iota(jnp.int32, (count, AUG), 0) + first_row) // BLOCK
    lane_slot = (lax.broadcasted_iota(jnp.int32, (count, AUG), 1) // RANK) % SLOTS
    slot = jnp.zeros((count, AUG), jnp.int32)
    for b in range(blocks):
        slot = jnp.where(block == b, slot_ref[b], slot)
    return slot == lane_slot


def row_call(body, name, core, slots, rows, moving, fixed, outs):
    chunk = ROW_CHUNK
    steps = rows // chunk
    blocks = slots.shape[0]
    n_in = len(moving) + len(fixed)

    def kernel(core_ref, slot_ref, *refs):
        first = core_ref[0] * rows + pl.program_id(0) * chunk
        pick = own_pick(first, chunk, slot_ref, blocks)
        results = body(pick, *[r[...] for r in refs[:n_in]])
        for ref, value in zip(refs[n_in:], results):
            ref[...] = value

    specs = []
    for array, offset in moving:
        if offset:
            specs.append(
                pl.BlockSpec((chunk, array.shape[1]), lambda i, c, s: (c[0] * steps + i, 0))
            )
        else:
            specs.append(pl.BlockSpec((chunk, array.shape[1]), lambda i, c, s: (i, 0)))
    for array in fixed:
        specs.append(pl.BlockSpec(array.shape, lambda i, c, s: (0, 0)))
    return pl.pallas_call(
        kernel,
        grid_spec=pltpu.PrefetchScalarGridSpec(
            num_scalar_prefetch=2,
            grid=(steps,),
            in_specs=specs,
            out_specs=[pl.BlockSpec((chunk, c), lambda i, c_, s: (i, 0)) for c, _ in outs],
        ),
        out_shape=[jax.ShapeDtypeStruct((rows, c), d) for c, d in outs],
        compiler_params=pltpu.CompilerParams(vmem_limit_bytes=40 << 20),
        name=name,
    )(core, slots, *[a for a, _ in moving], *fixed)


def after_attention(pick, mine, far, rows, exit_row, gain, shift, b_o_rows, a_up_rows):
    width = rows.shape[1]
    total = mine.astype(f32) + far.astype(f32)
    down_o = factor * jnp.where(pick, total[:, width:], 0.0).astype(bf16)
    middle = rows.astype(f32) + total[:, :width] + exit_row + dot_nn(down_o, b_o_rows)
    unit, _ = standardize(middle)
    low = (unit * gain + shift).astype(bf16)
    down_up = factor * jnp.where(pick, dot_nt(low, a_up_rows), 0.0).astype(bf16)
    return middle, jnp.concatenate([low, down_up + down_o], axis=1)


def after_hidden(pick, mine, far, middle, exit_row, b_down_rows):
    width = middle.shape[1]
    total = mine.astype(f32) + far.astype(f32)
    down = factor * jnp.where(pick, total[:, width:], 0.0).astype(bf16)
    out = middle + total[:, :width] + exit_row + dot_nn(down, b_down_rows)
    return (jnp.concatenate([out.astype(bf16), down], axis=1),)


def back_middle(pick, mine, far, middle, loss, gain, a_up_rows, b_o_rows):
    width = middle.shape[1]
    total = mine.astype(f32) + far.astype(f32)
    grad_down = (factor * jnp.where(pick, total[:, width:], 0.0)).astype(bf16)
    grad_normed = total[:, :width] + dot_nn(grad_down, a_up_rows)
    unit, inverse = standardize(middle)
    grad = loss.astype(f32) + norm_back(grad_normed * gain, unit, inverse)
    low = grad.astype(bf16)
    grad_o = (factor * jnp.where(pick, dot_nt(low, b_o_rows), 0.0)).astype(bf16)
    return grad, jnp.concatenate([low, grad_o + grad_down], axis=1)


def back_first(pick, mine, far, grad_down, rows, grad_middle, gain, a_rows):
    total = mine.astype(f32) + far.astype(f32)
    grad_normed = total + dot_nn(grad_down, a_rows)
    unit, inverse = standardize(rows.astype(f32))
    return ((grad_middle + norm_back(grad_normed * gain, unit, inverse)).astype(bf16),)


def pack_terms(tensor, two, back, attended, grad_pre, hidden, grad_dd, dd, loss, local):
    width = loss.shape[1]
    cut = local // 4

    def kernel(t_ref, two_ref, back_ref, att_ref, gp_ref, hid_ref, gdd_ref, dd_ref, loss_ref, out):
        lanes = pl.ds(pl.multiple_of(t_ref[0] * local, local), local)
        two_tail = two_ref[:, width:]
        back_tail = back_ref[:, width:]
        terms = [
            dot_tn(back_tail, att_ref[...])[PAIR : 2 * PAIR],
            dot_tn(two_tail, back_ref[:, lanes])[PAIR : 2 * PAIR],
            dot_tn(back_tail, two_ref[:, lanes])[:PAIR],
            dot_tn(dd_ref[...], loss_ref[:, lanes])[:PAIR],
        ]
        for n, term in enumerate(terms):
            low = term.astype(bf16)
            for g in range(4):
                out[g, n * PAIR : (n + 1) * PAIR, :] = low[:, g * cut : (g + 1) * cut]
        base = len(terms) * PAIR
        for left, right in ((two_tail, gp_ref), (gdd_ref[...], hid_ref)):
            low = dot_tn(left, right[...])[:PAIR].astype(bf16)
            tiles = low.shape[1] // (4 * cut)
            for g in range(4):
                for t in range(tiles):
                    c = (g * tiles + t) * cut
                    out[g, base + t * PAIR : base + (t + 1) * PAIR, :] = low[:, c : c + cut]
            base += tiles * PAIR

    tiles = hidden.shape[1] // local
    whole = pl.BlockSpec(memory_space=pltpu.VMEM)
    return pl.pallas_call(
        kernel,
        grid_spec=pltpu.PrefetchScalarGridSpec(
            num_scalar_prefetch=1, grid=(), in_specs=[whole] * 8, out_specs=whole
        ),
        out_shape=jax.ShapeDtypeStruct((4, (4 + 2 * tiles) * PAIR, cut), bf16),
        compiler_params=pltpu.CompilerParams(vmem_limit_bytes=40 << 20),
        name="pack_terms",
    )(tensor, two, back, attended, grad_pre, hidden, grad_dd, dd, loss)


def pack_projections(tensor, grad_down, normed_wide, grad_qkv, local):
    width = normed_wide.shape[1] - AUG
    cut = local // 4

    def kernel(t_ref, gd_ref, nw_ref, gq_ref, out):
        lanes = pl.ds(pl.multiple_of(t_ref[0] * local, local), local)
        down = dot_tn(gd_ref[...], nw_ref[:, lanes]).astype(bf16)
        up = dot_tn(nw_ref[:, width:], gq_ref[...]).astype(bf16)
        for i in range(3):
            rows = slice(i * PAIR, (i + 1) * PAIR)
            for g in range(4):
                out[g, rows, :] = down[rows, g * cut : (g + 1) * cut]
                c = i * local + g * cut
                out[g, (3 + i) * PAIR : (4 + i) * PAIR, :] = up[rows, c : c + cut]

    whole = pl.BlockSpec(memory_space=pltpu.VMEM)
    return pl.pallas_call(
        kernel,
        grid_spec=pltpu.PrefetchScalarGridSpec(
            num_scalar_prefetch=1, grid=(), in_specs=[whole] * 3, out_specs=whole
        ),
        out_shape=jax.ShapeDtypeStruct((4, 6 * PAIR, cut), bf16),
        compiler_params=pltpu.CompilerParams(vmem_limit_bytes=24 << 20),
        name="pack_projections",
    )(tensor, grad_down, normed_wide, grad_qkv)


def unpack_terms(context, owner, near, cross, tiles):
    cut = near.shape[2]
    half = cut // 2
    base = (4 + 2 * tiles) * PAIR

    def kernel(c_ref, owner_ref, near_ref, cross_ref, a_attn, b_attn, a_up, b_up, a_down, b_down):
        first = c_ref[0] == 0

        for k in range(4):
            for s in range(SLOTS):
                who = owner_ref[k * SLOTS + s]

                def value(row):
                    rows = slice(row + s * RANK, row + (s + 1) * RANK)
                    return near_ref[k, rows, :].astype(f32) + cross_ref[k, rows, :].astype(f32)

                def narrow(row):
                    v = value(row)
                    return jnp.where(first, v[:, :half], v[:, half:])

                for i in range(3):
                    a_attn[i, pl.ds(who, 1)] = narrow(base + i * PAIR)[None]
                    b_attn[i, pl.ds(who, 1)] = narrow(base + (3 + i) * PAIR)[None]
                a_attn[3, pl.ds(who, 1)] = narrow(0)[None]
                b_attn[3, pl.ds(who, 1)] = narrow(PAIR)[None]
                a_up[pl.ds(who, 1)] = narrow(2 * PAIR)[None]
                b_down[pl.ds(who, 1)] = narrow(3 * PAIR)[None]
                for n, ref in enumerate((b_up, a_down)):
                    start = (4 + n * tiles) * PAIR
                    for t in range(tiles // 2):
                        ref[pl.ds(who, 1), :, t * cut : (t + 1) * cut] = jnp.where(
                            first,
                            value(start + t * PAIR),
                            value(start + (tiles // 2 + t) * PAIR),
                        )[None]

    narrow_shape = (ADAPTERS, RANK, half)
    wide_shape = (ADAPTERS, RANK, tiles * half)
    whole = pl.BlockSpec(memory_space=pltpu.VMEM)
    shapes = [(4,) + narrow_shape, (4,) + narrow_shape, narrow_shape, wide_shape, wide_shape, narrow_shape]
    return pl.pallas_call(
        kernel,
        grid_spec=pltpu.PrefetchScalarGridSpec(
            num_scalar_prefetch=2, grid=(), in_specs=[whole] * 2, out_specs=[whole] * 6
        ),
        out_shape=[jax.ShapeDtypeStruct(shape, f32) for shape in shapes],
        compiler_params=pltpu.CompilerParams(vmem_limit_bytes=24 << 20),
        name="unpack_terms",
    )(context, owner, near, cross)


def unpack_plain(context, owner, total, tiles, ctx_size):
    cut = total.shape[2]
    place = (jnp.arange(ADAPTERS, dtype=jnp.int32)[:, None] == owner[None, :]).astype(f32)
    parts = total.reshape(4, -1, SLOTS, RANK, cut)
    placed = jnp.einsum("ag,ngrc->narc", place, jnp.transpose(parts, (1, 0, 2, 3, 4)).reshape(
        parts.shape[1], 4 * SLOTS, RANK, cut), precision=lax.Precision.HIGHEST)

    def narrow(items):
        size = items.shape[-1] // ctx_size
        return lax.dynamic_slice_in_dim(items, context * size, size, items.ndim - 1)

    def broad(items):
        joined = jnp.transpose(items, (1, 2, 0, 3)).reshape(ADAPTERS, RANK, -1)
        return narrow(joined)

    base = 4 + 2 * tiles
    return (
        narrow(jnp.concatenate([placed[base : base + 3], placed[:1]])),
        narrow(jnp.concatenate([placed[base + 3 : base + 6], placed[1:2]])),
        narrow(placed[2]),
        broad(placed[4 : 4 + tiles]),
        broad(placed[4 + tiles : 4 + 2 * tiles]),
        narrow(placed[3]),
    )


def gate(value, *waits):
    if not waits:
        return value
    return lax.optimization_barrier((value,) + waits)[0]


def make_body(ctx_size):
    pair_ctx = ctx_size == 2

    def body(
        inputs,
        loss_sensitivity,
        parent_block,
        adapter_of,
        w_qkv,
        bias_qv,
        w_o,
        exit_offsets,
        ln_gain,
        ln_bias,
        w_in,
        hidden_offset_frozen,
        w_out,
        a_attn,
        b_attn,
        a_up,
        b_up,
        a_down,
        b_down,
    ):
        group = lax.axis_index("fsdp")
        context = lax.axis_index("ctx")
        tensor = lax.axis_index("tp")
        core = tensor % 2
        tokens, width = inputs.shape
        half = tokens // 2
        local = w_qkv.shape[2]
        shard = w_qkv.shape[1]
        hidden_local = w_in.shape[1]
        heads = local // HD
        blocks = tokens // BLOCK
        scale = HD ** (-0.5)
        wide = width + AUG

        def on(value, axis, pairs):
            return lax.ppermute(value, axis, pairs)

        def own_rows(matrix):
            return lax.dynamic_slice_in_dim(matrix, core * half, half, 0)

        def other_rows(matrix):
            return lax.dynamic_slice_in_dim(matrix, (1 - core) * half, half, 0)

        def natural(own, other):
            return jnp.concatenate(
                [jnp.where(core == 0, own, other), jnp.where(core == 0, other, own)], axis=0
            )

        def local_lanes(matrix):
            return lax.dynamic_slice_in_dim(matrix, tensor * local, local, matrix.ndim - 1)

        def put(buffer, piece, row, column):
            return lax.dynamic_update_slice(buffer, piece, (row, column))

        swap_y = [(0, 1), (1, 0)]
        spot = jnp.stack([group, context]).astype(jnp.int32)

        def spread_weight(own, half_axis, first_waits, last_waits):
            size = own.shape[half_axis] // 2
            both = ("fsdp", "ctx")
            inner_y = [(2, 3), (3, 2), (4, 5), (5, 4)]
            outer_y = [(0, 1), (1, 0), (6, 7), (7, 6)]
            outward = [(1, 0), (2, 3)]
            part = lax.dynamic_slice_in_dim(own, context * size, size, half_axis)
            one = on(part, "fsdp", [(0, 1), (1, 0), (2, 3), (3, 2)])
            in_far = on(part, "fsdp", [(1, 2), (2, 1)])
            one, in_far, *first = lax.optimization_barrier((one, in_far, *first_waits))
            y_one = on(one, "ctx", swap_y)
            y_in_far = on(in_far, both, inner_y)
            out_two = on(in_far, "fsdp", outward)
            in_two = on(one, "fsdp", [(1, 2), (2, 1)])
            y_one, out_two, in_two = lax.optimization_barrier((y_one, out_two, in_two))
            out_far = on(in_two, "fsdp", outward)
            y_out_two = on(out_two, both, outer_y)
            y_in_two = on(in_two, both, inner_y)
            out_far, y_out_two, *last = lax.optimization_barrier((out_far, y_out_two, *last_waits(*first)))
            y_out_far = on(out_far, both, outer_y)
            pieces = (own, one, y_one, in_two, y_in_two, out_two, y_out_two)
            pieces += (in_far, y_in_far, out_far, y_out_far)
            return pieces, last, (in_two, out_two), (out_far,)

        def gather_weight(own, chunks, waits, swap_waits=()):
            half_rows = own.shape[0] // 2
            size = half_rows // chunks
            gathered = []
            swapped = []
            for j in range(chunks):
                part = lax.dynamic_slice_in_dim(own, context * half_rows + j * size, size, 0)
                part = gate(part, *waits)
                every = lax.all_gather(part, "fsdp", axis=0, tiled=True)
                gathered.append(every)
                every = gate(every, *swap_waits)
                others = jnp.concatenate(
                    [
                        lax.dynamic_slice_in_dim(every, (group ^ i) * size, size, 0)
                        for i in range(1, 4)
                    ],
                    axis=0,
                )
                swapped.append(on(others, "ctx", swap_y))
            return gathered, swapped

        def send_tp(other_low, own_full):
            got = on(other_low, "tp", CORE_SWAP)
            mine = round_low(own_full + got.astype(f32))
            return mine, on(mine, "tp", X_SWAP)

        def sum_sent(sent, waits=()):
            mine, far = sent
            return mine.astype(f32) + gate(far, *waits).astype(f32)

        pair = lax.dynamic_slice_in_dim(adapter_of, group * SLOTS, SLOTS)

        def pick_pair(array, axis):
            return jnp.concatenate(
                [lax.dynamic_slice_in_dim(array, pair[s], 1, axis) for s in range(SLOTS)], axis
            )

        a_pair = jnp.swapaxes(pick_pair(a_attn, 1), 2, 3)
        def down_up_pad(matrix, before=0):
            return jnp.pad(matrix, ((before, AUG - before - matrix.shape[0]), (0, 0)))

        a_qkv_rows = down_up_pad(a_pair[:3].reshape(3 * PAIR, width).astype(bf16))
        a_o_rows = local_lanes(a_pair[3].reshape(PAIR, width)).astype(bf16)
        b_pair = pick_pair(b_attn, 1)
        b_qkv_rows = local_lanes(b_pair[:3]).reshape(3, PAIR, local).astype(bf16)
        b_o_rows = down_up_pad(b_pair[3].reshape(PAIR, width).astype(bf16), PAIR)
        a_up_rows = down_up_pad(
            jnp.swapaxes(pick_pair(a_up, 0), 1, 2).reshape(PAIR, width).astype(bf16)
        )
        b_up_rows = pick_pair(b_up, 0).reshape(PAIR, hidden_local).astype(bf16)
        a_down_rows = (
            jnp.swapaxes(pick_pair(a_down, 0), 1, 2).reshape(PAIR, hidden_local).astype(bf16)
        )
        b_down_rows = down_up_pad(pick_pair(b_down, 0).reshape(PAIR, width).astype(bf16))

        def bias_lanes(opened):
            count = opened.shape[1]
            block = jnp.arange(count * BLOCK, dtype=jnp.int32) // BLOCK
            hit = opened[:, :, None] & (block[None, None, :] == jnp.arange(count)[None, :, None])
            return jnp.where(jnp.any(hit, axis=1), 0.0, neg_fill).astype(f32)

        reach, slot = ancestry(parent_block[0])
        all_blocks = reach.shape[0]
        first_block = context * blocks
        far_blocks = blocks if pair_ctx else all_blocks
        reach_rows = lax.dynamic_slice_in_dim(reach, first_block, blocks, 0)
        block_ids = jnp.arange(far_blocks, dtype=jnp.int32)
        far_open = (reach_rows[:, :far_blocks] > 0.5) & (block_ids[None, :] < first_block)
        own_open = lax.dynamic_slice_in_dim(reach_rows, first_block, blocks, 1) > 0.5
        far_bias = bias_lanes(far_open)
        own_bias = bias_lanes(own_open)

        slots = lax.dynamic_slice_in_dim(slot, first_block, blocks).astype(jnp.int32)
        lane_slot = (jnp.arange(AUG, dtype=jnp.int32) // RANK) % SLOTS

        def picks(first_row, count):
            block = (jnp.arange(count, dtype=jnp.int32) + first_row) // BLOCK
            row_slot = jnp.sum(
                jnp.where(block[:, None] == jnp.arange(blocks)[None, :], slots[None, :], 0), axis=1
            )
            return (row_slot[:, None] == lane_slot[None, :]).astype(f32)

        pick_own = picks(core * half, half)

        gain_one, shift_one = ln_gain[0][None, :], ln_bias[0][None, :]
        gain_two, shift_two = ln_gain[1][None, :], ln_bias[1][None, :]

        def widen(low, tail):
            return jnp.concatenate([low, tail], axis=1)

        normed_wide = norm_wide(
            [inputs], jnp.arange(4, dtype=jnp.int32), slots, a_qkv_rows, gain_one, shift_one, tokens
        )
        q_aug = jnp.concatenate(
            [jnp.pad(b_qkv_rows[i], ((0, 0), (i * local, (2 - i) * local))) for i in range(3)]
            + [jnp.zeros((AUG - 3 * PAIR, 3 * local), bf16)],
            axis=0,
        )
        o_aug = down_up_pad(a_o_rows, PAIR).T
        in_aug = down_up_pad(b_up_rows)
        out_aug = down_up_pad(a_down_rows).T
        if pair_ctx:
            quarter = tokens // 4
            sent = lax.dynamic_slice_in_dim(inputs, tensor * quarter, quarter, 0)
            far_quarter = on(sent, "ctx", [(0, 1)])

            def last_waits(quarter_rows):
                return (
                    quarter_rows,
                    on(quarter_rows, "tp", X_SWAP),
                    on(quarter_rows, "tp", CORE_SWAP),
                    normed_wide,
                )

            far_places = jnp.stack([tensor, tensor ^ 2, tensor ^ 1, tensor ^ 3]).astype(jnp.int32)
            q_pieces, last, q_second, q_third = spread_weight(
                w_qkv, 1, (far_quarter,), last_waits
            )
            far_quarter, far_x, far_core, normed_wide = last
            far_both = on(far_x, "tp", CORE_SWAP)
            q_through = (q_pieces[5], q_pieces[7])
            o_near, o_cross = gather_weight(w_o, 1, q_second)
            in_near, in_cross = gather_weight(w_in, 2, q_third)
            q_full = assemble(
                spot, q_pieces, q_aug, wide, 3 * local, ("rows", shard, shard // 2), 3
            )
            o_full = assemble_gathered(spot, w_o, o_near, o_cross, o_aug, local, wide, "columns")
            in_full = assemble_gathered(
                spot, w_in, in_near, in_cross, in_aug, wide, hidden_local, "rows"
            )
            out_near, out_cross = gather_weight(w_out, 2, q_third)
        else:
            own_q = jnp.transpose(w_qkv, (1, 0, 2)).reshape(shard, 3 * local)
            q_full = jnp.concatenate([lax.all_gather(own_q, "fsdp", axis=0, tiled=True), q_aug], 0)
            o_full = jnp.concatenate([lax.all_gather(w_o, "fsdp", axis=1, tiled=True), o_aug], 1)
            in_full = jnp.concatenate([lax.all_gather(w_in, "fsdp", axis=0, tiled=True), in_aug], 0)
            out_full = jnp.concatenate(
                [lax.all_gather(w_out, "fsdp", axis=1, tiled=True), out_aug], 1
            )

        normed, reduced_qkv = normed_wide[:, :width], normed_wide[:, width:]
        zero_bias = jnp.zeros((local,), f32)
        q_bias = jnp.concatenate([bias_qv[0], zero_bias, bias_qv[1]])[None, :]
        qkv = (dot_nn(normed_wide, q_full) + q_bias).astype(bf16)
        if pair_ctx:
            far_wide = norm_wide(
                [far_quarter, far_x, far_core, far_both],
                far_places,
                slot[:blocks].astype(jnp.int32),
                a_qkv_rows,
                gain_one,
                shift_one,
                tokens,
            )
            far_kv = (dot_nn(far_wide, q_full[:, local:]) + q_bias[:, local:]).astype(bf16)
        else:
            far_kv = lax.all_gather(qkv[:, local:], "ctx", axis=0, tiled=True)

        attended_f, probs_far, probs_own = attend_forward(
            qkv, far_kv, far_bias, own_bias, heads, scale
        )
        attended = attended_f.astype(bf16)
        attended_own = own_rows(attended)
        attended_other = other_rows(attended)
        branch_sent = send_tp(
            dot_nn(attended_other, o_full).astype(bf16), dot_nn(attended_own, o_full)
        )
        core_id = core.astype(jnp.int32)[None]
        middle, two_own = row_call(
            after_attention,
            "after_attention",
            core_id,
            slots,
            half,
            [(branch_sent[0], False), (branch_sent[1], False), (inputs, True)],
            [exit_offsets[:1], gain_two, shift_two, b_o_rows, a_up_rows],
            [(width, f32), (wide, bf16)],
        )
        two_other = on(two_own, "tp", CORE_SWAP)
        two_wide = jnp.concatenate([two_own, two_other], axis=0)

        pre_act = dot_nn(two_wide, in_full) + hidden_offset_frozen[None, :]
        phi = 0.5 * (1.0 + lax.erf(pre_act * (2.0 ** -0.5)))
        hidden = (pre_act * phi).astype(bf16)
        slope = (
            phi + pre_act * jnp.exp(-0.5 * pre_act * pre_act) * (0.5 / jnp.pi) ** 0.5
        ).astype(bf16)

        if pair_ctx:
            out_full = assemble_gathered(
                gate(spot, hidden),
                w_out,
                out_near,
                out_cross,
                out_aug,
                hidden_local,
                wide,
                "columns",
            )

        loss_own = own_rows(loss_sensitivity)
        loss_rel = jnp.concatenate([loss_own, other_rows(loss_sensitivity)], axis=0)
        pick_rel = jnp.concatenate([pick_own, picks((1 - core) * half, half)], axis=0)
        grad_down_down = (factor * dot_nt(loss_rel, b_down_rows) * pick_rel).astype(bf16)
        loss_wide = widen(loss_rel, grad_down_down)
        grad_pre = (dot_nt(loss_wide, out_full) * slope.astype(f32)).astype(bf16)
        two_sent = send_tp(
            dot_nt(grad_pre[half:], in_full).astype(bf16), dot_nt(grad_pre[:half], in_full)
        )
        grad_middle, back_own = row_call(
            back_middle,
            "back_middle",
            core_id,
            slots,
            half,
            [
                (two_sent[0], False),
                (two_sent[1], False),
                (middle, False),
                (loss_sensitivity, True),
            ],
            [gain_two, a_up_rows, b_o_rows],
            [(width, f32), (wide, bf16)],
        )
        back_other = on(back_own, "tp", CORE_SWAP)
        grad_attended = natural(
            dot_nt(back_own, o_full).astype(bf16), dot_nt(back_other, o_full).astype(bf16)
        )

        grad_q, grad_k, grad_v, far_grad_k, far_grad_v = attend_backward(
            qkv, far_kv, grad_attended, attended_f, probs_far, probs_own, heads, scale
        )
        late_hidden = gate(hidden, two_sent[0])
        exit_sent = send_tp(
            dot_nn(late_hidden[half:], out_full).astype(bf16), dot_nn(late_hidden[:half], out_full)
        )
        if pair_ctx:
            more_k = on(far_grad_k, "ctx", [(1, 0)])
            more_v = on(far_grad_v, "ctx", [(1, 0)])
        else:
            more_k = lax.psum_scatter(far_grad_k, "ctx", scatter_dimension=0, tiled=True)
            more_v = lax.psum_scatter(far_grad_v, "ctx", scatter_dimension=0, tiled=True)
        (layer_wide,) = row_call(
            after_hidden,
            "after_hidden",
            core_id,
            slots,
            half,
            [(exit_sent[0], False), (gate(exit_sent[1], more_v), False), (middle, False)],
            [exit_offsets[1:], b_down_rows],
            [(wide, bf16)],
        )
        layer_other = on(layer_wide, "tp", CORE_SWAP)
        layer_out = natural(layer_wide[:, :width], layer_other[:, :width])
        down_down_rel = jnp.concatenate([layer_wide[:, width:], layer_other[:, width:]], axis=0)

        grad_qkv = jnp.concatenate(
            [
                grad_q,
                (grad_k.astype(f32) + more_k.astype(f32)).astype(bf16),
                (grad_v.astype(f32) + more_v.astype(f32)).astype(bf16),
            ],
            axis=1,
        )
        low_part = dot_nt(grad_qkv, q_full[width:]).astype(bf16)
        low_core = on(low_part, "tp", CORE_SWAP)
        low_pair = round_low(low_part.astype(f32) + low_core.astype(f32))
        low_far = on(low_pair, "tp", X_SWAP)
        low_sum = low_pair.astype(f32) + low_far.astype(f32)
        grad_down_qkv = (factor * low_sum * picks(0, tokens)).astype(bf16)
        grad_one_other = dot_nt(other_rows(grad_qkv), q_full[:width]).astype(bf16)
        grad_one_own = dot_nt(own_rows(grad_qkv), q_full[:width])
        one_sent = send_tp(grad_one_other, grad_one_own)
        tensor_id = tensor.astype(jnp.int32)[None]
        tiles = hidden_local // local
        packed = pack_terms(
            gate(tensor_id, more_v),
            two_wide,
            jnp.concatenate([back_own, back_other], axis=0),
            jnp.concatenate([attended_own, attended_other], axis=0),
            grad_pre,
            hidden,
            grad_down_down,
            down_down_rel,
            loss_rel,
            local,
        )
        packed_qkv = pack_projections(
            gate(tensor_id, one_sent[0]), grad_down_qkv, normed_wide, grad_qkv, local
        )
        received = []
        for k in range(4):
            piece = jnp.concatenate(
                [
                    lax.dynamic_index_in_dim(packed, group ^ k, 0, keepdims=False),
                    lax.dynamic_index_in_dim(packed_qkv, group ^ k, 0, keepdims=False),
                ],
                axis=0,
            )
            received.append(on(piece, "fsdp", [(i, i ^ k) for i in range(4)]) if k else piece)
        near = jnp.stack(received)
        holder = jnp.stack([group ^ k for k in range(4)])
        owner = adapter_of.reshape(4, SLOTS)[holder].reshape(4 * SLOTS)
        if pair_ctx:
            cross = on(near, "ctx", swap_y)
            adapter_grads = unpack_terms(
                context.astype(jnp.int32)[None], owner, near, cross, tiles
            )
        else:
            adapter_grads = unpack_plain(
                context, owner, lax.psum(near.astype(f32), "ctx"), tiles, ctx_size
            )
        (grad_own,) = row_call(
            back_first,
            "back_first",
            core_id,
            slots,
            half,
            [
                (one_sent[0], False),
                (gate(one_sent[1], adapter_grads[0]), False),
                (grad_down_qkv, True),
                (inputs, True),
                (grad_middle, False),
            ],
            [gain_one, a_qkv_rows],
            [(width, bf16)],
        )
        grad_other = on(grad_own, "tp", CORE_SWAP)
        grad_inputs = natural(grad_own, grad_other)

        out_a_attn, out_b_attn, out_a_up, out_b_up, out_a_down, out_b_down = adapter_grads
        return (
            layer_out,
            grad_inputs,
            jnp.swapaxes(out_a_attn, 2, 3),
            out_b_attn,
            jnp.swapaxes(out_a_up, 1, 2),
            out_b_up,
            jnp.swapaxes(out_a_down, 1, 2),
            out_b_down,
        )

    return body


def solution(mesh):
    in_specs = (
        P(("fsdp", "ctx"), None),
        P(("fsdp", "ctx"), None),
        P("fsdp", None),
        P(),
        P(None, "fsdp", "tp"),
        P(None, "tp"),
        P("tp", "fsdp"),
        P(),
        P(),
        P(),
        P("fsdp", "tp"),
        P("tp"),
        P("tp", "fsdp"),
        P(),
        P(),
        P(),
        P(None, None, "tp"),
        P(None, "tp", None),
        P(),
    )
    out_specs = (
        P(("fsdp", "ctx"), None),
        P(("fsdp", "ctx"), None),
        P(None, None, ("tp", "fsdp", "ctx"), None),
        P(None, None, None, ("tp", "fsdp", "ctx")),
        P(None, ("tp", "fsdp", "ctx"), None),
        P(None, None, ("tp", "fsdp", "ctx")),
        P(None, ("tp", "fsdp", "ctx"), None),
        P(None, None, ("tp", "fsdp", "ctx")),
    )
    return jax.shard_map(
        make_body(mesh.shape["ctx"]),
        mesh=mesh,
        in_specs=in_specs,
        out_specs=out_specs,
        check_vma=False,
    )
```

time: 858 us -> 614 us (0.72); the launches traced: 841 us -> 607 us
  local copies, waits for them, and re-layouts: 282 us -> 63.1 us
  waiting for transfers between devices: 201 us -> 264 us
  other arithmetic: 78.3 us -> 29.6 us
  matrix products: 138 us -> 97.3 us
  starting transfers between devices: 101 us -> 62.8 us
  Pallas kernels: 34.7 us -> 70.8 us
  between operations: 6.88 us -> 19.7 us
    dynamic_update_slice x28 -> x0, local copies, waits for them, and re-layouts: 120 us -> none  [put(): return lax.dynamic_update_slice(buffer, piece, (row, column))]
    pallas_call x0 -> x13, Pallas kernels: none -> 45.3 us  [the longest x4 20.9 us: row_call(): pl.pallas_call(kernel, grid_spec=pltpu.PrefetchScalarGridSpec(num_scalar_...]
    concatenate x15 -> x2, local copies, waits for them, and re-layouts: 41.5 us -> 3.01 us  [the longest x1 2.43 us: body(): two_wide = jnp.concatenate([two_own, two_other], axis=0)]
    ppermute x63 -> x39, starting transfers between devices: 101 us -> 62.4 us  [on(): return lax.ppermute(value, axis, pairs)]
    ppermute x63 -> x39, waiting for transfers between devices: 201 us -> 232 us  [on(): return lax.ppermute(value, axis, pairs)]
    all_gather x0 -> x5, waiting for transfers between devices: none -> 30.8 us  [gather_weight(): every = lax.all_gather(part, 'fsdp', axis=0, tiled=True)]
    unnamed x296 -> x198, local copies, waits for them, and re-layouts: 51.4 us -> 21.9 us
    dot_general x11 -> x7, matrix products: 63.1 us -> 44.3 us  [dot_nn(): lax.dot_general(a, b, (((1,), (0,)), ((), ())), preferred_element_type=f32)]
  transfers between devices with their start and end apart: 63 -> 44, of which waited for: 22 -> 19; matrix products, arithmetic and copies ran while one was open for 44% -> 22% of each run, Pallas kernels for 0% -> 10%
where the time goes in v2:
time: 614 us; the launch traced here: 607 us
  waiting for transfers between devices  264 us (43%)
  matrix products  97.3 us (16%)
  Pallas kernels  70.8 us (12%)
  local copies, waits for them, and re-layouts  63.1 us (10%)
  starting transfers between devices  62.8 us (10%)
  other arithmetic  29.6 us (5%)
  between operations  19.7 us (3%)
    ppermute x39, waiting for transfers between devices, on(): return lax.ppermute(value, axis, pairs)  232 us
    ppermute x39, starting transfers between devices, on(): return lax.ppermute(value, axis, pairs)  62.4 us
    dot_general x9, matrix products, dot_nt(): lax.dot_general(a, b, (((1,), (1,)), ((), ())), preferred_element_type=f32)  53 us
    dot_general x7, matrix products, dot_nn(): lax.dot_general(a, b, (((1,), (0,)), ((), ())), preferred_element_type=f32)  44.3 us
    all_gather x5, waiting for transfers between devices, gather_weight(): every = lax.all_gather(part, 'fsdp', axis=0, tiled=True)  30.8 us
    unnamed x198, local copies, waits for them, and re-layouts  21.9 us
    pallas_call x4, Pallas kernels, row_call(): pl.pallas_call(kernel, grid_spec=pltpu.PrefetchScalarGridSpec(num_scalar_...  20.9 us
    pallas_call x1, Pallas kernels, attend_backward(): pl.pallas_call(kernel, grid=(heads,), in_specs=[head_spec, pl.BlockSpec((...  13.1 us
  transfers between devices with their start and end apart: 44, of which 19 were waited for; matrix products, arithmetic and copies ran while one was open for 22% of the time, Pallas kernels for 10%

profile of v2, /device:TPU:9, one launch (start us, length us, event | category | flops | bytes accessed | tf_op | source)
XLA Modules:
  0.0 607.0 jit_solution(9670292640171283365)
XLA Ops:
  26.8 8.4 %collective-permute-done.2.refs_0_ = bf16[192,2048]{1,0:T(8,128)(2,1)} collective-permute-done((bf16[192,2048]{1,0:T(8,128)(2,1)}, bf16[192,2048]{1,0:T(8,128)(2,1)}, u32[]{:S(2)}, u32[]{:S(2)}) %collective-permute-start.2) | collective-permute-done | bytes 786464 | tf_op jit(solution)/shard_map/ppermute | solution.py:673
  44.0 9.3 %collective-permute-done.3.refs_2_ = bf16[3,256,512]{2,1,0:T(8,128)(2,1)S(1)} collective-permute-done((bf16[3,256,512]{2,1,0:T(8,128)(2,1)}, bf16[3,256,512]{2,1,0:T(8,128)(2,1)S(1)}, u32[]{:S(2)}, u32[]{:S(2)}) %collective-permute-start.3) | collective-permute-done | bytes 786464 | tf_op jit(solution)/shard_map/ppermute | solution.py:673
  79.5 19.4 %collective-permute-done.6.refs_9_ = bf16[3,256,512]{2,1,0:T(8,128)(2,1)} collective-permute-done((bf16[3,256,512]{2,1,0:T(8,128)(2,1)}, bf16[3,256,512]{2,1,0:T(8,128)(2,1)}, u32[]{:S(2)}, u32[]{:S(2)}) %collective-permute-start.6) | collective-permute-done | bytes 786464 | tf_op jit(solution)/shard_map/ppermute | solution.py:673
  116.8 9.6 %collective-permute-done.11.refs_8_ = bf16[3,256,512]{2,1,0:T(8,128)(2,1)} collective-permute-done((bf16[3,256,512]{2,1,0:T(8,128)(2,1)}, bf16[3,256,512]{2,1,0:T(8,128)(2,1)}, u32[]{:S(2)}, u32[]{:S(2)}) %collective-permute-start.11) | collective-permute-done | bytes 786464 | tf_op jit(solution)/shard_map/ppermute | solution.py:673
  126.5 16.9 %collective-permute-done.10.refs_4_ = bf16[3,256,512]{2,1,0:T(8,128)(2,1)} collective-permute-done((bf16[3,256,512]{2,1,0:T(8,128)(2,1)}, bf16[3,256,512]{2,1,0:T(8,128)(2,1)}, u32[]{:S(2)}, u32[]{:S(2)}) %collective-permute-start.10) | collective-permute-done | bytes 786464 | tf_op jit(solution)/shard_map/ppermute | solution.py:673
  146.4 6.9 %add_convert_fusion.q_ref.k_ref.v_ref = bf16[768,1536]{1,0:T(8,128)(2,1)} fusion(bf16[768,2176]{1,0:T(8,128)(2,1)S(1)} %copy-done.2, bf16[2176,1536]{1,0:T(8,128)(2,1)S(1)} %assemble.1, f32[1536]{0:T(1024)S(1)} %copy-done.78), kind=kOutput, calls=%fused_computation.14 | convolution fusion | flops 5136187392 | bytes 12392448 | tf_op jit(solution)/shard_map/dot_general | solution.py:28
  163.9 12.5 %attend_forward.1 = (f32[768,512]{1,0:T(8,128)}, bf16[4,768,768]{2,1,0:T(8,128)(2,1)}, bf16[4,768,768]{2,1,0:T(8,128)(2,1)}) custom-call(bf16[768,1536]{1,0:T(8,128)(2,1)} %add_convert_fusion.q_ref.k_ref.v_ref, bf16[768,1536]{1,0:T(8,128)(2,1)} %add_convert_fusion.q_ref.k_ref.v_ref, bf16[768,1536]{1,0:T(8,128)(2,1)} %add_convert_fusion.q_ref.k_ref.v_ref, ...), custom_call_target="tpu_custom_call" | custom-call | tf_op jit(solution)/shard_map/attend_forward/pallas_call | solution.py:102
  207.5 28.5 %collective-permute-done.16.refs_1_ = bf16[384,2176]{1,0:T(8,128)(2,1)} collective-permute-done((bf16[384,2176]{1,0:T(8,128)(2,1)}, bf16[384,2176]{1,0:T(8,128)(2,1)}, u32[]{:S(2)}, u32[]{:S(2)}) %collective-permute-start.16) | collective-permute-done | bytes 1671200 | tf_op jit(solution)/shard_map/ppermute | solution.py:673
  236.0 6.1 %after_attention.1 = (f32[384,2048]{1,0:T(8,128)S(1)}, bf16[384,2176]{1,0:T(8,128)(2,1)}) custom-call(s32[1]{0:T(128)} %bitcast.core_ref, s32[3]{0:T(128)S(1)} %copy-done.53, bf16[384,2176]{1,0:T(8,128)(2,1)} %fusion.16.refs_0_, bf16[384,2176]{1,0:T(8,128)(2,1)} %collective-permute-done.16.refs_1_, bf16[768,2048]{1,0:T(8,128)(2,1)S(1)} %copy-done, ...), custom_call_target="tpu_custom_call" | custom-call | tf_op jit(solution)/shard_map/after_attention/pallas_call | solution.py:431
  251.0 30.8 %all-gather.14.cloned.1.call-done.refs_2_ = bf16[2048,512]{1,0:T(8,128)(2,1)} async-done(((bf16[512,512]{1,0:T(8,128)(2,1)}), bf16[2048,512]{1,0:T(8,128)(2,1)}) %all-gather.14.cloned.1.call-update) | async-done | bytes 2097168 | tf_op jit(solution)/shard_map/all_gather | solution.py:727
  294.9 10.3 %multiply_convert_fusion.1 = (bf16[768,2048]{1,0:T(8,128)(2,1)}, f32[768,2048]{1,0:T(8,128)}) fusion(f32[2048]{0:T(1024)S(1)} %copy-done.90, bf16[768,2176]{1,0:T(8,128)(2,1)S(1)} %constant_dynamic-update-slice_fusion.two_ref, bf16[2176,2048]{1,0:T(8,128)(2,1)S(1)} %assemble_gathered.4), kind=kOutput, calls=%fused_computation.8 | convolution fusion | flops 6854541312 | bytes 21700608 | tf_op jit(solution)/shard_map/dot_general | solution.py:28
  305.1 13.9 %collective-permute-done.20.refs_3_ = bf16[1536,512]{1,0:T(8,128)(2,1)S(1)} collective-permute-done((bf16[1536,512]{1,0:T(8,128)(2,1)S(1)}, bf16[1536,512]{1,0:T(8,128)(2,1)S(1)}, u32[]{:S(2)}, u32[]{:S(2)}) %collective-permute-start.20) | collective-permute-done | bytes 1572896 | tf_op jit(solution)/shard_map/ppermute | solution.py:673
  319.1 33.7 %collective-permute-done.21.refs_4_ = bf16[1536,512]{1,0:T(8,128)(2,1)S(1)} collective-permute-done((bf16[1536,512]{1,0:T(8,128)(2,1)S(1)}, bf16[1536,512]{1,0:T(8,128)(2,1)S(1)}, u32[]{:S(2)}, u32[]{:S(2)}) %collective-permute-start.21) | collective-permute-done | bytes 1572896 | tf_op jit(solution)/shard_map/ppermute | solution.py:673
  357.8 13.7 %multiply_convert_fusion.gp_ref = bf16[768,2048]{1,0:T(8,128)(2,1)S(1)} fusion(bf16[2048,2176]{1,0:T(8,128)(2,1)} %copy-done.9, bf16[768,128]{1,0:T(8,128)(2,1)S(1)} %fusion.36.gdd_ref, bf16[384,2048]{1,0:T(8,128)(2,1)} %get-tuple-element.103, bf16[384,2048]{1,0:T(8,128)(2,1)S(1)} %copy-done.59, f32[768,2048]{1,0:T(8,128)} %get-tuple-element.163, ...), kind=kOutput, calls=%fused_computation.7 | convolution fusion | flops 6875578368 | bytes 21700608 | tf_op jit(solution)/shard_map/dot_general | solution.py:32
  371.5 8.6 %convolution_convert_fusion.1 = bf16[384,2176]{1,0:T(8,128)(2,1)S(1)} fusion(bf16[2176,2048]{1,0:T(8,128)(2,1)} %copy-done.10, bf16[768,2048]{1,0:T(8,128)(2,1)S(1)} %multiply_convert_fusion.gp_ref), kind=kOutput, calls=%fused_computation.27 | convolution fusion | flops 3423387648 | bytes 12156928 | tf_op jit(solution)/shard_map/dot_general | solution.py:32
  385.3 10.9 %fusion.14.refs_0_ = bf16[384,2176]{1,0:T(8,128)(2,1)} fusion(bf16[2176,2048]{1,0:T(8,128)(2,1)} %copy-done.10, bf16[384,2176]{1,0:T(8,128)(2,1)} %collective-permute-done.22, bf16[768,2048]{1,0:T(8,128)(2,1)S(1)} %multiply_convert_fusion.gp_ref), kind=kOutput, calls=%fused_computation.23 | convolution fusion | flops 3425894400 | bytes 13828096 | tf_op jit(solution)/shard_map/dot_general | solution.py:32
  397.5 36.7 %collective-permute-done.25.refs_1_ = bf16[384,2176]{1,0:T(8,128)(2,1)S(1)} collective-permute-done((bf16[384,2176]{1,0:T(8,128)(2,1)}, bf16[384,2176]{1,0:T(8,128)(2,1)S(1)}, u32[]{:S(2)}, u32[]{:S(2)}) %collective-permute-start.25) | collective-permute-done | bytes 1671200 | tf_op jit(solution)/shard_map/ppermute | solution.py:673
  436.7 6.1 %back_middle.1 = (f32[384,2048]{1,0:T(8,128)S(1)}, bf16[384,2176]{1,0:T(8,128)(2,1)}) custom-call(s32[1]{0:T(128)} %bitcast.core_ref, s32[3]{0:T(128)S(1)} %copy-done.53, bf16[384,2176]{1,0:T(8,128)(2,1)S(1)} %copy-done.44, bf16[384,2176]{1,0:T(8,128)(2,1)S(1)} %collective-permute-done.25.refs_1_, f32[384,2048]{1,0:T(8,128)S(1)} %copy-done.5, ...), custom_call_target="tpu_custom_call" | custom-call | tf_op jit(solution)/shard_map/back_middle/pallas_call | solution.py:431
  444.1 6.5 %convolution_convert_fusion = bf16[384,2176]{1,0:T(8,128)(2,1)} fusion(bf16[2048,2176]{1,0:T(8,128)(2,1)S(1)} %bitcast.88, bf16[768,2048]{1,0:T(8,128)(2,1)} %get-tuple-element.69.hid_ref), kind=kOutput, calls=%fused_computation.26 | convolution fusion | flops 3423387648 | bytes 12156928 | tf_op jit(solution)/shard_map/dot_general | solution.py:28
  458.6 13.1 %attend_backward.1 = (bf16[768,512]{1,0:T(8,128)(2,1)}, bf16[768,512]{1,0:T(8,128)(2,1)}, bf16[768,512]{1,0:T(8,128)(2,1)}, bf16[768,512]{1,0:T(8,128)(2,1)}, bf16[768,512]{1,0:T(8,128)(2,1)}) custom-call(bf16[768,1536]{1,0:T(8,128)(2,1)} %add_convert_fusion.q_ref.k_ref.v_ref, bf16[768,1536]{1,0:T(8,128)(2,1)} %add_convert_fusion.q_ref.k_ref.v_ref, ...), custom_call_target="tpu_custom_call" | custom-call | tf_op jit(solution)/shard_map/attend_backward/pallas_call | solution.py:174
  474.6 9.6 %fusion.15.refs_0_ = bf16[384,2176]{1,0:T(8,128)(2,1)} fusion(bf16[2048,2176]{1,0:T(8,128)(2,1)} %copy-done.9, bf16[384,2176]{1,0:T(8,128)(2,1)} %collective-permute-done.23, bf16[768,2048]{1,0:T(8,128)(2,1)} %get-tuple-element.69.hid_ref), kind=kOutput, calls=%fused_computation.24 | convolution fusion | flops 3425894400 | bytes 13828096 | tf_op jit(solution)/shard_map/dot_general | solution.py:28
  485.4 24.5 %collective-permute-done.29 = bf16[768,512]{1,0:T(8,128)(2,1)S(1)} collective-permute-done((bf16[768,512]{1,0:T(8,128)(2,1)}, bf16[768,512]{1,0:T(8,128)(2,1)S(1)}, u32[]{:S(2)}, u32[]{:S(2)}) %collective-permute-start.29) | collective-permute-done | bytes 786464 | tf_op jit(solution)/shard_map/ppermute | solution.py:673
  558.7 7.0 %collective-permute-done.36 = bf16[576,128]{1,0:T(8,128)(2,1)S(1)} collective-permute-done((bf16[576,128]{1,0:T(8,128)(2,1)S(1)}, bf16[576,128]{1,0:T(8,128)(2,1)S(1)}, u32[]{:S(2)}, u32[]{:S(2)}) %collective-permute-start.36) | collective-permute-done | bytes 147488 | tf_op jit(solution)/shard_map/ppermute | solution.py:673
  569.6 11.7 %collective-permute-done.37.cross_ref = bf16[4,576,128]{2,1,0:T(8,128)(2,1)} collective-permute-done((bf16[4,576,128]{2,1,0:T(8,128)(2,1)}, bf16[4,576,128]{2,1,0:T(8,128)(2,1)}, u32[]{:S(2)}, u32[]{:S(2)}) %collective-permute-start.37) | collective-permute-done | bytes 589856 | tf_op jit(solution)/shard_map/ppermute | solution.py:673
  (413 shorter events, 232.5 us)
Async XLA Ops:
  7.2 108.1 %all-gather.6.cloned.1.call-start = ((), (), s32[]{:S(2)}) async-start(), calls=%async_computation | async-start | bytes 1310720 | tf_op jit(solution)/shard_map/all_gather | solution.py:727
  9.3 25.8 %collective-permute-start = (bf16[3,256,512]{2,1,0:T(8,128)(2,1)}, bf16[3,256,512]{2,1,0:T(8,128)(2,1)}, u32[]{:S(2)}, u32[]{:S(2)}) collective-permute-start(bf16[3,256,512]{2,1,0:T(8,128)(2,1)} %constant_dynamic-slice_fusion.31), channel_id=1, source_target_pairs={{0,8},{8,0},{16,24},{24,16},{1,9},{9,1},{17,25},{25,17},{2,10},{10... | collective-permute-start | bytes 2359304 | tf_op jit(solution)/shard_map/ppermute | solution.py:673
  9.3 25.8 %collective-permute-start.1 = (bf16[3,256,512]{2,1,0:T(8,128)(2,1)}, bf16[3,256,512]{2,1,0:T(8,128)(2,1)}, u32[]{:S(2)}, u32[]{:S(2)}) collective-permute-start(bf16[3,256,512]{2,1,0:T(8,128)(2,1)} %constant_dynamic-slice_fusion.31), channel_id=1, source_target_pairs={{8,16},{16,8},{9,17},{17,9},{10,18},{18,10},{11,19},{19,11},{12,20... | collective-permute-start | bytes 2359304 | tf_op jit(solution)/shard_map/ppermute | solution.py:673
  56.2 144.4 %all-gather.10.cloned.1.call-start = ((), (), s32[]{:S(2)}) async-start(), calls=%async_computation.2 | async-start | bytes 2621440 | tf_op jit(solution)/shard_map/all_gather | solution.py:727
  61.3 37.6 %collective-permute-start.6 = (bf16[3,256,512]{2,1,0:T(8,128)(2,1)}, bf16[3,256,512]{2,1,0:T(8,128)(2,1)}, u32[]{:S(2)}, u32[]{:S(2)}) collective-permute-start(bf16[3,256,512]{2,1,0:T(8,128)(2,1)} %collective-permute-done.5.refs_3_), channel_id=1, source_target_pairs={{8,0},{16,24},{9,1},{17,25},{10,2},{18,26},{11,3},{19,27},{12,4},{... | collective-permute-start | bytes 2359304 | tf_op jit(solution)/shard_map/ppermute | solution.py:673
  65.7 33.2 %collective-permute-start.7 = (bf16[3,256,512]{2,1,0:T(8,128)(2,1)}, bf16[3,256,512]{2,1,0:T(8,128)(2,1)}, u32[]{:S(2)}, u32[]{:S(2)}) collective-permute-start(bf16[3,256,512]{2,1,0:T(8,128)(2,1)} %collective-permute-done.4.refs_5_), channel_id=1, source_target_pairs={{0,4},{4,0},{24,28},{28,24},{1,5},{5,1},{25,29},{29,25},{2,6},{6,2... | collective-permute-start | bytes 2359304 | tf_op jit(solution)/shard_map/ppermute | solution.py:673
  98.9 101.6 %all-gather.8.cloned.1.call-start = ((), (), s32[]{:S(2)}) async-start(), calls=%async_computation.1 | async-start | bytes 2621440 | tf_op jit(solution)/shard_map/all_gather | solution.py:727
  99.7 151.4 %all-gather.12.cloned.1.call-start = ((), (), s32[]{:S(2)}) async-start(), calls=%async_computation.3 | async-start | bytes 2621440 | tf_op jit(solution)/shard_map/all_gather | solution.py:727
  107.9 35.4 %collective-permute-start.10 = (bf16[3,256,512]{2,1,0:T(8,128)(2,1)}, bf16[3,256,512]{2,1,0:T(8,128)(2,1)}, u32[]{:S(2)}, u32[]{:S(2)}) collective-permute-start(bf16[3,256,512]{2,1,0:T(8,128)(2,1)} %collective-permute-done.5.refs_3_), channel_id=1, source_target_pairs={{8,12},{12,8},{16,20},{20,16},{9,13},{13,9},{17,21},{21,17},{10,14... | collective-permute-start | bytes 2359304 | tf_op jit(solution)/shard_map/ppermute | solution.py:673
  111.3 32.0 %collective-permute-start.12 = (bf16[3,256,512]{2,1,0:T(8,128)(2,1)}, bf16[3,256,512]{2,1,0:T(8,128)(2,1)}, u32[]{:S(2)}, u32[]{:S(2)}) collective-permute-start(bf16[3,256,512]{2,1,0:T(8,128)(2,1)} %collective-permute-done.6.refs_9_), channel_id=1, source_target_pairs={{0,4},{4,0},{24,28},{28,24},{1,5},{5,1},{25,29},{29,25},{2,6},{6,2... | collective-permute-start | bytes 2359304 | tf_op jit(solution)/shard_map/ppermute | solution.py:673
  113.6 39.8 %collective-permute-start.13 = (bf16[192,2048]{1,0:T(8,128)(2,1)}, bf16[192,2048]{1,0:T(8,128)(2,1)}, u32[]{:S(2)}, u32[]{:S(2)}) collective-permute-start(bf16[192,2048]{1,0:T(8,128)(2,1)} %collective-permute-done.8.refs_1_), channel_id=1, source_target_pairs={{0,1},{1,0},{2,3},{3,2},{4,5},{5,4},{6,7},{7,6},{8,9},{9,8},{10,11... | collective-permute-start | bytes 2359304 | tf_op jit(solution)/shard_map/ppermute | solution.py:673
  115.0 166.8 %all-gather.14.cloned.1.call-start = ((), (), s32[]{:S(2)}) async-start(), calls=%async_computation.4 | async-start | bytes 2621440 | tf_op jit(solution)/shard_map/all_gather | solution.py:727
  116.8 62.1 %collective-permute-start.14 = (bf16[768,512]{1,0:T(8,128)(2,1)S(1)}, bf16[768,512]{1,0:T(8,128)(2,1)S(1)}, u32[]{:S(2)}, u32[]{:S(2)}) collective-permute-start(bf16[768,512]{1,0:T(8,128)(2,1)S(1)} %pad_maximum_fusion.9), channel_id=1, source_target_pairs={{0,4},{4,0},{1,5},{5,1},{2,6},{6,2},{3,7},{7,3},{8,12},{12,8},{9,1... | collective-permute-start | bytes 2359304 | tf_op jit(solution)/shard_map/ppermute | solution.py:673
  197.6 38.4 %collective-permute-start.16 = (bf16[384,2176]{1,0:T(8,128)(2,1)}, bf16[384,2176]{1,0:T(8,128)(2,1)}, u32[]{:S(2)}, u32[]{:S(2)}) collective-permute-start(bf16[384,2176]{1,0:T(8,128)(2,1)} %fusion.16.refs_0_), channel_id=1, source_target_pairs={{0,2},{2,0},{1,3},{3,1},{4,6},{6,4},{5,7},{7,5},{8,10},{10,8},{9,1... | collective-permute-start | bytes 5013512 | tf_op jit(solution)/shard_map/ppermute | solution.py:673
  204.1 81.7 %collective-permute-start.19 = (bf16[384,2048]{1,0:T(8,128)(2,1)}, bf16[384,2048]{1,0:T(8,128)(2,1)}, u32[]{:S(2)}, u32[]{:S(2)}) collective-permute-start(bf16[384,2048]{1,0:T(8,128)(2,1)} %pad_maximum_fusion.6), channel_id=1, source_target_pairs={{0,4},{4,0},{1,5},{5,1},{2,6},{6,2},{3,7},{7,3},{8,12},{12,8},{9,1... | collective-permute-start | bytes 4718600 | tf_op jit(solution)/shard_map/ppermute | solution.py:673
  205.5 80.3 %collective-permute-start.18 = (bf16[384,2048]{1,0:T(8,128)(2,1)}, bf16[384,2048]{1,0:T(8,128)(2,1)}, u32[]{:S(2)}, u32[]{:S(2)}) collective-permute-start(bf16[384,2048]{1,0:T(8,128)(2,1)} %pad_maximum_fusion.5), channel_id=1, source_target_pairs={{0,4},{4,0},{1,5},{5,1},{2,6},{6,2},{3,7},{7,3},{8,12},{12,8},{9,1... | collective-permute-start | bytes 4718600 | tf_op jit(solution)/shard_map/ppermute | solution.py:673
  243.8 48.6 %collective-permute-start.17 = (bf16[384,2176]{1,0:T(8,128)(2,1)}, bf16[384,2176]{1,0:T(8,128)(2,1)}, u32[]{:S(2)}, u32[]{:S(2)}) collective-permute-start(bf16[384,2176]{1,0:T(8,128)(2,1)} %get-tuple-element.63), channel_id=1, source_target_pairs={{0,1},{1,0},{2,3},{3,2},{4,5},{5,4},{6,7},{7,6},{8,9},{9,8},{10,11... | collective-permute-start | bytes 5013512 | tf_op jit(solution)/shard_map/ppermute | solution.py:673
  284.1 35.0 %collective-permute-start.20 = (bf16[1536,512]{1,0:T(8,128)(2,1)S(1)}, bf16[1536,512]{1,0:T(8,128)(2,1)S(1)}, u32[]{:S(2)}, u32[]{:S(2)}) collective-permute-start(bf16[1536,512]{1,0:T(8,128)(2,1)S(1)} %pad_maximum_fusion.7), channel_id=1, source_target_pairs={{0,4},{4,0},{1,5},{5,1},{2,6},{6,2},{3,7},{7,3},{8,12},{12,8},{9,1... | collective-permute-start | bytes 4718600 | tf_op jit(solution)/shard_map/ppermute | solution.py:673
  285.4 67.4 %collective-permute-start.21 = (bf16[1536,512]{1,0:T(8,128)(2,1)S(1)}, bf16[1536,512]{1,0:T(8,128)(2,1)S(1)}, u32[]{:S(2)}, u32[]{:S(2)}) collective-permute-start(bf16[1536,512]{1,0:T(8,128)(2,1)S(1)} %pad_maximum_fusion.8), channel_id=1, source_target_pairs={{0,4},{4,0},{1,5},{5,1},{2,6},{6,2},{3,7},{7,3},{8,12},{12,8},{9,1... | collective-permute-start | bytes 4718600 | tf_op jit(solution)/shard_map/ppermute | solution.py:673
  396.3 37.9 %collective-permute-start.25 = (bf16[384,2176]{1,0:T(8,128)(2,1)}, bf16[384,2176]{1,0:T(8,128)(2,1)S(1)}, u32[]{:S(2)}, u32[]{:S(2)}) collective-permute-start(bf16[384,2176]{1,0:T(8,128)(2,1)} %fusion.14.refs_0_), channel_id=1, source_target_pairs={{0,2},{2,0},{1,3},{3,1},{4,6},{6,4},{5,7},{7,5},{8,10},{10,8},{9,1... | collective-permute-start | bytes 5013512 | tf_op jit(solution)/shard_map/ppermute | solution.py:673
  471.7 38.5 %collective-permute-start.27 = (bf16[768,512]{1,0:T(8,128)(2,1)}, bf16[768,512]{1,0:T(8,128)(2,1)S(1)}, u32[]{:S(2)}, u32[]{:S(2)}) collective-permute-start(bf16[768,512]{1,0:T(8,128)(2,1)} %get-tuple-element.74), channel_id=1, source_target_pairs={{4,0},{5,1},{6,2},{7,3},{12,8},{13,9},{14,10},{15,11},{20,16},{21,... | collective-permute-start | bytes 2359304 | tf_op jit(solution)/shard_map/ppermute | solution.py:673
  473.0 36.9 %collective-permute-start.29 = (bf16[768,512]{1,0:T(8,128)(2,1)}, bf16[768,512]{1,0:T(8,128)(2,1)S(1)}, u32[]{:S(2)}, u32[]{:S(2)}) collective-permute-start(bf16[768,512]{1,0:T(8,128)(2,1)} %get-tuple-element.78), channel_id=1, source_target_pairs={{4,0},{5,1},{6,2},{7,3},{12,8},{13,9},{14,10},{15,11},{20,16},{21,... | collective-permute-start | bytes 2359304 | tf_op jit(solution)/shard_map/ppermute | solution.py:673
  484.2 38.5 %collective-permute-start.24 = (bf16[384,2176]{1,0:T(8,128)(2,1)}, bf16[384,2176]{1,0:T(8,128)(2,1)}, u32[]{:S(2)}, u32[]{:S(2)}) collective-permute-start(bf16[384,2176]{1,0:T(8,128)(2,1)} %fusion.15.refs_0_), channel_id=1, source_target_pairs={{0,2},{2,0},{1,3},{3,1},{4,6},{6,4},{5,7},{7,5},{8,10},{10,8},{9,1... | collective-permute-start | bytes 5013512 | tf_op jit(solution)/shard_map/ppermute | solution.py:673
  540.5 43.7 %collective-permute-start.31 = (bf16[384,2048]{1,0:T(8,128)(2,1)}, bf16[384,2048]{1,0:T(8,128)(2,1)}, u32[]{:S(2)}, u32[]{:S(2)}) collective-permute-start(bf16[384,2048]{1,0:T(8,128)(2,1)} %reduce-precision_convert_fusion.refs_0_), channel_id=1, source_target_pairs={{0,2},{2,0},{1,3},{3,1},{4,6},{6,4},{5,7},{7,5},{8,10},{10,8},{9,1... | collective-permute-start | bytes 4718600 | tf_op jit(solution)/shard_map/ppermute | solution.py:673
  (120 other events, 2007.4 us)
Sparse Core Ops, SparseCore 0:
  56.3 37.1 all-gather.5
  99.1 44.2 all-gather.9
  144.9 44.6 all-gather.7
  191.0 44.6 all-gather.11
  237.1 44.6 all-gather.13

commit v3 on v2

--- a/solution.py
+++ b/solution.py
@@ -13,6 +13,7 @@
 BLOCK = 256
 AUG = 128
 ROW_CHUNK = 128
+HINT = pl.CostEstimate(flops=1, transcendentals=0, bytes_accessed=1)
 
 layer_eps = 1e-05
 factor = 0.5
@@ -21,6 +22,7 @@
 f32 = jnp.float32
 
 CORE_SWAP = [(0, 1), (1, 0), (2, 3), (3, 2)]
+SWAP_Y = [(0, 1), (1, 0)]
 X_SWAP = [(0, 2), (2, 0), (1, 3), (3, 1)]
 
 
@@ -69,12 +71,12 @@
     return reach, slot
 
 
-def attend_forward(qkv, far, far_bias, own_bias, heads, scale):
+def attend_forward(qkv, far, far_base, far_bias, own_bias, heads, scale):
     tokens = qkv.shape[0]
     far_rows = far.shape[0]
     blocks = tokens // BLOCK
 
-    def kernel(q_ref, k_ref, v_ref, fk_ref, fv_ref, fb_ref, ob_ref, o_ref, pf_ref, po_ref):
+    def kernel(q_ref, k_ref, v_ref, fk_ref, fv_ref, fb_ref, ob_ref, o_ref, low_ref, pf_ref, po_ref):
         far_k = fk_ref[...]
         far_v = fv_ref[...]
         for b in range(blocks):
@@ -97,7 +99,9 @@
             p_own = (p_own * inverse).astype(bf16)
             pf_ref[0, rows, :] = p_far
             po_ref[0, rows, :width] = p_own
-            o_ref[rows, :] = dot_nn(p_far, far_v) + dot_nn(p_own, v_ref[:width, :])
+            mixed = dot_nn(p_far, far_v) + dot_nn(p_own, v_ref[:width, :])
+            o_ref[rows, :] = mixed
+            low_ref[rows, :] = mixed.astype(bf16)
 
     return pl.pallas_call(
         kernel,
@@ -106,27 +110,30 @@
             pl.BlockSpec((tokens, HD), lambda h: (0, h)),
             pl.BlockSpec((tokens, HD), lambda h: (0, heads + h)),
             pl.BlockSpec((tokens, HD), lambda h: (0, 2 * heads + h)),
-            pl.BlockSpec((far_rows, HD), lambda h: (0, h)),
-            pl.BlockSpec((far_rows, HD), lambda h: (0, heads + h)),
+            pl.BlockSpec((far_rows, HD), lambda h: (0, far_base + h)),
+            pl.BlockSpec((far_rows, HD), lambda h: (0, far_base + heads + h)),
             pl.BlockSpec((blocks, far_rows), lambda h: (0, 0)),
             pl.BlockSpec((blocks, tokens), lambda h: (0, 0)),
         ],
         out_specs=[
+            pl.BlockSpec((tokens, HD), lambda h: (0, h)),
             pl.BlockSpec((tokens, HD), lambda h: (0, h)),
             pl.BlockSpec((1, tokens, far_rows), lambda h: (h, 0, 0)),
             pl.BlockSpec((1, tokens, tokens), lambda h: (h, 0, 0)),
         ],
         out_shape=[
             jax.ShapeDtypeStruct((tokens, heads * HD), f32),
+            jax.ShapeDtypeStruct((tokens, heads * HD), bf16),
             jax.ShapeDtypeStruct((heads, tokens, far_rows), bf16),
             jax.ShapeDtypeStruct((heads, tokens, tokens), bf16),
         ],
         compiler_params=pltpu.CompilerParams(vmem_limit_bytes=56 << 20),
+        cost_estimate=HINT,
         name="attend_forward",
     )(qkv, qkv, qkv, far, far, far_bias, own_bias)
 
 
-def attend_backward(qkv, far, grad_attended, attended, probs_far, probs_own, heads, scale):
+def attend_backward(qkv, far, far_base, grad_attended, attended, probs_far, probs_own, heads, scale):
     tokens = qkv.shape[0]
     far_rows = far.shape[0]
     blocks = tokens // BLOCK
@@ -178,8 +185,8 @@
             head_spec,
             pl.BlockSpec((tokens, HD), lambda h: (0, heads + h)),
             pl.BlockSpec((tokens, HD), lambda h: (0, 2 * heads + h)),
-            far_spec,
-            pl.BlockSpec((far_rows, HD), lambda h: (0, heads + h)),
+            pl.BlockSpec((far_rows, HD), lambda h: (0, far_base + h)),
+            pl.BlockSpec((far_rows, HD), lambda h: (0, far_base + heads + h)),
             head_spec,
             head_spec,
             pl.BlockSpec((1, tokens, far_rows), lambda h: (h, 0, 0)),
@@ -194,6 +201,7 @@
             pltpu.VMEM((far_rows, HD), f32),
         ],
         compiler_params=pltpu.CompilerParams(vmem_limit_bytes=56 << 20),
+        cost_estimate=HINT,
         name="attend_backward",
     )(qkv, qkv, qkv, far, far, grad_attended, attended, probs_far, probs_own)
 
@@ -205,9 +213,7 @@
     tail_rows, tail_columns = tail.shape
 
     def kernel(spot_ref, *refs):
-        own, one, y_one = refs[:3]
-        in_two, y_in_two, out_two, y_out_two, in_far, y_in_far, out_far, y_out_far = refs[3:11]
-        tail_ref, out, sem = refs[11:]
+        own, one, y_one, two, y_two, three, y_three, tail_ref, out, sem = refs
         group = spot_ref[0]
         context = spot_ref[1]
         inner = (group == 1) | (group == 2)
@@ -230,6 +236,12 @@
         fixed = moves(own, group, 0, 0)
         fixed += moves(one, group ^ 1, context, count)
         fixed += moves(y_one, group ^ 1, 1 - context, 2 * count)
+        second = jnp.where(inner, group ^ 3, group ^ 2)
+        third = jnp.where(inner, group ^ 2, group ^ 3)
+        fixed += moves(two, second, context, 3 * count)
+        fixed += moves(y_two, second, 1 - context, 4 * count)
+        fixed += moves(three, third, context, 5 * count)
+        fixed += moves(y_three, third, 1 - context, 6 * count)
         row0 = rows - tail_rows if direction == "rows" else 0
         col0 = 0 if direction == "rows" else columns - tail_columns
         fixed.append(
@@ -239,30 +251,8 @@
                 sem.at[7 * count],
             )
         )
-        inside = moves(in_two, group ^ 2, context, 3 * count)
-        inside += moves(y_in_two, group ^ 2, 1 - context, 4 * count)
-        inside += moves(in_far, group ^ 3, context, 5 * count)
-        inside += moves(y_in_far, group ^ 3, 1 - context, 6 * count)
-        outside = moves(out_two, group ^ 2, context, 3 * count)
-        outside += moves(y_out_two, group ^ 2, 1 - context, 4 * count)
-        outside += moves(out_far, group ^ 3, context, 5 * count)
-        outside += moves(y_out_far, group ^ 3, 1 - context, 6 * count)
         for move in fixed:
             move.start()
-
-        @pl.when(inner)
-        def _():
-            for move in inside:
-                move.start()
-            for move in inside:
-                move.wait()
-
-        @pl.when(jnp.logical_not(inner))
-        def _():
-            for move in outside:
-                move.start()
-            for move in outside:
-                move.wait()
 
         for move in fixed:
             move.wait()
@@ -272,88 +262,15 @@
         grid_spec=pltpu.PrefetchScalarGridSpec(
             num_scalar_prefetch=1,
             grid=(),
-            in_specs=[pl.BlockSpec(memory_space=pl.ANY)] * 12,
+            in_specs=[pl.BlockSpec(memory_space=pl.ANY)] * 8,
             out_specs=pl.BlockSpec(memory_space=pltpu.VMEM),
             scratch_shapes=[pltpu.SemaphoreType.DMA((7 * count + 1,))],
         ),
         out_shape=jax.ShapeDtypeStruct((rows, columns), bf16),
         compiler_params=pltpu.CompilerParams(vmem_limit_bytes=24 << 20),
+        cost_estimate=HINT,
         name="assemble",
     )(spot, *pieces, tail)
-
-
-def assemble_gathered(spot, own, gathered, swapped, tail, rows, columns, direction):
-    shard_rows, shard_columns = own.shape
-    shard = shard_rows if direction == "rows" else shard_columns
-    half = shard_rows // 2
-    chunks = len(gathered)
-    size = half // chunks
-    tail_rows, tail_columns = tail.shape
-    copies = 7 * chunks + 2
-
-    def kernel(spot_ref, *refs):
-        own_ref = refs[0]
-        near = refs[1 : 1 + chunks]
-        cross = refs[1 + chunks : 1 + 2 * chunks]
-        tail_ref, out, sem = refs[1 + 2 * chunks :]
-        group = spot_ref[0]
-        context = spot_ref[1]
-        moves = []
-
-        def move(src, source, which, chunk_row):
-            count, width = src.shape
-            row = which * half + chunk_row
-            if direction == "rows":
-                dst = out.at[
-                    pl.ds(pl.multiple_of(source * shard + row, size), count), pl.ds(0, width)
-                ]
-            else:
-                dst = out.at[
-                    pl.ds(pl.multiple_of(row, size), count),
-                    pl.ds(pl.multiple_of(source * shard, shard), width),
-                ]
-            moves.append(pltpu.make_async_copy(src, dst, sem.at[len(moves)]))
-
-        for j in range(chunks):
-            for g in range(4):
-                move(near[j].at[pl.ds(g * size, size)], g, context, j * size)
-            for i in range(3):
-                move(
-                    cross[j].at[pl.ds(i * size, size)], group ^ (i + 1), 1 - context, j * size
-                )
-        move(
-            own_ref.at[pl.ds(pl.multiple_of((1 - context) * half, half), half)],
-            group,
-            1 - context,
-            0,
-        )
-        row0 = rows - tail_rows if direction == "rows" else 0
-        col0 = 0 if direction == "rows" else columns - tail_columns
-        moves.append(
-            pltpu.make_async_copy(
-                tail_ref,
-                out.at[pl.ds(row0, tail_rows), pl.ds(col0, tail_columns)],
-                sem.at[len(moves)],
-            )
-        )
-        for m in moves:
-            m.start()
-        for m in moves:
-            m.wait()
-
-    return pl.pallas_call(
-        kernel,
-        grid_spec=pltpu.PrefetchScalarGridSpec(
-            num_scalar_prefetch=1,
-            grid=(),
-            in_specs=[pl.BlockSpec(memory_space=pl.ANY)] * (2 + 2 * chunks),
-            out_specs=pl.BlockSpec(memory_space=pltpu.VMEM),
-            scratch_shapes=[pltpu.SemaphoreType.DMA((copies,))],
-        ),
-        out_shape=jax.ShapeDtypeStruct((rows, columns), bf16),
-        compiler_params=pltpu.CompilerParams(vmem_limit_bytes=24 << 20),
-        name="assemble_gathered",
-    )(spot, own, *gathered, *swapped, tail)
 
 
 def norm_wide(pieces, places, slots, down_rows, gain, shift, tokens):
@@ -392,6 +309,7 @@
         ),
         out_shape=jax.ShapeDtypeStruct((tokens, width + AUG), bf16),
         compiler_params=pltpu.CompilerParams(vmem_limit_bytes=32 << 20),
+        cost_estimate=HINT,
         name="norm_wide",
     )(places, slots, *pieces, down_rows, gain, shift)
 
@@ -438,6 +356,7 @@
         ),
         out_shape=[jax.ShapeDtypeStruct((rows, c), d) for c, d in outs],
         compiler_params=pltpu.CompilerParams(vmem_limit_bytes=40 << 20),
+        cost_estimate=HINT,
         name=name,
     )(core, slots, *[a for a, _ in moving], *fixed)
 
@@ -480,27 +399,39 @@
     return ((grad_middle + norm_back(grad_normed * gain, unit, inverse)).astype(bf16),)
 
 
-def pack_terms(tensor, two, back, attended, grad_pre, hidden, grad_dd, dd, loss, local):
+def pack_terms(where, two, back, attended, grad_pre, hidden, grad_dd, dd, loss, local):
     width = loss.shape[1]
+    half = loss.shape[0] // 2
     cut = local // 4
 
-    def kernel(t_ref, two_ref, back_ref, att_ref, gp_ref, hid_ref, gdd_ref, dd_ref, loss_ref, out):
+    def kernel(
+        t_ref, two_a, two_b, back_a, back_b, att_ref, gp_ref, hid_ref, gdd_ref, dd_a, dd_b, loss_ref, out
+    ):
         lanes = pl.ds(pl.multiple_of(t_ref[0] * local, local), local)
-        two_tail = two_ref[:, width:]
-        back_tail = back_ref[:, width:]
+        mine = pl.ds(pl.multiple_of(t_ref[1] * half, half), half)
+        theirs = pl.ds(pl.multiple_of((1 - t_ref[1]) * half, half), half)
+        halves = ((two_a, back_a, dd_a, mine), (two_b, back_b, dd_b, theirs))
+
+        def both(make):
+            return make(*halves[0]) + make(*halves[1])
+
         terms = [
-            dot_tn(back_tail, att_ref[...])[PAIR : 2 * PAIR],
-            dot_tn(two_tail, back_ref[:, lanes])[PAIR : 2 * PAIR],
-            dot_tn(back_tail, two_ref[:, lanes])[:PAIR],
-            dot_tn(dd_ref[...], loss_ref[:, lanes])[:PAIR],
+            both(lambda t, b, d, r: dot_tn(b[:, width:], att_ref[r, :]))[PAIR : 2 * PAIR],
+            both(lambda t, b, d, r: dot_tn(t[:, width:], b[:, lanes]))[PAIR : 2 * PAIR],
+            both(lambda t, b, d, r: dot_tn(b[:, width:], t[:, lanes]))[:PAIR],
+            both(lambda t, b, d, r: dot_tn(d[...], loss_ref[r, lanes]))[:PAIR],
         ]
         for n, term in enumerate(terms):
             low = term.astype(bf16)
             for g in range(4):
                 out[g, n * PAIR : (n + 1) * PAIR, :] = low[:, g * cut : (g + 1) * cut]
         base = len(terms) * PAIR
-        for left, right in ((two_tail, gp_ref), (gdd_ref[...], hid_ref)):
-            low = dot_tn(left, right[...])[:PAIR].astype(bf16)
+        wide_terms = (
+            dot_tn(two_a[:, width:], gp_ref[:half, :]) + dot_tn(two_b[:, width:], gp_ref[half:, :]),
+            dot_tn(gdd_ref[...], hid_ref[...]),
+        )
+        for term in wide_terms:
+            low = term[:PAIR].astype(bf16)
             tiles = low.shape[1] // (4 * cut)
             for g in range(4):
                 for t in range(tiles):
@@ -513,12 +444,13 @@
     return pl.pallas_call(
         kernel,
         grid_spec=pltpu.PrefetchScalarGridSpec(
-            num_scalar_prefetch=1, grid=(), in_specs=[whole] * 8, out_specs=whole
+            num_scalar_prefetch=1, grid=(), in_specs=[whole] * 11, out_specs=whole
         ),
         out_shape=jax.ShapeDtypeStruct((4, (4 + 2 * tiles) * PAIR, cut), bf16),
         compiler_params=pltpu.CompilerParams(vmem_limit_bytes=40 << 20),
+        cost_estimate=HINT,
         name="pack_terms",
-    )(tensor, two, back, attended, grad_pre, hidden, grad_dd, dd, loss)
+    )(where, *two, *back, attended, grad_pre, hidden, grad_dd, *dd, loss)
 
 
 def pack_projections(tensor, grad_down, normed_wide, grad_qkv, local):
@@ -544,6 +476,7 @@
         ),
         out_shape=jax.ShapeDtypeStruct((4, 6 * PAIR, cut), bf16),
         compiler_params=pltpu.CompilerParams(vmem_limit_bytes=24 << 20),
+        cost_estimate=HINT,
         name="pack_projections",
     )(tensor, grad_down, normed_wide, grad_qkv)
 
@@ -595,6 +528,7 @@
         ),
         out_shape=[jax.ShapeDtypeStruct(shape, f32) for shape in shapes],
         compiler_params=pltpu.CompilerParams(vmem_limit_bytes=24 << 20),
+        cost_estimate=HINT,
         name="unpack_terms",
     )(context, owner, near, cross)
 
@@ -623,6 +557,215 @@
         broad(placed[4 + tiles : 4 + 2 * tiles]),
         narrow(placed[3]),
     )
+
+
+def project(own, far, weight, bias, local):
+    tokens, wide = own.shape
+    blocks = 3 + (2 if far is not None else 0)
+
+    def kernel(*refs):
+        bias_ref, w_ref, out_ref = refs[-3:]
+
+        def write(x_ref):
+            out_ref[...] = (dot_nn(x_ref[...], w_ref[...]) + bias_ref[...]).astype(bf16)
+
+        if far is None:
+            write(refs[0])
+        else:
+            pl.when(pl.program_id(0) < 3)(lambda: write(refs[0]))
+            pl.when(pl.program_id(0) >= 3)(lambda: write(refs[1]))
+
+    def column(n):
+        return jnp.where(n < 3, n, n - 2)
+
+    rows = [own] if far is None else [own, far]
+    return pl.pallas_call(
+        kernel,
+        grid=(blocks,),
+        in_specs=[pl.BlockSpec((tokens, wide), lambda n: (0, 0))] * len(rows)
+        + [
+            pl.BlockSpec((1, local), lambda n: (0, column(n))),
+            pl.BlockSpec((wide, local), lambda n: (0, column(n))),
+        ],
+        out_specs=pl.BlockSpec((tokens, local), lambda n: (0, n)),
+        out_shape=jax.ShapeDtypeStruct((tokens, blocks * local), bf16),
+        compiler_params=pltpu.CompilerParams(vmem_limit_bytes=40 << 20),
+        cost_estimate=HINT,
+        name="project",
+    )(*rows, bias, weight)
+
+
+def expand(own, other, weight, bias):
+    size, wide = own.shape
+    hidden = weight.shape[1]
+    cut = 512
+    part = 128
+
+    def kernel(own_ref, other_ref, w_ref, b_ref, h_ref, s_ref):
+        for i, x_ref in enumerate((own_ref, other_ref)):
+            for r in range(0, size, part):
+                pre = dot_nn(x_ref[r : r + part, :], w_ref[...]) + b_ref[...]
+                phi = 0.5 * (1.0 + lax.erf(pre * (2.0**-0.5)))
+                bell = jnp.exp(-0.5 * pre * pre) * (0.5 / jnp.pi) ** 0.5
+                to = slice(i * size + r, i * size + r + part)
+                h_ref[to, :] = (pre * phi).astype(bf16)
+                s_ref[to, :] = (phi + pre * bell).astype(bf16)
+
+    block = pl.BlockSpec((2 * size, cut), lambda n: (0, n))
+    shape = jax.ShapeDtypeStruct((2 * size, hidden), bf16)
+    return pl.pallas_call(
+        kernel,
+        grid=(hidden // cut,),
+        in_specs=[
+            pl.BlockSpec((size, wide), lambda n: (0, 0)),
+            pl.BlockSpec((size, wide), lambda n: (0, 0)),
+            pl.BlockSpec((wide, cut), lambda n: (0, n)),
+            pl.BlockSpec((1, cut), lambda n: (0, n)),
+        ],
+        out_specs=[block, block],
+        out_shape=[shape, shape],
+        compiler_params=pltpu.CompilerParams(vmem_limit_bytes=40 << 20),
+        cost_estimate=HINT,
+        name="expand",
+    )(own, other, weight, bias)
+
+
+def back_hidden(loss, weight, slope):
+    tokens, wide = loss.shape
+    hidden = weight.shape[0]
+    cut = 512
+
+    def kernel(x_ref, w_ref, s_ref, out_ref):
+        grad = dot_nt(x_ref[...], w_ref[...])
+        out_ref[...] = (grad * s_ref[...].astype(f32)).astype(bf16)
+
+    block = pl.BlockSpec((tokens, cut), lambda n: (0, n))
+    return pl.pallas_call(
+        kernel,
+        grid=(hidden // cut,),
+        in_specs=[
+            pl.BlockSpec((tokens, wide), lambda n: (0, 0)),
+            pl.BlockSpec((cut, wide), lambda n: (n, 0)),
+            block,
+        ],
+        out_specs=block,
+        out_shape=jax.ShapeDtypeStruct((tokens, hidden), bf16),
+        compiler_params=pltpu.CompilerParams(vmem_limit_bytes=40 << 20),
+        cost_estimate=HINT,
+        name="back_hidden",
+    )(loss, weight, slope)
+
+
+class Ring:
+    def __init__(self, own, half_axis, context, inner):
+        size = own.shape[half_axis] // 2
+        self.own = own
+        self.inner = inner
+        self.part = lax.dynamic_slice_in_dim(own, context * size, size, half_axis)
+
+    def first(self, *waits):
+        part = gate(self.part, *waits)
+        self.one = lax.ppermute(part, "fsdp", [(0, 1), (1, 0), (2, 3), (3, 2)])
+        self.across = lax.ppermute(part, "fsdp", [(1, 2), (2, 1)])
+
+    def second(self, *waits):
+        self.one, across, *_ = lax.optimization_barrier((self.one, self.across, *waits))
+        self.y_one = lax.ppermute(self.one, "ctx", SWAP_Y)
+        outward = lax.ppermute(across, "fsdp", [(1, 0), (2, 3)])
+        self.back = lax.ppermute(self.one, "fsdp", [(1, 2), (2, 1)])
+        self.two = jnp.where(self.inner, across, outward)
+
+    def third(self, *waits):
+        self.two, back, self.y_one, *_ = lax.optimization_barrier(
+            (self.two, self.back, self.y_one, *waits)
+        )
+        self.y_two = lax.ppermute(self.two, "ctx", SWAP_Y)
+        outward = lax.ppermute(back, "fsdp", [(1, 0), (2, 3)])
+        self.three = jnp.where(self.inner, back, outward)
+
+    def fourth(self, *waits):
+        self.three, self.y_two, *_ = lax.optimization_barrier((self.three, self.y_two, *waits))
+        self.y_three = lax.ppermute(self.three, "ctx", SWAP_Y)
+
+    def pieces(self):
+        return (
+            self.own,
+            self.one,
+            self.y_one,
+            self.two,
+            self.y_two,
+            self.three,
+            self.y_three,
+        )
+
+
+def matmul(rows, half, weight, cut, dtype, flipped, count=None):
+    summed = rows.shape[1]
+    steps = summed // cut
+    wide = count or (weight.shape[0] if flipped else weight.shape[1])
+    size = rows.shape[0] // 2 if half is not None else rows.shape[0]
+
+    def kernel(half_ref, x_ref, w_ref, out_ref, *acc):
+        part = dot_nt(x_ref[...], w_ref[...]) if flipped else dot_nn(x_ref[...], w_ref[...])
+        if steps == 1:
+            out_ref[...] = part.astype(dtype)
+            return
+        step = pl.program_id(0)
+
+        @pl.when(step == 0)
+        def _():
+            acc[0][...] = part
+
+        @pl.when((step > 0) & (step < steps - 1))
+        def _():
+            acc[0][...] += part
+
+        @pl.when(step == steps - 1)
+        def _():
+            out_ref[...] = (acc[0][...] + part).astype(dtype)
+
+    if flipped:
+        w_spec = pl.BlockSpec((wide, cut), lambda k, h: (0, k))
+    else:
+        w_spec = pl.BlockSpec((cut, wide), lambda k, h: (k, 0))
+    return pl.pallas_call(
+        kernel,
+        grid_spec=pltpu.PrefetchScalarGridSpec(
+            num_scalar_prefetch=1,
+            grid=(steps,),
+            in_specs=[pl.BlockSpec((size, cut), lambda k, h: (h[0], k)), w_spec],
+            out_specs=pl.BlockSpec((size, wide), lambda k, h: (0, 0)),
+            scratch_shapes=[pltpu.VMEM((size, wide), f32)] if steps > 1 else [],
+        ),
+        out_shape=jax.ShapeDtypeStruct((size, wide), dtype),
+        compiler_params=pltpu.CompilerParams(vmem_limit_bytes=48 << 20),
+        cost_estimate=HINT,
+        name="matmul",
+    )(jnp.zeros((1,), jnp.int32) if half is None else half, rows, weight)
+
+
+def back_attend(core, own, other, weight):
+    size = own.shape[0]
+    local = weight.shape[0]
+
+    def kernel(core_ref, own_ref, other_ref, w_ref, out_ref):
+        w = w_ref[...]
+        mine = pl.multiple_of(core_ref[0] * size, size)
+        theirs = pl.multiple_of((1 - core_ref[0]) * size, size)
+        out_ref[pl.ds(mine, size), :] = dot_nt(own_ref[...], w).astype(bf16)
+        out_ref[pl.ds(theirs, size), :] = dot_nt(other_ref[...], w).astype(bf16)
+
+    whole = pl.BlockSpec(memory_space=pltpu.VMEM)
+    return pl.pallas_call(
+        kernel,
+        grid_spec=pltpu.PrefetchScalarGridSpec(
+            num_scalar_prefetch=1, grid=(), in_specs=[whole] * 3, out_specs=whole
+        ),
+        out_shape=jax.ShapeDtypeStruct((2 * size, local), bf16),
+        compiler_params=pltpu.CompilerParams(vmem_limit_bytes=32 << 20),
+        cost_estimate=HINT,
+        name="back_attend",
+    )(core, own, other, weight)
 
 
 def gate(value, *waits):
@@ -692,54 +835,9 @@
         swap_y = [(0, 1), (1, 0)]
         spot = jnp.stack([group, context]).astype(jnp.int32)
 
-        def spread_weight(own, half_axis, first_waits, last_waits):
-            size = own.shape[half_axis] // 2
-            both = ("fsdp", "ctx")
-            inner_y = [(2, 3), (3, 2), (4, 5), (5, 4)]
-            outer_y = [(0, 1), (1, 0), (6, 7), (7, 6)]
-            outward = [(1, 0), (2, 3)]
-            part = lax.dynamic_slice_in_dim(own, context * size, size, half_axis)
-            one = on(part, "fsdp", [(0, 1), (1, 0), (2, 3), (3, 2)])
-            in_far = on(part, "fsdp", [(1, 2), (2, 1)])
-            one, in_far, *first = lax.optimization_barrier((one, in_far, *first_waits))
-            y_one = on(one, "ctx", swap_y)
-            y_in_far = on(in_far, both, inner_y)
-            out_two = on(in_far, "fsdp", outward)
-            in_two = on(one, "fsdp", [(1, 2), (2, 1)])
-            y_one, out_two, in_two = lax.optimization_barrier((y_one, out_two, in_two))
-            out_far = on(in_two, "fsdp", outward)
-            y_out_two = on(out_two, both, outer_y)
-            y_in_two = on(in_two, both, inner_y)
-            out_far, y_out_two, *last = lax.optimization_barrier((out_far, y_out_two, *last_waits(*first)))
-            y_out_far = on(out_far, both, outer_y)
-            pieces = (own, one, y_one, in_two, y_in_two, out_two, y_out_two)
-            pieces += (in_far, y_in_far, out_far, y_out_far)
-            return pieces, last, (in_two, out_two), (out_far,)
-
-        def gather_weight(own, chunks, waits, swap_waits=()):
-            half_rows = own.shape[0] // 2
-            size = half_rows // chunks
-            gathered = []
-            swapped = []
-            for j in range(chunks):
-                part = lax.dynamic_slice_in_dim(own, context * half_rows + j * size, size, 0)
-                part = gate(part, *waits)
-                every = lax.all_gather(part, "fsdp", axis=0, tiled=True)
-                gathered.append(every)
-                every = gate(every, *swap_waits)
-                others = jnp.concatenate(
-                    [
-                        lax.dynamic_slice_in_dim(every, (group ^ i) * size, size, 0)
-                        for i in range(1, 4)
-                    ],
-                    axis=0,
-                )
-                swapped.append(on(others, "ctx", swap_y))
-            return gathered, swapped
-
-        def send_tp(other_low, own_full):
+        def send_tp(other_low, own_low):
             got = on(other_low, "tp", CORE_SWAP)
-            mine = round_low(own_full + got.astype(f32))
+            mine = round_low(own_low.astype(f32) + got.astype(f32))
             return mine, on(mine, "tp", X_SWAP)
 
         def sum_sent(sent, waits=()):
@@ -822,45 +920,26 @@
             sent = lax.dynamic_slice_in_dim(inputs, tensor * quarter, quarter, 0)
             far_quarter = on(sent, "ctx", [(0, 1)])
 
-            def last_waits(quarter_rows):
-                return (
-                    quarter_rows,
-                    on(quarter_rows, "tp", X_SWAP),
-                    on(quarter_rows, "tp", CORE_SWAP),
-                    normed_wide,
-                )
-
             far_places = jnp.stack([tensor, tensor ^ 2, tensor ^ 1, tensor ^ 3]).astype(jnp.int32)
-            q_pieces, last, q_second, q_third = spread_weight(
-                w_qkv, 1, (far_quarter,), last_waits
-            )
-            far_quarter, far_x, far_core, normed_wide = last
+            inner = (group == 1) | (group == 2)
+            q_ring = Ring(w_qkv, 1, context, inner)
+            o_ring = Ring(w_o, 0, context, inner)
+            in_ring = Ring(w_in, 0, context, inner)
+            out_ring = Ring(w_out, 0, context, inner)
+            q_ring.first()
+            q_ring.second()
+            q_ring.third(far_quarter)
+            far_quarter, _ = lax.optimization_barrier((far_quarter, q_ring.two))
+            far_x = on(far_quarter, "tp", X_SWAP)
+            far_core = on(far_quarter, "tp", CORE_SWAP)
+            o_ring.first(q_ring.two)
+            far_x, far_core, normed_wide, _ = lax.optimization_barrier(
+                (far_x, far_core, normed_wide, q_ring.three)
+            )
+            q_ring.fourth(normed_wide, o_ring.one, o_ring.across)
             far_both = on(far_x, "tp", CORE_SWAP)
-            q_through = (q_pieces[5], q_pieces[7])
-            o_near, o_cross = gather_weight(w_o, 1, q_second)
-            in_near, in_cross = gather_weight(w_in, 2, q_third)
-            q_full = assemble(
-                spot, q_pieces, q_aug, wide, 3 * local, ("rows", shard, shard // 2), 3
-            )
-            o_full = assemble_gathered(spot, w_o, o_near, o_cross, o_aug, local, wide, "columns")
-            in_full = assemble_gathered(
-                spot, w_in, in_near, in_cross, in_aug, wide, hidden_local, "rows"
-            )
-            out_near, out_cross = gather_weight(w_out, 2, q_third)
-        else:
-            own_q = jnp.transpose(w_qkv, (1, 0, 2)).reshape(shard, 3 * local)
-            q_full = jnp.concatenate([lax.all_gather(own_q, "fsdp", axis=0, tiled=True), q_aug], 0)
-            o_full = jnp.concatenate([lax.all_gather(w_o, "fsdp", axis=1, tiled=True), o_aug], 1)
-            in_full = jnp.concatenate([lax.all_gather(w_in, "fsdp", axis=0, tiled=True), in_aug], 0)
-            out_full = jnp.concatenate(
-                [lax.all_gather(w_out, "fsdp", axis=1, tiled=True), out_aug], 1
-            )
-
-        normed, reduced_qkv = normed_wide[:, :width], normed_wide[:, width:]
-        zero_bias = jnp.zeros((local,), f32)
-        q_bias = jnp.concatenate([bias_qv[0], zero_bias, bias_qv[1]])[None, :]
-        qkv = (dot_nn(normed_wide, q_full) + q_bias).astype(bf16)
-        if pair_ctx:
+            o_ring.second(q_ring.three)
+            in_ring.first(o_ring.two, o_ring.back)
             far_wide = norm_wide(
                 [far_quarter, far_x, far_core, far_both],
                 far_places,
@@ -870,50 +949,103 @@
                 shift_one,
                 tokens,
             )
-            far_kv = (dot_nn(far_wide, q_full[:, local:]) + q_bias[:, local:]).astype(bf16)
+            o_ring.third(far_wide, q_ring.y_three)
+            q_full = assemble(
+                gate(spot, o_ring.two, far_wide),
+                q_ring.pieces(),
+                q_aug,
+                wide,
+                3 * local,
+                ("rows", shard, shard // 2),
+                3,
+            )
         else:
+            own_q = jnp.transpose(w_qkv, (1, 0, 2)).reshape(shard, 3 * local)
+            q_full = jnp.concatenate([lax.all_gather(own_q, "fsdp", axis=0, tiled=True), q_aug], 0)
+            o_full = jnp.concatenate([lax.all_gather(w_o, "fsdp", axis=1, tiled=True), o_aug], 1)
+            in_full = jnp.concatenate([lax.all_gather(w_in, "fsdp", axis=0, tiled=True), in_aug], 0)
+            out_full = jnp.concatenate(
+                [lax.all_gather(w_out, "fsdp", axis=1, tiled=True), out_aug], 1
+            )
+
+        normed, reduced_qkv = normed_wide[:, :width], normed_wide[:, width:]
+        zero_bias = jnp.zeros((local,), f32)
+        q_bias = jnp.concatenate([bias_qv[0], zero_bias, bias_qv[1]])[None, :]
+        if pair_ctx:
+            qkv = project(normed_wide, far_wide, q_full, q_bias, local)
+            far_kv = qkv
+            far_base = 3 * heads
+            qkv, _, _, _ = lax.optimization_barrier(
+                (qkv, in_ring.one, in_ring.across, o_ring.three)
+            )
+            in_ring.second(qkv)
+            o_ring.fourth(qkv)
+            far_kv = qkv
+        else:
+            qkv = project(normed_wide, None, q_full, q_bias, local)
             far_kv = lax.all_gather(qkv[:, local:], "ctx", axis=0, tiled=True)
-
-        attended_f, probs_far, probs_own = attend_forward(
-            qkv, far_kv, far_bias, own_bias, heads, scale
-        )
-        attended = attended_f.astype(bf16)
-        attended_own = own_rows(attended)
-        attended_other = other_rows(attended)
+            far_base = 0
+
+        attended_f, attended, probs_far, probs_own = attend_forward(
+            qkv, far_kv, far_base, far_bias, own_bias, heads, scale
+        )
+        if pair_ctx:
+            o_full = assemble(
+                gate(spot, attended, in_ring.two, in_ring.back),
+                o_ring.pieces(),
+                o_aug,
+                local,
+                wide,
+                ("columns", shard, local // 2),
+                0,
+            )
+        core_id = core.astype(jnp.int32)[None]
+        other_id = 1 - core_id
         branch_sent = send_tp(
-            dot_nn(attended_other, o_full).astype(bf16), dot_nn(attended_own, o_full)
-        )
-        core_id = core.astype(jnp.int32)[None]
+            matmul(attended, other_id, o_full, local, bf16, False),
+            matmul(attended, core_id, o_full, local, bf16, False),
+        )
+        branch_far = branch_sent[1]
+        if pair_ctx:
+            in_ring.third()
+            in_ring.fourth()
+            out_ring.first(in_ring.three)
+            branch_far = gate(branch_far, in_ring.y_three, out_ring.one, out_ring.across)
         middle, two_own = row_call(
             after_attention,
             "after_attention",
             core_id,
             slots,
             half,
-            [(branch_sent[0], False), (branch_sent[1], False), (inputs, True)],
+            [(branch_sent[0], False), (branch_far, False), (inputs, True)],
             [exit_offsets[:1], gain_two, shift_two, b_o_rows, a_up_rows],
             [(width, f32), (wide, bf16)],
         )
         two_other = on(two_own, "tp", CORE_SWAP)
-        two_wide = jnp.concatenate([two_own, two_other], axis=0)
-
-        pre_act = dot_nn(two_wide, in_full) + hidden_offset_frozen[None, :]
-        phi = 0.5 * (1.0 + lax.erf(pre_act * (2.0 ** -0.5)))
-        hidden = (pre_act * phi).astype(bf16)
-        slope = (
-            phi + pre_act * jnp.exp(-0.5 * pre_act * pre_act) * (0.5 / jnp.pi) ** 0.5
-        ).astype(bf16)
 
         if pair_ctx:
-            out_full = assemble_gathered(
+            out_ring.second(in_ring.y_three)
+            in_full = assemble(
+                gate(spot, out_ring.two, out_ring.back),
+                in_ring.pieces(),
+                in_aug,
+                wide,
+                hidden_local,
+                ("rows", shard, shard // 2),
+                0,
+            )
+        hidden, slope = expand(two_own, two_other, in_full, hidden_offset_frozen[None, :])
+        if pair_ctx:
+            out_ring.third()
+            out_ring.fourth()
+            out_full = assemble(
                 gate(spot, hidden),
-                w_out,
-                out_near,
-                out_cross,
+                out_ring.pieces(),
                 out_aug,
                 hidden_local,
                 wide,
-                "columns",
+                ("columns", shard, hidden_local // 2),
+                0,
             )
 
         loss_own = own_rows(loss_sensitivity)
@@ -921,9 +1053,18 @@
         pick_rel = jnp.concatenate([pick_own, picks((1 - core) * half, half)], axis=0)
         grad_down_down = (factor * dot_nt(loss_rel, b_down_rows) * pick_rel).astype(bf16)
         loss_wide = widen(loss_rel, grad_down_down)
-        grad_pre = (dot_nt(loss_wide, out_full) * slope.astype(f32)).astype(bf16)
+        grad_pre = back_hidden(loss_wide, out_full, slope)
+        first_id = jnp.zeros((1,), jnp.int32)
+        second_id = first_id + 1
+        ff_cut = hidden_local // 2
         two_sent = send_tp(
-            dot_nt(grad_pre[half:], in_full).astype(bf16), dot_nt(grad_pre[:half], in_full)
+            matmul(grad_pre, second_id, in_full, ff_cut, bf16, True),
+            matmul(grad_pre, first_id, in_full, ff_cut, bf16, True),
+        )
+        late_hidden = gate(hidden, two_sent[0])
+        exit_sent = send_tp(
+            matmul(late_hidden, second_id, out_full, ff_cut, bf16, False),
+            matmul(late_hidden, first_id, out_full, ff_cut, bf16, False),
         )
         grad_middle, back_own = row_call(
             back_middle,
@@ -933,7 +1074,7 @@
             half,
             [
                 (two_sent[0], False),
-                (two_sent[1], False),
+                (gate(two_sent[1], exit_sent[0]), False),
                 (middle, False),
                 (loss_sensitivity, True),
             ],
@@ -941,16 +1082,10 @@
             [(width, f32), (wide, bf16)],
         )
         back_other = on(back_own, "tp", CORE_SWAP)
-        grad_attended = natural(
-            dot_nt(back_own, o_full).astype(bf16), dot_nt(back_other, o_full).astype(bf16)
-        )
+        grad_attended = back_attend(core_id, back_own, back_other, o_full)
 
         grad_q, grad_k, grad_v, far_grad_k, far_grad_v = attend_backward(
-            qkv, far_kv, grad_attended, attended_f, probs_far, probs_own, heads, scale
-        )
-        late_hidden = gate(hidden, two_sent[0])
-        exit_sent = send_tp(
-            dot_nn(late_hidden[half:], out_full).astype(bf16), dot_nn(late_hidden[:half], out_full)
+            qkv, far_kv, far_base, grad_attended, attended_f, probs_far, probs_own, heads, scale
         )
         if pair_ctx:
             more_k = on(far_grad_k, "ctx", [(1, 0)])
@@ -970,8 +1105,21 @@
         )
         layer_other = on(layer_wide, "tp", CORE_SWAP)
         layer_out = natural(layer_wide[:, :width], layer_other[:, :width])
-        down_down_rel = jnp.concatenate([layer_wide[:, width:], layer_other[:, width:]], axis=0)
-
+        where = jnp.stack([tensor, core]).astype(jnp.int32)
+        tiles = hidden_local // local
+        packed = pack_terms(
+            where,
+            (two_own, two_other),
+            (back_own, back_other),
+            attended,
+            grad_pre,
+            hidden,
+            grad_down_down,
+            (layer_wide[:, width:], layer_other[:, width:]),
+            loss_sensitivity,
+            local,
+        )
+        more_k = gate(more_k, packed, layer_out)
         grad_qkv = jnp.concatenate(
             [
                 grad_q,
@@ -986,23 +1134,12 @@
         low_far = on(low_pair, "tp", X_SWAP)
         low_sum = low_pair.astype(f32) + low_far.astype(f32)
         grad_down_qkv = (factor * low_sum * picks(0, tokens)).astype(bf16)
-        grad_one_other = dot_nt(other_rows(grad_qkv), q_full[:width]).astype(bf16)
-        grad_one_own = dot_nt(own_rows(grad_qkv), q_full[:width])
-        one_sent = send_tp(grad_one_other, grad_one_own)
+        qkv_cut = 3 * local // 2
+        one_sent = send_tp(
+            matmul(grad_qkv, other_id, q_full, qkv_cut, bf16, True, width),
+            matmul(grad_qkv, core_id, q_full, qkv_cut, bf16, True, width),
+        )
         tensor_id = tensor.astype(jnp.int32)[None]
-        tiles = hidden_local // local
-        packed = pack_terms(
-            gate(tensor_id, more_v),
-            two_wide,
-            jnp.concatenate([back_own, back_other], axis=0),
-            jnp.concatenate([attended_own, attended_other], axis=0),
-            grad_pre,
-            hidden,
-            grad_down_down,
-            down_down_rel,
-            loss_rel,
-            local,
-        )
         packed_qkv = pack_projections(
             gate(tensor_id, one_sent[0]), grad_down_qkv, normed_wide, grad_qkv, local
         )

time: 614 us -> 549 us (0.89)
  matrix products: 97.3 us -> 3.41 us
  Pallas kernels: 70.8 us -> 151 us
  waiting for transfers between devices: 264 us -> 188 us
  starting transfers between devices: 62.8 us -> 82.7 us
  between operations: 19.7 us -> 6.47 us
  other arithmetic: 29.6 us -> 38.7 us
    ppermute x39 -> x24, waiting for transfers between devices: 232 us -> 88.8 us  [on(): return lax.ppermute(value, axis, pairs)]
    ppermute x0 -> x32, waiting for transfers between devices: none -> 99.5 us  [the longest x4 39.9 us: second(): outward = lax.ppermute(across, 'fsdp', [(1, 0), (2, 3)])]
    pallas_call x3 -> x12, Pallas kernels: 5.33 us -> 80.1 us  [the longest x8 44.4 us: matmul(): pl.pallas_call(kernel, grid_spec=pltpu.PrefetchScalarGridSpec(num_scalar_...]
    ppermute x0 -> x32, starting transfers between devices: none -> 49.9 us  [the longest x4 11.8 us: second(): self.back = lax.ppermute(self.one, 'fsdp', [(1, 2), (2, 1)])]
    dot_general x9 -> x2, matrix products: 53 us -> 3.41 us  [dot_nt(): lax.dot_general(a, b, (((1,), (1,)), ((), ())), preferred_element_type=f32)]
    dot_general x7 -> x0, matrix products: 44.3 us -> none  [dot_nn(): lax.dot_general(a, b, (((1,), (0,)), ((), ())), preferred_element_type=f32)]
    all_gather x5 -> x0, waiting for transfers between devices: 30.8 us -> none  [gather_weight(): every = lax.all_gather(part, 'fsdp', axis=0, tiled=True)]
    ppermute x39 -> x24, starting transfers between devices: 62.4 us -> 32.8 us  [on(): return lax.ppermute(value, axis, pairs)]
  transfers between devices with their start and end apart: 44 -> 56, of which waited for: 19 -> 31; matrix products, arithmetic and copies ran while one was open for 22% -> 12% of each run, Pallas kernels for 10% -> 19%
where the time goes in v3:
time: 549 us; the launch traced here: 539 us
  waiting for transfers between devices  188 us (34%)
  Pallas kernels  151 us (28%)
  starting transfers between devices  82.7 us (15%)
  local copies, waits for them, and re-layouts  68.4 us (12%)
  other arithmetic  38.7 us (7%)
  between operations  6.47 us (1%)
    ppermute x24, waiting for transfers between devices, on(): return lax.ppermute(value, axis, pairs)  88.8 us
    pallas_call x8, Pallas kernels, matmul(): pl.pallas_call(kernel, grid_spec=pltpu.PrefetchScalarGridSpec(num_scalar_...  44.4 us
    unnamed x201, local copies, waits for them, and re-layouts  40.5 us
    ppermute x4, waiting for transfers between devices, second(): outward = lax.ppermute(across, 'fsdp', [(1, 0), (2, 3)])  39.9 us
    ppermute x24, starting transfers between devices, on(): return lax.ppermute(value, axis, pairs)  32.8 us
    ppermute x4, waiting for transfers between devices, first(): self.one = lax.ppermute(part, 'fsdp', [(0, 1), (1, 0), (2, 3), (3, 2)])  19.4 us
    pallas_call x4, Pallas kernels, row_call(): pl.pallas_call(kernel, grid_spec=pltpu.PrefetchScalarGridSpec(num_scalar_...  18.8 us
    ppermute x4, waiting for transfers between devices, fourth(): self.y_three = lax.ppermute(self.three, 'ctx', SWAP_Y)  14.8 us
  transfers between devices with their start and end apart: 56, of which 31 were waited for; matrix products, arithmetic and copies ran while one was open for 12% of the time, Pallas kernels for 19%

profile of v3, /device:TPU:9, one launch (start us, length us, event | category | flops | bytes accessed | tf_op | source)
XLA Modules:
  0.0 539.2 jit_solution(7939509427743778152)
XLA Ops:
  32.5 9.2 %collective-permute-done.3 = bf16[3,256,512]{2,1,0:T(8,128)(2,1)} collective-permute-done((bf16[3,256,512]{2,1,0:T(8,128)(2,1)}, bf16[3,256,512]{2,1,0:T(8,128)(2,1)}, u32[]{:S(2)}, u32[]{:S(2)}) %collective-permute-start.3) | collective-permute-done | bytes 786464 | tf_op jit(solution)/shard_map/ppermute | solution.py:674
  90.3 5.5 %norm_wide.3.refs_1_ = bf16[768,2176]{1,0:T(8,128)(2,1)S(1)} custom-call(s32[4]{0:T(128)S(1)} %pad_add_fusion.place_ref, s32[3]{0:T(128)S(1)} %copy-done.71, bf16[192,2048]{1,0:T(8,128)(2,1)} %collective-permute-done.refs_0_, bf16[192,2048]{1,0:T(8,128)(2,1)} %collective-permute-done.6.refs_1_, bf16[192,2048]{1,0:T(8,128)(2,1)} %collective-permute-done.7.refs_2_, ...), custom_call_target="tpu_custom_call" | custom-call | flops 1 | bytes 1 | tf_op jit(solution)/shard_map/norm_wide/pallas_call | solution.py:302
  95.8 7.7 %collective-permute-done.15.refs_2_ = bf16[256,512]{1,0:T(8,128)(2,1)S(1)} collective-permute-done((bf16[256,512]{1,0:T(8,128)(2,1)S(1)}, bf16[256,512]{1,0:T(8,128)(2,1)S(1)}, u32[]{:S(2)}, u32[]{:S(2)}) %collective-permute-start.15) | collective-permute-done | bytes 262176 | tf_op jit(solution)/shard_map/ppermute | solution.py:673
  111.1 11.9 %project.1.q_ref.k_ref.v_ref.fk_ref.fv_ref = bf16[768,2560]{1,0:T(8,128)(2,1)S(1)} custom-call(bf16[768,2176]{1,0:T(8,128)(2,1)S(1)} %copy-done.10, bf16[768,2176]{1,0:T(8,128)(2,1)S(1)} %norm_wide.3.refs_1_, f32[1,1536]{1,0:T(1,128)S(1)} %broadcast_in_dim.114.refs_2_, bf16[2176,1536]{1,0:T(8,128)(2,1)} %copy-done.3), custom_call_target="tpu_custom_call" | custom-call | flops 1 | bytes 1 | tf_op jit(solution)/shard_map/project/pallas_call | solution.py:582
  130.0 17.1 %collective-permute-done.20 = bf16[256,2048]{1,0:T(8,128)(2,1)S(1)} collective-permute-done((bf16[256,2048]{1,0:T(8,128)(2,1)}, bf16[256,2048]{1,0:T(8,128)(2,1)S(1)}, u32[]{:S(2)}, u32[]{:S(2)}) %collective-permute-start.20) | collective-permute-done | bytes 1048608 | tf_op jit(solution)/shard_map/ppermute | solution.py:674
  162.2 12.6 %attend_forward.1 = (f32[768,512]{1,0:T(8,128)}, bf16[768,512]{1,0:T(8,128)(2,1)}, bf16[4,768,768]{2,1,0:T(8,128)(2,1)}, bf16[4,768,768]{2,1,0:T(8,128)(2,1)}) custom-call(bf16[768,2560]{1,0:T(8,128)(2,1)} %copy-done, bf16[768,2560]{1,0:T(8,128)(2,1)} %copy-done, bf16[768,2560]{1,0:T(8,128)(2,1)} %copy-done, bf16[768,2560]{1,0:T(8,128)(2,1)} %copy-done, ...), custom_call_target="tpu_custom_call" | custom-call | flops 1 | bytes 1 | tf_op jit(solution)/shard_map/attend_forward/pallas_call | solution.py:106
  174.8 14.1 %collective-permute-done.23.refs_6_ = bf16[256,512]{1,0:T(8,128)(2,1)S(1)} collective-permute-done((bf16[256,512]{1,0:T(8,128)(2,1)S(1)}, bf16[256,512]{1,0:T(8,128)(2,1)S(1)}, u32[]{:S(2)}, u32[]{:S(2)}) %collective-permute-start.23) | collective-permute-done | bytes 262176 | tf_op jit(solution)/shard_map/ppermute | solution.py:688
  211.1 15.4 %collective-permute-done.30.refs_1_ = bf16[1024,512]{1,0:T(8,128)(2,1)} collective-permute-done((bf16[1024,512]{1,0:T(8,128)(2,1)}, bf16[1024,512]{1,0:T(8,128)(2,1)}, u32[]{:S(2)}, u32[]{:S(2)}) %collective-permute-start.30) | collective-permute-done | bytes 1048608 | tf_op jit(solution)/shard_map/ppermute | solution.py:668
  239.9 13.6 %collective-permute-done.33 = bf16[1024,512]{1,0:T(8,128)(2,1)} collective-permute-done((bf16[1024,512]{1,0:T(8,128)(2,1)}, bf16[1024,512]{1,0:T(8,128)(2,1)}, u32[]{:S(2)}, u32[]{:S(2)}) %collective-permute-start.33) | collective-permute-done | bytes 1048608 | tf_op jit(solution)/shard_map/ppermute | solution.py:674
  262.6 8.8 %collective-permute-done.25.refs_1_ = bf16[384,2176]{1,0:T(8,128)(2,1)S(1)} collective-permute-done((bf16[384,2176]{1,0:T(8,128)(2,1)S(1)}, bf16[384,2176]{1,0:T(8,128)(2,1)S(1)}, u32[]{:S(2)}, u32[]{:S(2)}) %collective-permute-start.25) | collective-permute-done | bytes 1671200 | tf_op jit(solution)/shard_map/ppermute | solution.py:816
  299.6 11.7 %expand.1 = (bf16[768,2048]{1,0:T(8,128)(2,1)S(1)}, bf16[768,2048]{1,0:T(8,128)(2,1)S(1)}) custom-call(bf16[384,2176]{1,0:T(8,128)(2,1)S(1)} %get-tuple-element.107.own_ref.two_a, bf16[384,2176]{1,0:T(8,128)(2,1)S(1)} %collective-permute-done.32.other_ref.two_b, bf16[2176,2048]{1,0:T(8,128)(2,1)} %copy-done.2, f32[1,2048]{1,0:T(1,128)S(1)} %bitcast.69), custom_call_target="tpu_custom_call" | custom-call | flops 1 | bytes 1 | tf_op jit(solution)/shard_map/expand/pallas_call | solution.py:616
  318.3 10.1 %back_hidden.1.x_ref.gp_ref = bf16[768,2048]{1,0:T(8,128)(2,1)S(1)} custom-call(bf16[768,2176]{1,0:T(8,128)(2,1)S(1)} %pad_maximum_fusion.x_ref, bf16[2048,2176]{1,0:T(8,128)(2,1)} %copy-done.1, bf16[768,2048]{1,0:T(8,128)(2,1)S(1)} %get-tuple-element.120.s_ref), custom_call_target="tpu_custom_call" | custom-call | flops 1 | bytes 1 | tf_op jit(solution)/shard_map/back_hidden/pallas_call | solution.py:643
  328.4 6.9 %matmul.11 = bf16[384,2176]{1,0:T(8,128)(2,1)S(1)} custom-call(s32[1]{0:T(128)} %constant.159.clone.1.half_ref, bf16[768,2048]{1,0:T(8,128)(2,1)S(1)} %back_hidden.1.x_ref.gp_ref, bf16[2176,2048]{1,0:T(8,128)(2,1)} %copy-done.2), custom_call_target="tpu_custom_call" | custom-call | flops 1 | bytes 1 | tf_op jit(solution)/shard_map/matmul/pallas_call | solution.py:731
  336.3 6.9 %matmul.10 = bf16[384,2176]{1,0:T(8,128)(2,1)S(1)} custom-call(s32[1]{0:T(128)} %constant.146.clone.1.half_ref, bf16[768,2048]{1,0:T(8,128)(2,1)S(1)} %back_hidden.1.x_ref.gp_ref, bf16[2176,2048]{1,0:T(8,128)(2,1)} %copy-done.2), custom_call_target="tpu_custom_call" | custom-call | flops 1 | bytes 1 | tf_op jit(solution)/shard_map/matmul/pallas_call | solution.py:731
  343.6 8.5 %matmul.13 = bf16[384,2176]{1,0:T(8,128)(2,1)} custom-call(s32[1]{0:T(128)} %constant.159.clone.1.half_ref, bf16[768,2048]{1,0:T(8,128)(2,1)S(1)} %get-tuple-element.121.x_ref.hid_ref, bf16[2048,2176]{1,0:T(8,128)(2,1)} %copy-done.1), custom_call_target="tpu_custom_call" | custom-call | flops 1 | bytes 1 | tf_op jit(solution)/shard_map/matmul/pallas_call | solution.py:731
  352.2 7.0 %matmul.12 = bf16[384,2176]{1,0:T(8,128)(2,1)S(1)} custom-call(s32[1]{0:T(128)} %constant.146.clone.1.half_ref, bf16[768,2048]{1,0:T(8,128)(2,1)S(1)} %get-tuple-element.121.x_ref.hid_ref, bf16[2048,2176]{1,0:T(8,128)(2,1)} %copy-done.1), custom_call_target="tpu_custom_call" | custom-call | flops 1 | bytes 1 | tf_op jit(solution)/shard_map/matmul/pallas_call | solution.py:731
  362.4 27.5 %collective-permute-done.42.refs_1_ = bf16[384,2176]{1,0:T(8,128)(2,1)} collective-permute-done((bf16[384,2176]{1,0:T(8,128)(2,1)S(1)}, bf16[384,2176]{1,0:T(8,128)(2,1)}, u32[]{:S(2)}, u32[]{:S(2)}) %collective-permute-start.42) | collective-permute-done | bytes 1671200 | tf_op jit(solution)/shard_map/ppermute | solution.py:816
  389.9 5.3 back_middle.1
  404.4 13.1 %attend_backward.1 = (bf16[768,512]{1,0:T(8,128)(2,1)}, bf16[768,512]{1,0:T(8,128)(2,1)}, bf16[768,512]{1,0:T(8,128)(2,1)}, bf16[768,512]{1,0:T(8,128)(2,1)}, bf16[768,512]{1,0:T(8,128)(2,1)}) custom-call(bf16[768,2560]{1,0:T(8,128)(2,1)} %copy-done, bf16[768,2560]{1,0:T(8,128)(2,1)} %copy-done, bf16[768,2560]{1,0:T(8,128)(2,1)} %copy-done, ...), custom_call_target="tpu_custom_call" | custom-call | flops 1 | bytes 1 | tf_op jit(solution)/shard_map/attend_backward/pallas_call | solution.py:181
  418.8 17.9 %collective-permute-done.41.refs_1_ = bf16[384,2176]{1,0:T(8,128)(2,1)} collective-permute-done((bf16[384,2176]{1,0:T(8,128)(2,1)}, bf16[384,2176]{1,0:T(8,128)(2,1)}, u32[]{:S(2)}, u32[]{:S(2)}) %collective-permute-start.41) | collective-permute-done | bytes 1671200 | tf_op jit(solution)/shard_map/ppermute | solution.py:816
  467.3 6.5 %matmul.15 = bf16[384,2048]{1,0:T(8,128)(2,1)} custom-call(s32[1]{0:T(128)S(6)} %sub.49.half_ref, bf16[768,1536]{1,0:T(8,128)(2,1)S(1)} %pad_maximum_fusion.3.x_ref.gq_ref, bf16[2176,1536]{1,0:T(8,128)(2,1)} %copy-done.3), custom_call_target="tpu_custom_call" | custom-call | flops 1 | bytes 1 | tf_op jit(solution)/shard_map/matmul/pallas_call | solution.py:731
  476.8 5.2 matmul.14
  496.7 9.1 %collective-permute-done.53 = bf16[576,128]{1,0:T(8,128)(2,1)S(1)} collective-permute-done((bf16[576,128]{1,0:T(8,128)(2,1)S(1)}, bf16[576,128]{1,0:T(8,128)(2,1)S(1)}, u32[]{:S(2)}, u32[]{:S(2)}) %collective-permute-start.53) | collective-permute-done | bytes 147488 | tf_op jit(solution)/shard_map/ppermute | solution.py:816
  508.9 11.5 %collective-permute-done.54.cross_ref = bf16[4,576,128]{2,1,0:T(8,128)(2,1)} collective-permute-done((bf16[4,576,128]{2,1,0:T(8,128)(2,1)}, bf16[4,576,128]{2,1,0:T(8,128)(2,1)}, u32[]{:S(2)}, u32[]{:S(2)}) %collective-permute-start.54) | collective-permute-done | bytes 589856 | tf_op jit(solution)/shard_map/ppermute | solution.py:816
  (426 shorter events, 269.8 us)
Async XLA Ops:
  9.4 34.4 %collective-permute-start = (bf16[192,2048]{1,0:T(8,128)(2,1)}, bf16[192,2048]{1,0:T(8,128)(2,1)}, u32[]{:S(2)}, u32[]{:S(2)}) collective-permute-start(bf16[192,2048]{1,0:T(8,128)(2,1)} %constant_dynamic-slice_fusion.12), channel_id=1, source_target_pairs={{0,4},{1,5},{2,6},{3,7},{8,12},{9,13},{10,14},{11,15},{16,20},{17,... | collective-permute-start | bytes 2359304 | tf_op jit(solution)/shard_map/ppermute | solution.py:816
  54.3 22.1 %collective-permute-start.12 = (bf16[3,256,512]{2,1,0:T(8,128)(2,1)}, bf16[3,256,512]{2,1,0:T(8,128)(2,1)}, u32[]{:S(2)}, u32[]{:S(2)}) collective-permute-start(bf16[3,256,512]{2,1,0:T(8,128)(2,1)} %broadcast_select_fusion.9.refs_3_), channel_id=1, source_target_pairs={{0,4},{4,0},{1,5},{5,1},{2,6},{6,2},{3,7},{7,3},{8,12},{12,8},{9,1... | collective-permute-start | bytes 2359304 | tf_op jit(solution)/shard_map/ppermute | solution.py:682
  80.2 23.4 %collective-permute-start.16 = (bf16[3,256,512]{2,1,0:T(8,128)(2,1)S(1)}, bf16[3,256,512]{2,1,0:T(8,128)(2,1)}, u32[]{:S(2)}, u32[]{:S(2)}) collective-permute-start(bf16[3,256,512]{2,1,0:T(8,128)(2,1)S(1)} %broadcast_select_fusion.8.refs_5_), channel_id=1, source_target_pairs={{0,4},{4,0},{1,5},{5,1},{2,6},{6,2},{3,7},{7,3},{8,12},{12,8},{9,1... | collective-permute-start | bytes 2359304 | tf_op jit(solution)/shard_map/ppermute | solution.py:688
  80.2 23.4 %collective-permute-start.15 = (bf16[256,512]{1,0:T(8,128)(2,1)S(1)}, bf16[256,512]{1,0:T(8,128)(2,1)S(1)}, u32[]{:S(2)}, u32[]{:S(2)}) collective-permute-start(bf16[256,512]{1,0:T(8,128)(2,1)S(1)} %collective-permute-done.10.refs_1_), channel_id=1, source_target_pairs={{0,4},{4,0},{1,5},{5,1},{2,6},{6,2},{3,7},{7,3},{8,12},{12,8},{9,1... | collective-permute-start | bytes 786440 | tf_op jit(solution)/shard_map/ppermute | solution.py:673
  86.5 38.4 %collective-permute-start.17 = (bf16[256,2048]{1,0:T(8,128)(2,1)}, bf16[256,2048]{1,0:T(8,128)(2,1)S(1)}, u32[]{:S(2)}, u32[]{:S(2)}) collective-permute-start(bf16[256,2048]{1,0:T(8,128)(2,1)} %constant_dynamic-slice_fusion.5), channel_id=1, source_target_pairs={{0,8},{8,0},{16,24},{24,16},{1,9},{9,1},{17,25},{25,17},{2,10},{10... | collective-permute-start | bytes 3145736 | tf_op jit(solution)/shard_map/ppermute | solution.py:668
  86.5 38.5 %collective-permute-start.18 = (bf16[256,2048]{1,0:T(8,128)(2,1)}, bf16[256,2048]{1,0:T(8,128)(2,1)}, u32[]{:S(2)}, u32[]{:S(2)}) collective-permute-start(bf16[256,2048]{1,0:T(8,128)(2,1)} %constant_dynamic-slice_fusion.5), channel_id=1, source_target_pairs={{8,16},{16,8},{9,17},{17,9},{10,18},{18,10},{11,19},{19,11},{12,20... | collective-permute-start | bytes 3145736 | tf_op jit(solution)/shard_map/ppermute | solution.py:669
  126.4 24.9 %collective-permute-start.21 = (bf16[256,2048]{1,0:T(8,128)(2,1)S(1)}, bf16[256,2048]{1,0:T(8,128)(2,1)}, u32[]{:S(2)}, u32[]{:S(2)}) collective-permute-start(bf16[256,2048]{1,0:T(8,128)(2,1)S(1)} %collective-permute-done.17.refs_1_), channel_id=1, source_target_pairs={{8,16},{16,8},{9,17},{17,9},{10,18},{18,10},{11,19},{19,11},{12,20... | collective-permute-start | bytes 3145736 | tf_op jit(solution)/shard_map/ppermute | solution.py:675
  129.9 22.4 %collective-permute-start.26 = (bf16[256,2048]{1,0:T(8,128)(2,1)S(1)}, bf16[256,2048]{1,0:T(8,128)(2,1)S(1)}, u32[]{:S(2)}, u32[]{:S(2)}) collective-permute-start(bf16[256,2048]{1,0:T(8,128)(2,1)S(1)} %collective-permute-done.17.refs_1_), channel_id=1, source_target_pairs={{0,4},{4,0},{1,5},{5,1},{2,6},{6,2},{3,7},{7,3},{8,12},{12,8},{9,1... | collective-permute-start | bytes 3145736 | tf_op jit(solution)/shard_map/ppermute | solution.py:673
  153.2 46.6 %collective-permute-start.27 = (bf16[256,2048]{1,0:T(8,128)(2,1)}, bf16[256,2048]{1,0:T(8,128)(2,1)}, u32[]{:S(2)}, u32[]{:S(2)}) collective-permute-start(bf16[256,2048]{1,0:T(8,128)(2,1)} %collective-permute-done.21), channel_id=1, source_target_pairs={{8,0},{16,24},{9,1},{17,25},{10,2},{18,26},{11,3},{19,27},{12,4},{... | collective-permute-start | bytes 3145736 | tf_op jit(solution)/shard_map/ppermute | solution.py:683
  157.1 45.1 %collective-permute-start.28 = (bf16[256,2048]{1,0:T(8,128)(2,1)}, bf16[256,2048]{1,0:T(8,128)(2,1)}, u32[]{:S(2)}, u32[]{:S(2)}) collective-permute-start(bf16[256,2048]{1,0:T(8,128)(2,1)} %broadcast_select_fusion.7.refs_3_), channel_id=1, source_target_pairs={{0,4},{4,0},{1,5},{5,1},{2,6},{6,2},{3,7},{7,3},{8,12},{12,8},{9,1... | collective-permute-start | bytes 3145736 | tf_op jit(solution)/shard_map/ppermute | solution.py:682
  161.4 27.5 %collective-permute-start.23 = (bf16[256,512]{1,0:T(8,128)(2,1)S(1)}, bf16[256,512]{1,0:T(8,128)(2,1)S(1)}, u32[]{:S(2)}, u32[]{:S(2)}) collective-permute-start(bf16[256,512]{1,0:T(8,128)(2,1)S(1)} %broadcast_select_fusion.10.refs_5_), channel_id=1, source_target_pairs={{0,4},{4,0},{1,5},{5,1},{2,6},{6,2},{3,7},{7,3},{8,12},{12,8},{9,1... | collective-permute-start | bytes 786440 | tf_op jit(solution)/shard_map/ppermute | solution.py:688
  194.6 39.2 %collective-permute-start.24 = (bf16[384,2176]{1,0:T(8,128)(2,1)}, bf16[384,2176]{1,0:T(8,128)(2,1)}, u32[]{:S(2)}, u32[]{:S(2)}) collective-permute-start(bf16[384,2176]{1,0:T(8,128)(2,1)} %matmul.9), channel_id=1, source_target_pairs={{0,1},{1,0},{2,3},{3,2},{4,5},{5,4},{6,7},{7,6},{8,9},{9,8},{10,11... | collective-permute-start | bytes 5013512 | tf_op jit(solution)/shard_map/ppermute | solution.py:816
  202.2 24.3 %collective-permute-start.30 = (bf16[1024,512]{1,0:T(8,128)(2,1)}, bf16[1024,512]{1,0:T(8,128)(2,1)}, u32[]{:S(2)}, u32[]{:S(2)}) collective-permute-start(bf16[1024,512]{1,0:T(8,128)(2,1)} %constant_dynamic-slice_fusion.2), channel_id=1, source_target_pairs={{0,8},{8,0},{16,24},{24,16},{1,9},{9,1},{17,25},{25,17},{2,10},{10... | collective-permute-start | bytes 3145736 | tf_op jit(solution)/shard_map/ppermute | solution.py:668
  202.2 26.2 %collective-permute-start.31 = (bf16[1024,512]{1,0:T(8,128)(2,1)}, bf16[1024,512]{1,0:T(8,128)(2,1)}, u32[]{:S(2)}, u32[]{:S(2)}) collective-permute-start(bf16[1024,512]{1,0:T(8,128)(2,1)} %constant_dynamic-slice_fusion.2), channel_id=1, source_target_pairs={{8,16},{16,8},{9,17},{17,9},{10,18},{18,10},{11,19},{19,11},{12,20... | collective-permute-start | bytes 3145736 | tf_op jit(solution)/shard_map/ppermute | solution.py:669
  204.4 24.0 %collective-permute-start.29 = (bf16[256,2048]{1,0:T(8,128)(2,1)}, bf16[256,2048]{1,0:T(8,128)(2,1)}, u32[]{:S(2)}, u32[]{:S(2)}) collective-permute-start(bf16[256,2048]{1,0:T(8,128)(2,1)} %broadcast_select_fusion.6.refs_5_), channel_id=1, source_target_pairs={{0,4},{4,0},{1,5},{5,1},{2,6},{6,2},{3,7},{7,3},{8,12},{12,8},{9,1... | collective-permute-start | bytes 3145736 | tf_op jit(solution)/shard_map/ppermute | solution.py:688
  228.5 27.3 %collective-permute-start.34 = (bf16[1024,512]{1,0:T(8,128)(2,1)}, bf16[1024,512]{1,0:T(8,128)(2,1)}, u32[]{:S(2)}, u32[]{:S(2)}) collective-permute-start(bf16[1024,512]{1,0:T(8,128)(2,1)} %collective-permute-done.30.refs_1_), channel_id=1, source_target_pairs={{8,16},{16,8},{9,17},{17,9},{10,18},{18,10},{11,19},{19,11},{12,20... | collective-permute-start | bytes 3145736 | tf_op jit(solution)/shard_map/ppermute | solution.py:675
  231.5 24.3 %collective-permute-start.35 = (bf16[1024,512]{1,0:T(8,128)(2,1)}, bf16[1024,512]{1,0:T(8,128)(2,1)}, u32[]{:S(2)}, u32[]{:S(2)}) collective-permute-start(bf16[1024,512]{1,0:T(8,128)(2,1)} %collective-permute-done.30.refs_1_), channel_id=1, source_target_pairs={{0,4},{4,0},{1,5},{5,1},{2,6},{6,2},{3,7},{7,3},{8,12},{12,8},{9,1... | collective-permute-start | bytes 3145736 | tf_op jit(solution)/shard_map/ppermute | solution.py:673
  235.7 35.7 %collective-permute-start.25 = (bf16[384,2176]{1,0:T(8,128)(2,1)S(1)}, bf16[384,2176]{1,0:T(8,128)(2,1)S(1)}, u32[]{:S(2)}, u32[]{:S(2)}) collective-permute-start(bf16[384,2176]{1,0:T(8,128)(2,1)S(1)} %reduce-precision_convert_fusion.2.refs_0_), channel_id=1, source_target_pairs={{0,2},{2,0},{1,3},{3,1},{4,6},{6,4},{5,7},{7,5},{8,10},{10,8},{9,1... | collective-permute-start | bytes 5013512 | tf_op jit(solution)/shard_map/ppermute | solution.py:816
  255.8 30.0 %collective-permute-start.36 = (bf16[1024,512]{1,0:T(8,128)(2,1)}, bf16[1024,512]{1,0:T(8,128)(2,1)}, u32[]{:S(2)}, u32[]{:S(2)}) collective-permute-start(bf16[1024,512]{1,0:T(8,128)(2,1)} %collective-permute-done.34), channel_id=1, source_target_pairs={{8,0},{16,24},{9,1},{17,25},{10,2},{18,26},{11,3},{19,27},{12,4},{... | collective-permute-start | bytes 3145736 | tf_op jit(solution)/shard_map/ppermute | solution.py:683
  261.1 26.0 %collective-permute-start.37 = (bf16[1024,512]{1,0:T(8,128)(2,1)}, bf16[1024,512]{1,0:T(8,128)(2,1)}, u32[]{:S(2)}, u32[]{:S(2)}) collective-permute-start(bf16[1024,512]{1,0:T(8,128)(2,1)} %broadcast_select_fusion.5.refs_3_), channel_id=1, source_target_pairs={{0,4},{4,0},{1,5},{5,1},{2,6},{6,2},{3,7},{7,3},{8,12},{12,8},{9,1... | collective-permute-start | bytes 3145736 | tf_op jit(solution)/shard_map/ppermute | solution.py:682
  287.1 24.8 %collective-permute-start.38 = (bf16[1024,512]{1,0:T(8,128)(2,1)S(1)}, bf16[1024,512]{1,0:T(8,128)(2,1)S(1)}, u32[]{:S(2)}, u32[]{:S(2)}) collective-permute-start(bf16[1024,512]{1,0:T(8,128)(2,1)S(1)} %broadcast_select_fusion.4.refs_5_), channel_id=1, source_target_pairs={{0,4},{4,0},{1,5},{5,1},{2,6},{6,2},{3,7},{7,3},{8,12},{12,8},{9,1... | collective-permute-start | bytes 3145736 | tf_op jit(solution)/shard_map/ppermute | solution.py:688
  352.2 37.7 %collective-permute-start.42 = (bf16[384,2176]{1,0:T(8,128)(2,1)S(1)}, bf16[384,2176]{1,0:T(8,128)(2,1)}, u32[]{:S(2)}, u32[]{:S(2)}) collective-permute-start(bf16[384,2176]{1,0:T(8,128)(2,1)S(1)} %reduce-precision_convert_fusion.1.refs_0_), channel_id=1, source_target_pairs={{0,2},{2,0},{1,3},{3,1},{4,6},{6,4},{5,7},{7,5},{8,10},{10,8},{9,1... | collective-permute-start | bytes 5013512 | tf_op jit(solution)/shard_map/ppermute | solution.py:816
  398.2 38.4 %collective-permute-start.41 = (bf16[384,2176]{1,0:T(8,128)(2,1)}, bf16[384,2176]{1,0:T(8,128)(2,1)}, u32[]{:S(2)}, u32[]{:S(2)}) collective-permute-start(bf16[384,2176]{1,0:T(8,128)(2,1)} %reduce-precision_convert_fusion.refs_0_), channel_id=1, source_target_pairs={{0,2},{2,0},{1,3},{3,1},{4,6},{6,4},{5,7},{7,5},{8,10},{10,8},{9,1... | collective-permute-start | bytes 5013512 | tf_op jit(solution)/shard_map/ppermute | solution.py:816
  486.5 36.8 %collective-permute-start.48 = (bf16[384,2048]{1,0:T(8,128)(2,1)}, bf16[384,2048]{1,0:T(8,128)(2,1)}, u32[]{:S(2)}, u32[]{:S(2)}) collective-permute-start(bf16[384,2048]{1,0:T(8,128)(2,1)} %reduce-precision_convert_fusion.3.refs_0_), channel_id=1, source_target_pairs={{0,2},{2,0},{1,3},{3,1},{4,6},{6,4},{5,7},{7,5},{8,10},{10,8},{9,1... | collective-permute-start | bytes 4718600 | tf_op jit(solution)/shard_map/ppermute | solution.py:816
  (134 other events, 1695.6 us)

commit v4 on v3

--- a/solution.py
+++ b/solution.py
@@ -127,7 +127,7 @@
             jax.ShapeDtypeStruct((heads, tokens, far_rows), bf16),
             jax.ShapeDtypeStruct((heads, tokens, tokens), bf16),
         ],
-        compiler_params=pltpu.CompilerParams(vmem_limit_bytes=56 << 20),
+        compiler_params=pltpu.CompilerParams(vmem_limit_bytes=(14 if far_rows == tokens else 56) << 20),
         cost_estimate=HINT,
         name="attend_forward",
     )(qkv, qkv, qkv, far, far, far_bias, own_bias)
@@ -140,7 +140,7 @@
 
     def kernel(
         q_ref, k_ref, v_ref, fk_ref, fv_ref, g_ref, o_ref, pf_ref, po_ref,
-        dq_ref, dk_ref, dv_ref, dfk_ref, dfv_ref,
+        dq_ref, dk_ref, dv_ref, far_ref,
         dk_acc, dv_acc, dfk_acc, dfv_acc,
     ):
         far_k = fk_ref[...]
@@ -171,13 +171,13 @@
                 dv_acc[:width, :] += dot_tn(p_own, g)
         dk_ref[...] = (dk_acc[...] * scale).astype(bf16)
         dv_ref[...] = dv_acc[...].astype(bf16)
-        dfk_ref[...] = (dfk_acc[...] * scale).astype(bf16)
-        dfv_ref[...] = dfv_acc[...].astype(bf16)
+        far_ref[0] = (dfk_acc[...] * scale).astype(bf16)
+        far_ref[1] = dfv_acc[...].astype(bf16)
 
     head_spec = pl.BlockSpec((tokens, HD), lambda h: (0, h))
-    far_spec = pl.BlockSpec((far_rows, HD), lambda h: (0, h))
+    far_spec = pl.BlockSpec((2, far_rows, HD), lambda h: (0, 0, h))
     own_shape = jax.ShapeDtypeStruct((tokens, heads * HD), bf16)
-    far_shape = jax.ShapeDtypeStruct((far_rows, heads * HD), bf16)
+    far_shape = jax.ShapeDtypeStruct((2, far_rows, heads * HD), bf16)
     return pl.pallas_call(
         kernel,
         grid=(heads,),
@@ -192,21 +192,21 @@
             pl.BlockSpec((1, tokens, far_rows), lambda h: (h, 0, 0)),
             pl.BlockSpec((1, tokens, tokens), lambda h: (h, 0, 0)),
         ],
-        out_specs=[head_spec, head_spec, head_spec, far_spec, far_spec],
-        out_shape=[own_shape, own_shape, own_shape, far_shape, far_shape],
+        out_specs=[head_spec, head_spec, head_spec, far_spec],
+        out_shape=[own_shape, own_shape, own_shape, far_shape],
         scratch_shapes=[
             pltpu.VMEM((tokens, HD), f32),
             pltpu.VMEM((tokens, HD), f32),
             pltpu.VMEM((far_rows, HD), f32),
             pltpu.VMEM((far_rows, HD), f32),
         ],
-        compiler_params=pltpu.CompilerParams(vmem_limit_bytes=56 << 20),
+        compiler_params=pltpu.CompilerParams(vmem_limit_bytes=(16 if far_rows == tokens else 56) << 20),
         cost_estimate=HINT,
         name="attend_backward",
     )(qkv, qkv, qkv, far, far, grad_attended, attended, probs_far, probs_own)
 
 
-def assemble(spot, pieces, tail, rows, columns, step, parts):
+def assemble(spot, pieces, tail, rows, columns, step, parts, straight=False):
     direction, shard, half_rows = step
     count = max(parts, 1)
     part_columns = columns // count if parts else columns
@@ -236,8 +236,8 @@
         fixed = moves(own, group, 0, 0)
         fixed += moves(one, group ^ 1, context, count)
         fixed += moves(y_one, group ^ 1, 1 - context, 2 * count)
-        second = jnp.where(inner, group ^ 3, group ^ 2)
-        third = jnp.where(inner, group ^ 2, group ^ 3)
+        second = group ^ 2 if straight else jnp.where(inner, group ^ 3, group ^ 2)
+        third = group ^ 3 if straight else jnp.where(inner, group ^ 2, group ^ 3)
         fixed += moves(two, second, context, 3 * count)
         fixed += moves(y_two, second, 1 - context, 4 * count)
         fixed += moves(three, third, context, 5 * count)
@@ -262,12 +262,12 @@
         grid_spec=pltpu.PrefetchScalarGridSpec(
             num_scalar_prefetch=1,
             grid=(),
-            in_specs=[pl.BlockSpec(memory_space=pl.ANY)] * 8,
+            in_specs=[pl.BlockSpec(memory_space=pltpu.HBM)] * 8,
             out_specs=pl.BlockSpec(memory_space=pltpu.VMEM),
             scratch_shapes=[pltpu.SemaphoreType.DMA((7 * count + 1,))],
         ),
         out_shape=jax.ShapeDtypeStruct((rows, columns), bf16),
-        compiler_params=pltpu.CompilerParams(vmem_limit_bytes=24 << 20),
+        compiler_params=pltpu.CompilerParams(vmem_limit_bytes=4 << 20),
         cost_estimate=HINT,
         name="assemble",
     )(spot, *pieces, tail)
@@ -308,7 +308,7 @@
             out_specs=whole,
         ),
         out_shape=jax.ShapeDtypeStruct((tokens, width + AUG), bf16),
-        compiler_params=pltpu.CompilerParams(vmem_limit_bytes=32 << 20),
+        compiler_params=pltpu.CompilerParams(vmem_limit_bytes=12 << 20),
         cost_estimate=HINT,
         name="norm_wide",
     )(places, slots, *pieces, down_rows, gain, shift)
@@ -355,10 +355,104 @@
             out_specs=[pl.BlockSpec((chunk, c), lambda i, c_, s: (i, 0)) for c, _ in outs],
         ),
         out_shape=[jax.ShapeDtypeStruct((rows, c), d) for c, d in outs],
-        compiler_params=pltpu.CompilerParams(vmem_limit_bytes=40 << 20),
+        compiler_params=pltpu.CompilerParams(vmem_limit_bytes=12 << 20),
         cost_estimate=HINT,
         name=name,
     )(core, slots, *[a for a, _ in moving], *fixed)
+
+
+def join(mine, got):
+    piece = got[0].shape[0]
+
+    def kernel(a_ref, *refs):
+        out_ref, sum_ref, sem = refs[len(got) :]
+        for i, b_ref in enumerate(refs[: len(got)]):
+            rows = slice(i * piece, (i + 1) * piece)
+            sum_ref[rows, :] = (a_ref[rows, :].astype(f32) + b_ref[...].astype(f32)).astype(bf16)
+        move = pltpu.make_async_copy(sum_ref, out_ref, sem)
+        move.start()
+        move.wait()
+
+    whole = pl.BlockSpec(memory_space=pltpu.VMEM)
+    return pl.pallas_call(
+        kernel,
+        in_specs=[whole] * (1 + len(got)),
+        out_specs=pl.BlockSpec(memory_space=pltpu.HBM),
+        out_shape=jax.ShapeDtypeStruct(mine.shape, bf16),
+        scratch_shapes=[pltpu.VMEM(mine.shape, bf16), pltpu.SemaphoreType.DMA],
+        compiler_params=pltpu.CompilerParams(vmem_limit_bytes=8 << 20),
+        cost_estimate=HINT,
+        name="join",
+    )(mine, *got)
+
+
+def back_project(grad, core, weight, width):
+    tokens, summed = grad.shape
+    size = tokens // 2
+
+    def kernel(core_ref, x_ref, w_ref, other_ref, own_ref):
+        part = dot_nt(x_ref[...], w_ref[...]).astype(bf16)
+
+        @pl.when(pl.program_id(0) == 0)
+        def _():
+            other_ref[...] = part
+
+        @pl.when(pl.program_id(0) == 1)
+        def _():
+            own_ref[...] = part
+
+    whole = pl.BlockSpec((size, width), lambda n, c: (0, 0))
+    shape = jax.ShapeDtypeStruct((size, width), bf16)
+    return pl.pallas_call(
+        kernel,
+        grid_spec=pltpu.PrefetchScalarGridSpec(
+            num_scalar_prefetch=1,
+            grid=(2,),
+            in_specs=[
+                pl.BlockSpec((size, summed), lambda n, c: (jnp.where(n == 0, 1 - c[0], c[0]), 0)),
+                pl.BlockSpec((width, summed), lambda n, c: (0, 0)),
+            ],
+            out_specs=[whole, whole],
+        ),
+        out_shape=[shape, shape],
+        compiler_params=pltpu.CompilerParams(vmem_limit_bytes=26 << 20),
+        cost_estimate=HINT,
+        name="back_project",
+    )(core, grad, weight)
+
+
+def place_rows(core, own, other, width):
+    size = own.shape[0]
+
+    def kernel(core_ref, own_ref, other_ref, out_ref, sem):
+        moves = []
+        for n, (ref, side) in enumerate(((own_ref, core_ref[0]), (other_ref, 1 - core_ref[0]))):
+            start = pl.multiple_of(side * size, size)
+            moves.append(
+                pltpu.make_async_copy(
+                    ref.at[:, pl.ds(0, width)], out_ref.at[pl.ds(start, size), :], sem.at[n]
+                )
+            )
+        for move in moves:
+            move.start()
+        for move in moves:
+            move.wait()
+
+    whole = pl.BlockSpec(memory_space=pltpu.VMEM)
+    return pl.pallas_call(
+        kernel,
+        grid_spec=pltpu.PrefetchScalarGridSpec(
+            num_scalar_prefetch=1,
+            grid=(),
+            in_specs=[whole] * 2,
+            out_specs=pl.BlockSpec(memory_space=pltpu.HBM),
+            scratch_shapes=[pltpu.SemaphoreType.DMA((2,))],
+        ),
+        out_shape=jax.ShapeDtypeStruct((2 * size, width), bf16),
+        compiler_params=pltpu.CompilerParams(vmem_limit_bytes=8 << 20),
+        cost_estimate=HINT,
+        name="place_rows",
+    )(core, own, other)
 
 
 def after_attention(pick, mine, far, rows, exit_row, gain, shift, b_o_rows, a_up_rows):
@@ -377,7 +471,7 @@
     total = mine.astype(f32) + far.astype(f32)
     down = factor * jnp.where(pick, total[:, width:], 0.0).astype(bf16)
     out = middle + total[:, :width] + exit_row + dot_nn(down, b_down_rows)
-    return (jnp.concatenate([out.astype(bf16), down], axis=1),)
+    return out.astype(bf16), down
 
 
 def back_middle(pick, mine, far, middle, loss, gain, a_up_rows, b_o_rows):
@@ -399,27 +493,24 @@
     return ((grad_middle + norm_back(grad_normed * gain, unit, inverse)).astype(bf16),)
 
 
-def pack_terms(where, two, back, attended, grad_pre, hidden, grad_dd, dd, loss, local):
-    width = loss.shape[1]
-    half = loss.shape[0] // 2
+def pack_terms(tensor, core, two, back, attended, grad_pre, hidden, grad_dd, local):
+    width = two[0].shape[1] - AUG
+    half = two[0].shape[0]
     cut = local // 4
 
-    def kernel(
-        t_ref, two_a, two_b, back_a, back_b, att_ref, gp_ref, hid_ref, gdd_ref, dd_a, dd_b, loss_ref, out
-    ):
+    def kernel(t_ref, two_a, two_b, back_a, back_b, att_ref, gp_ref, hid_ref, gdd_ref, out):
         lanes = pl.ds(pl.multiple_of(t_ref[0] * local, local), local)
         mine = pl.ds(pl.multiple_of(t_ref[1] * half, half), half)
         theirs = pl.ds(pl.multiple_of((1 - t_ref[1]) * half, half), half)
-        halves = ((two_a, back_a, dd_a, mine), (two_b, back_b, dd_b, theirs))
+        halves = ((two_a, back_a, mine), (two_b, back_b, theirs))
 
         def both(make):
             return make(*halves[0]) + make(*halves[1])
 
         terms = [
-            both(lambda t, b, d, r: dot_tn(b[:, width:], att_ref[r, :]))[PAIR : 2 * PAIR],
-            both(lambda t, b, d, r: dot_tn(t[:, width:], b[:, lanes]))[PAIR : 2 * PAIR],
-            both(lambda t, b, d, r: dot_tn(b[:, width:], t[:, lanes]))[:PAIR],
-            both(lambda t, b, d, r: dot_tn(d[...], loss_ref[r, lanes]))[:PAIR],
+            both(lambda t, b, r: dot_tn(b[:, width:], att_ref[r, :]))[PAIR : 2 * PAIR],
+            both(lambda t, b, r: dot_tn(t[:, width:], b[:, lanes]))[PAIR : 2 * PAIR],
+            both(lambda t, b, r: dot_tn(b[:, width:], t[:, lanes]))[:PAIR],
         ]
         for n, term in enumerate(terms):
             low = term.astype(bf16)
@@ -444,13 +535,45 @@
     return pl.pallas_call(
         kernel,
         grid_spec=pltpu.PrefetchScalarGridSpec(
-            num_scalar_prefetch=1, grid=(), in_specs=[whole] * 11, out_specs=whole
+            num_scalar_prefetch=1, grid=(), in_specs=[whole] * 8, out_specs=whole
         ),
-        out_shape=jax.ShapeDtypeStruct((4, (4 + 2 * tiles) * PAIR, cut), bf16),
-        compiler_params=pltpu.CompilerParams(vmem_limit_bytes=40 << 20),
+        out_shape=jax.ShapeDtypeStruct((4, (3 + 2 * tiles) * PAIR, cut), bf16),
+        compiler_params=pltpu.CompilerParams(vmem_limit_bytes=24 << 20),
         cost_estimate=HINT,
         name="pack_terms",
-    )(where, *two, *back, attended, grad_pre, hidden, grad_dd, *dd, loss)
+    )(jnp.stack([tensor, core]), *two, *back, attended, grad_pre, hidden, grad_dd)
+
+
+def pack_layer(tensor, core, down, loss, local):
+    half = down[0].shape[0]
+    cut = local // 4
+
+    def kernel(t_ref, own_ref, other_ref, loss_ref, out, low, sem):
+        lanes = pl.ds(pl.multiple_of(t_ref[0] * local, local), local)
+        move = pltpu.make_async_copy(loss_ref.at[:, lanes], low, sem)
+        move.start()
+        move.wait()
+        mine = pl.ds(pl.multiple_of(t_ref[1] * half, half), half)
+        theirs = pl.ds(pl.multiple_of((1 - t_ref[1]) * half, half), half)
+        term = dot_tn(own_ref[...], low[mine, :]) + dot_tn(other_ref[...], low[theirs, :])
+        for g in range(4):
+            out[g] = term[:PAIR, g * cut : (g + 1) * cut].astype(bf16)
+
+    whole = pl.BlockSpec(memory_space=pltpu.VMEM)
+    return pl.pallas_call(
+        kernel,
+        grid_spec=pltpu.PrefetchScalarGridSpec(
+            num_scalar_prefetch=1,
+            grid=(),
+            in_specs=[whole] * 2 + [pl.BlockSpec(memory_space=pltpu.HBM)],
+            out_specs=whole,
+            scratch_shapes=[pltpu.VMEM((2 * half, local), bf16), pltpu.SemaphoreType.DMA],
+        ),
+        out_shape=jax.ShapeDtypeStruct((4, PAIR, cut), bf16),
+        compiler_params=pltpu.CompilerParams(vmem_limit_bytes=4 << 20),
+        cost_estimate=HINT,
+        name="pack_layer",
+    )(jnp.stack([tensor, core]), *down, loss)
 
 
 def pack_projections(tensor, grad_down, normed_wide, grad_qkv, local):
@@ -475,41 +598,40 @@
             num_scalar_prefetch=1, grid=(), in_specs=[whole] * 3, out_specs=whole
         ),
         out_shape=jax.ShapeDtypeStruct((4, 6 * PAIR, cut), bf16),
-        compiler_params=pltpu.CompilerParams(vmem_limit_bytes=24 << 20),
+        compiler_params=pltpu.CompilerParams(vmem_limit_bytes=4 << 20),
         cost_estimate=HINT,
         name="pack_projections",
     )(tensor, grad_down, normed_wide, grad_qkv)
 
 
 def unpack_terms(context, owner, near, cross, tiles):
-    cut = near.shape[2]
+    cut = near[0].shape[2]
     half = cut // 2
-    base = (4 + 2 * tiles) * PAIR
-
-    def kernel(c_ref, owner_ref, near_ref, cross_ref, a_attn, b_attn, a_up, b_up, a_down, b_down):
+
+    def kernel(c_ref, owner_ref, n0, n1, c0, c1, a_attn, b_attn, a_up, b_up, a_down, b_down):
         first = c_ref[0] == 0
 
         for k in range(4):
             for s in range(SLOTS):
                 who = owner_ref[k * SLOTS + s]
 
-                def value(row):
+                def value(row, n_ref=n0, c_ref=c0):
                     rows = slice(row + s * RANK, row + (s + 1) * RANK)
-                    return near_ref[k, rows, :].astype(f32) + cross_ref[k, rows, :].astype(f32)
-
-                def narrow(row):
-                    v = value(row)
+                    return n_ref[k, rows, :].astype(f32) + c_ref[k, rows, :].astype(f32)
+
+                def narrow(row, *refs):
+                    v = value(row, *refs)
                     return jnp.where(first, v[:, :half], v[:, half:])
 
                 for i in range(3):
-                    a_attn[i, pl.ds(who, 1)] = narrow(base + i * PAIR)[None]
-                    b_attn[i, pl.ds(who, 1)] = narrow(base + (3 + i) * PAIR)[None]
+                    a_attn[i, pl.ds(who, 1)] = narrow(i * PAIR, n1, c1)[None]
+                    b_attn[i, pl.ds(who, 1)] = narrow((3 + i) * PAIR, n1, c1)[None]
                 a_attn[3, pl.ds(who, 1)] = narrow(0)[None]
                 b_attn[3, pl.ds(who, 1)] = narrow(PAIR)[None]
                 a_up[pl.ds(who, 1)] = narrow(2 * PAIR)[None]
-                b_down[pl.ds(who, 1)] = narrow(3 * PAIR)[None]
+                b_down[pl.ds(who, 1)] = narrow(6 * PAIR, n1, c1)[None]
                 for n, ref in enumerate((b_up, a_down)):
-                    start = (4 + n * tiles) * PAIR
+                    start = (3 + n * tiles) * PAIR
                     for t in range(tiles // 2):
                         ref[pl.ds(who, 1), :, t * cut : (t + 1) * cut] = jnp.where(
                             first,
@@ -524,13 +646,13 @@
     return pl.pallas_call(
         kernel,
         grid_spec=pltpu.PrefetchScalarGridSpec(
-            num_scalar_prefetch=2, grid=(), in_specs=[whole] * 2, out_specs=[whole] * 6
+            num_scalar_prefetch=2, grid=(), in_specs=[whole] * 4, out_specs=[whole] * 6
         ),
         out_shape=[jax.ShapeDtypeStruct(shape, f32) for shape in shapes],
-        compiler_params=pltpu.CompilerParams(vmem_limit_bytes=24 << 20),
+        compiler_params=pltpu.CompilerParams(vmem_limit_bytes=4 << 20),
         cost_estimate=HINT,
         name="unpack_terms",
-    )(context, owner, near, cross)
+    )(context, owner, *near, *cross)
 
 
 def unpack_plain(context, owner, total, tiles, ctx_size):
@@ -548,14 +670,14 @@
         joined = jnp.transpose(items, (1, 2, 0, 3)).reshape(ADAPTERS, RANK, -1)
         return narrow(joined)
 
-    base = 4 + 2 * tiles
+    base = 3 + 2 * tiles
     return (
         narrow(jnp.concatenate([placed[base : base + 3], placed[:1]])),
         narrow(jnp.concatenate([placed[base + 3 : base + 6], placed[1:2]])),
         narrow(placed[2]),
-        broad(placed[4 : 4 + tiles]),
-        broad(placed[4 + tiles : 4 + 2 * tiles]),
-        narrow(placed[3]),
+        broad(placed[3 : 3 + tiles]),
+        broad(placed[3 + tiles : base]),
+        narrow(placed[base + 6]),
     )
 
 
@@ -589,7 +711,7 @@
         ],
         out_specs=pl.BlockSpec((tokens, local), lambda n: (0, n)),
         out_shape=jax.ShapeDtypeStruct((tokens, blocks * local), bf16),
-        compiler_params=pltpu.CompilerParams(vmem_limit_bytes=40 << 20),
+        compiler_params=pltpu.CompilerParams(vmem_limit_bytes=12 << 20),
         cost_estimate=HINT,
         name="project",
     )(*rows, bias, weight)
@@ -624,7 +746,7 @@
         ],
         out_specs=[block, block],
         out_shape=[shape, shape],
-        compiler_params=pltpu.CompilerParams(vmem_limit_bytes=40 << 20),
+        compiler_params=pltpu.CompilerParams(vmem_limit_bytes=14 << 20),
         cost_estimate=HINT,
         name="expand",
     )(own, other, weight, bias)
@@ -650,10 +772,30 @@
         ],
         out_specs=block,
         out_shape=jax.ShapeDtypeStruct((tokens, hidden), bf16),
-        compiler_params=pltpu.CompilerParams(vmem_limit_bytes=40 << 20),
+        compiler_params=pltpu.CompilerParams(vmem_limit_bytes=14 << 20),
         cost_estimate=HINT,
         name="back_hidden",
     )(loss, weight, slope)
+
+
+class Direct:
+    def __init__(self, own, half_axis, context):
+        size = own.shape[half_axis] // 2
+        self.own = own
+        self.part = lax.dynamic_slice_in_dim(own, context * size, size, half_axis)
+
+    def first(self, *waits):
+        part = gate(self.part, *waits)
+        self.near = [
+            lax.ppermute(part, "fsdp", [(i, i ^ k) for i in range(4)]) for k in range(1, 4)
+        ]
+
+    def second(self, *waits):
+        *self.near, _ = lax.optimization_barrier((*self.near, waits))
+        self.far = [lax.ppermute(piece, "ctx", SWAP_Y) for piece in self.near]
+
+    def pieces(self):
+        return (self.own, *[p for pair in zip(self.near, self.far) for p in pair])
 
 
 class Ring:
@@ -669,22 +811,24 @@
         self.across = lax.ppermute(part, "fsdp", [(1, 2), (2, 1)])
 
     def second(self, *waits):
-        self.one, across, *_ = lax.optimization_barrier((self.one, self.across, *waits))
+        self.one, self.across, *_ = lax.optimization_barrier((self.one, self.across, *waits))
         self.y_one = lax.ppermute(self.one, "ctx", SWAP_Y)
-        outward = lax.ppermute(across, "fsdp", [(1, 0), (2, 3)])
+        self.outward = lax.ppermute(self.across, "fsdp", [(1, 0), (2, 3)])
         self.back = lax.ppermute(self.one, "fsdp", [(1, 2), (2, 1)])
+
+    def third(self, *waits):
+        outward, self.back, self.y_one, across, *_ = lax.optimization_barrier(
+            (self.outward, self.back, self.y_one, self.across, *waits)
+        )
         self.two = jnp.where(self.inner, across, outward)
-
-    def third(self, *waits):
-        self.two, back, self.y_one, *_ = lax.optimization_barrier(
-            (self.two, self.back, self.y_one, *waits)
-        )
         self.y_two = lax.ppermute(self.two, "ctx", SWAP_Y)
-        outward = lax.ppermute(back, "fsdp", [(1, 0), (2, 3)])
-        self.three = jnp.where(self.inner, back, outward)
+        self.last = lax.ppermute(self.back, "fsdp", [(1, 0), (2, 3)])
 
     def fourth(self, *waits):
-        self.three, self.y_two, *_ = lax.optimization_barrier((self.three, self.y_two, *waits))
+        last, self.y_two, back, *_ = lax.optimization_barrier(
+            (self.last, self.y_two, self.back, *waits)
+        )
+        self.three = jnp.where(self.inner, back, last)
         self.y_three = lax.ppermute(self.three, "ctx", SWAP_Y)
 
     def pieces(self):
@@ -699,30 +843,38 @@
         )
 
 
-def matmul(rows, half, weight, cut, dtype, flipped, count=None):
+def matmul(rows, half, weight, cut, flipped, parts=1):
     summed = rows.shape[1]
     steps = summed // cut
-    wide = count or (weight.shape[0] if flipped else weight.shape[1])
-    size = rows.shape[0] // 2 if half is not None else rows.shape[0]
-
-    def kernel(half_ref, x_ref, w_ref, out_ref, *acc):
+    wide = weight.shape[0] if flipped else weight.shape[1]
+    size = rows.shape[0] // 2
+    piece = size // parts
+
+    def kernel(half_ref, x_ref, w_ref, *refs):
+        outs = refs[:parts]
         part = dot_nt(x_ref[...], w_ref[...]) if flipped else dot_nn(x_ref[...], w_ref[...])
+
+        def finish(total):
+            for i, out_ref in enumerate(outs):
+                out_ref[...] = total[i * piece : (i + 1) * piece].astype(bf16)
+
         if steps == 1:
-            out_ref[...] = part.astype(dtype)
+            finish(part)
             return
+        acc = refs[parts]
         step = pl.program_id(0)
 
         @pl.when(step == 0)
         def _():
-            acc[0][...] = part
+            acc[...] = part
 
         @pl.when((step > 0) & (step < steps - 1))
         def _():
-            acc[0][...] += part
+            acc[...] += part
 
         @pl.when(step == steps - 1)
         def _():
-            out_ref[...] = (acc[0][...] + part).astype(dtype)
+            finish(acc[...] + part)
 
     if flipped:
         w_spec = pl.BlockSpec((wide, cut), lambda k, h: (0, k))
@@ -734,14 +886,14 @@
             num_scalar_prefetch=1,
             grid=(steps,),
             in_specs=[pl.BlockSpec((size, cut), lambda k, h: (h[0], k)), w_spec],
-            out_specs=pl.BlockSpec((size, wide), lambda k, h: (0, 0)),
+            out_specs=[pl.BlockSpec((piece, wide), lambda k, h: (0, 0))] * parts,
             scratch_shapes=[pltpu.VMEM((size, wide), f32)] if steps > 1 else [],
         ),
-        out_shape=jax.ShapeDtypeStruct((size, wide), dtype),
-        compiler_params=pltpu.CompilerParams(vmem_limit_bytes=48 << 20),
+        out_shape=[jax.ShapeDtypeStruct((piece, wide), bf16)] * parts,
+        compiler_params=pltpu.CompilerParams(vmem_limit_bytes=22 << 20),
         cost_estimate=HINT,
         name="matmul",
-    )(jnp.zeros((1,), jnp.int32) if half is None else half, rows, weight)
+    )(half, rows, weight)
 
 
 def back_attend(core, own, other, weight):
@@ -762,7 +914,7 @@
             num_scalar_prefetch=1, grid=(), in_specs=[whole] * 3, out_specs=whole
         ),
         out_shape=jax.ShapeDtypeStruct((2 * size, local), bf16),
-        compiler_params=pltpu.CompilerParams(vmem_limit_bytes=32 << 20),
+        compiler_params=pltpu.CompilerParams(vmem_limit_bytes=6 << 20),
         cost_estimate=HINT,
         name="back_attend",
     )(core, own, other, weight)
@@ -835,10 +987,9 @@
         swap_y = [(0, 1), (1, 0)]
         spot = jnp.stack([group, context]).astype(jnp.int32)
 
-        def send_tp(other_low, own_low):
-            got = on(other_low, "tp", CORE_SWAP)
-            mine = round_low(own_low.astype(f32) + got.astype(f32))
-            return mine, on(mine, "tp", X_SWAP)
+        def send_tp(others, own_low, *waits):
+            mine = join(own_low, [on(other, "tp", CORE_SWAP) for other in others])
+            return mine, on(gate(mine, *waits), "tp", X_SWAP)
 
         def sum_sent(sent, waits=()):
             mine, far = sent
@@ -904,9 +1055,9 @@
         def widen(low, tail):
             return jnp.concatenate([low, tail], axis=1)
 
-        normed_wide = norm_wide(
-            [inputs], jnp.arange(4, dtype=jnp.int32), slots, a_qkv_rows, gain_one, shift_one, tokens
-        )
+        def own_norm(places):
+            return norm_wide([inputs], places, slots, a_qkv_rows, gain_one, shift_one, tokens)
+
         q_aug = jnp.concatenate(
             [jnp.pad(b_qkv_rows[i], ((0, 0), (i * local, (2 - i) * local))) for i in range(3)]
             + [jnp.zeros((AUG - 3 * PAIR, 3 * local), bf16)],
@@ -923,23 +1074,22 @@
             far_places = jnp.stack([tensor, tensor ^ 2, tensor ^ 1, tensor ^ 3]).astype(jnp.int32)
             inner = (group == 1) | (group == 2)
             q_ring = Ring(w_qkv, 1, context, inner)
-            o_ring = Ring(w_o, 0, context, inner)
+            o_ring = Direct(w_o, 0, context)
             in_ring = Ring(w_in, 0, context, inner)
             out_ring = Ring(w_out, 0, context, inner)
             q_ring.first()
             q_ring.second()
             q_ring.third(far_quarter)
+            normed_wide = own_norm(gate(jnp.arange(4, dtype=jnp.int32), q_ring.y_one))
             far_quarter, _ = lax.optimization_barrier((far_quarter, q_ring.two))
             far_x = on(far_quarter, "tp", X_SWAP)
             far_core = on(far_quarter, "tp", CORE_SWAP)
-            o_ring.first(q_ring.two)
             far_x, far_core, normed_wide, _ = lax.optimization_barrier(
-                (far_x, far_core, normed_wide, q_ring.three)
-            )
-            q_ring.fourth(normed_wide, o_ring.one, o_ring.across)
+                (far_x, far_core, normed_wide, q_ring.last)
+            )
+            q_ring.fourth(normed_wide)
+            o_ring.first(q_ring.last)
             far_both = on(far_x, "tp", CORE_SWAP)
-            o_ring.second(q_ring.three)
-            in_ring.first(o_ring.two, o_ring.back)
             far_wide = norm_wide(
                 [far_quarter, far_x, far_core, far_both],
                 far_places,
@@ -949,9 +1099,10 @@
                 shift_one,
                 tokens,
             )
-            o_ring.third(far_wide, q_ring.y_three)
+            o_ring.second(q_ring.y_three, far_wide)
+            in_ring.first(*o_ring.near)
             q_full = assemble(
-                gate(spot, o_ring.two, far_wide),
+                gate(spot, *o_ring.near, far_wide),
                 q_ring.pieces(),
                 q_aug,
                 wide,
@@ -960,6 +1111,7 @@
                 3,
             )
         else:
+            normed_wide = own_norm(jnp.arange(4, dtype=jnp.int32))
             own_q = jnp.transpose(w_qkv, (1, 0, 2)).reshape(shard, 3 * local)
             q_full = jnp.concatenate([lax.all_gather(own_q, "fsdp", axis=0, tiled=True), q_aug], 0)
             o_full = jnp.concatenate([lax.all_gather(w_o, "fsdp", axis=1, tiled=True), o_aug], 1)
@@ -975,11 +1127,8 @@
             qkv = project(normed_wide, far_wide, q_full, q_bias, local)
             far_kv = qkv
             far_base = 3 * heads
-            qkv, _, _, _ = lax.optimization_barrier(
-                (qkv, in_ring.one, in_ring.across, o_ring.three)
-            )
+            qkv, *_ = lax.optimization_barrier((qkv, in_ring.one, in_ring.across, *o_ring.far))
             in_ring.second(qkv)
-            o_ring.fourth(qkv)
             far_kv = qkv
         else:
             qkv = project(normed_wide, None, q_full, q_bias, local)
@@ -990,26 +1139,27 @@
             qkv, far_kv, far_base, far_bias, own_bias, heads, scale
         )
         if pair_ctx:
+            in_ring.third(attended)
             o_full = assemble(
-                gate(spot, attended, in_ring.two, in_ring.back),
+                gate(spot, attended),
                 o_ring.pieces(),
                 o_aug,
                 local,
                 wide,
                 ("columns", shard, local // 2),
                 0,
+                True,
             )
         core_id = core.astype(jnp.int32)[None]
         other_id = 1 - core_id
         branch_sent = send_tp(
-            matmul(attended, other_id, o_full, local, bf16, False),
-            matmul(attended, core_id, o_full, local, bf16, False),
+            matmul(attended, other_id, o_full, local, False),
+            matmul(attended, core_id, o_full, local, False)[0],
         )
         branch_far = branch_sent[1]
         if pair_ctx:
-            in_ring.third()
-            in_ring.fourth()
-            out_ring.first(in_ring.three)
+            in_ring.fourth(branch_sent[0])
+            out_ring.first(in_ring.last, branch_sent[0])
             branch_far = gate(branch_far, in_ring.y_three, out_ring.one, out_ring.across)
         middle, two_own = row_call(
             after_attention,
@@ -1026,7 +1176,7 @@
         if pair_ctx:
             out_ring.second(in_ring.y_three)
             in_full = assemble(
-                gate(spot, out_ring.two, out_ring.back),
+                gate(spot, out_ring.outward, out_ring.back),
                 in_ring.pieces(),
                 in_aug,
                 wide,
@@ -1058,13 +1208,14 @@
         second_id = first_id + 1
         ff_cut = hidden_local // 2
         two_sent = send_tp(
-            matmul(grad_pre, second_id, in_full, ff_cut, bf16, True),
-            matmul(grad_pre, first_id, in_full, ff_cut, bf16, True),
+            matmul(grad_pre, second_id, in_full, ff_cut, True),
+            matmul(grad_pre, first_id, in_full, ff_cut, True)[0],
         )
         late_hidden = gate(hidden, two_sent[0])
         exit_sent = send_tp(
-            matmul(late_hidden, second_id, out_full, ff_cut, bf16, False),
-            matmul(late_hidden, first_id, out_full, ff_cut, bf16, False),
+            matmul(late_hidden, second_id, out_full, ff_cut, False, 2),
+            matmul(late_hidden, first_id, out_full, ff_cut, False)[0],
+            two_sent[1],
         )
         grad_middle, back_own = row_call(
             back_middle,
@@ -1084,47 +1235,56 @@
         back_other = on(back_own, "tp", CORE_SWAP)
         grad_attended = back_attend(core_id, back_own, back_other, o_full)
 
-        grad_q, grad_k, grad_v, far_grad_k, far_grad_v = attend_backward(
+        grad_q, grad_k, grad_v, far_grads = attend_backward(
             qkv, far_kv, far_base, grad_attended, attended_f, probs_far, probs_own, heads, scale
         )
         if pair_ctx:
-            more_k = on(far_grad_k, "ctx", [(1, 0)])
-            more_v = on(far_grad_v, "ctx", [(1, 0)])
+            more = on(far_grads, "ctx", [(1, 0)])
         else:
-            more_k = lax.psum_scatter(far_grad_k, "ctx", scatter_dimension=0, tiled=True)
-            more_v = lax.psum_scatter(far_grad_v, "ctx", scatter_dimension=0, tiled=True)
-        (layer_wide,) = row_call(
+            more = lax.psum_scatter(far_grads, "ctx", scatter_dimension=1, tiled=True)
+        layer_own, down_own = row_call(
             after_hidden,
             "after_hidden",
             core_id,
             slots,
             half,
-            [(exit_sent[0], False), (gate(exit_sent[1], more_v), False), (middle, False)],
+            [(exit_sent[0], False), (exit_sent[1], False), (middle, False)],
             [exit_offsets[1:], b_down_rows],
-            [(wide, bf16)],
-        )
-        layer_other = on(layer_wide, "tp", CORE_SWAP)
-        layer_out = natural(layer_wide[:, :width], layer_other[:, :width])
-        where = jnp.stack([tensor, core]).astype(jnp.int32)
+            [(width, bf16), (AUG, bf16)],
+        )
+        down_other = on(down_own, "tp", CORE_SWAP)
         tiles = hidden_local // local
+
+        def to_owners(slabs):
+            pieces = [
+                lax.dynamic_index_in_dim(slabs, group ^ k, 0, keepdims=False) for k in range(4)
+            ]
+            return jnp.stack(
+                pieces[:1]
+                + [on(pieces[k], "fsdp", [(i, i ^ k) for i in range(4)]) for k in range(1, 4)]
+            )
+
+        tensor_id, core_at = tensor.astype(jnp.int32), core.astype(jnp.int32)
         packed = pack_terms(
-            where,
+            tensor_id,
+            core_at,
             (two_own, two_other),
             (back_own, back_other),
             attended,
             grad_pre,
             hidden,
             grad_down_down,
-            (layer_wide[:, width:], layer_other[:, width:]),
-            loss_sensitivity,
             local,
         )
-        more_k = gate(more_k, packed, layer_out)
+        packed_layer = pack_layer(
+            tensor_id, core_at, (down_own, down_other), loss_sensitivity, local
+        )
+        grad_k = gate(grad_k, packed, packed_layer)
         grad_qkv = jnp.concatenate(
             [
                 grad_q,
-                (grad_k.astype(f32) + more_k.astype(f32)).astype(bf16),
-                (grad_v.astype(f32) + more_v.astype(f32)).astype(bf16),
+                (grad_k.astype(f32) + more[0].astype(f32)).astype(bf16),
+                (grad_v.astype(f32) + more[1].astype(f32)).astype(bf16),
             ],
             axis=1,
         )
@@ -1134,36 +1294,36 @@
         low_far = on(low_pair, "tp", X_SWAP)
         low_sum = low_pair.astype(f32) + low_far.astype(f32)
         grad_down_qkv = (factor * low_sum * picks(0, tokens)).astype(bf16)
-        qkv_cut = 3 * local // 2
-        one_sent = send_tp(
-            matmul(grad_qkv, other_id, q_full, qkv_cut, bf16, True, width),
-            matmul(grad_qkv, core_id, q_full, qkv_cut, bf16, True, width),
-        )
-        tensor_id = tensor.astype(jnp.int32)[None]
-        packed_qkv = pack_projections(
-            gate(tensor_id, one_sent[0]), grad_down_qkv, normed_wide, grad_qkv, local
-        )
-        received = []
-        for k in range(4):
-            piece = jnp.concatenate(
+        one_other, one_own = back_project(
+            gate(grad_qkv, low_part), core_id, q_full, width
+        )
+        one_sent = send_tp([one_other], one_own, low_far)
+        layer_other = on(layer_own, "tp", CORE_SWAP)
+        layer_out = place_rows(core_id, layer_own, layer_other, width)
+        near = to_owners(packed)
+        near_qkv = to_owners(
+            jnp.concatenate(
                 [
-                    lax.dynamic_index_in_dim(packed, group ^ k, 0, keepdims=False),
-                    lax.dynamic_index_in_dim(packed_qkv, group ^ k, 0, keepdims=False),
+                    pack_projections(tensor_id[None], grad_down_qkv, normed_wide, grad_qkv, local),
+                    packed_layer,
                 ],
-                axis=0,
-            )
-            received.append(on(piece, "fsdp", [(i, i ^ k) for i in range(4)]) if k else piece)
-        near = jnp.stack(received)
+                axis=1,
+            )
+        )
         holder = jnp.stack([group ^ k for k in range(4)])
         owner = adapter_of.reshape(4, SLOTS)[holder].reshape(4 * SLOTS)
         if pair_ctx:
-            cross = on(near, "ctx", swap_y)
             adapter_grads = unpack_terms(
-                context.astype(jnp.int32)[None], owner, near, cross, tiles
+                context.astype(jnp.int32)[None],
+                owner,
+                (near, near_qkv),
+                (on(near, "ctx", swap_y), on(near_qkv, "ctx", swap_y)),
+                tiles,
             )
         else:
+            total = lax.psum((near.astype(f32), near_qkv.astype(f32)), "ctx")
             adapter_grads = unpack_plain(
-                context, owner, lax.psum(near.astype(f32), "ctx"), tiles, ctx_size
+                context, owner, jnp.concatenate(total, axis=1), tiles, ctx_size
             )
         (grad_own,) = row_call(
             back_first,
@@ -1173,7 +1333,7 @@
             half,
             [
                 (one_sent[0], False),
-                (gate(one_sent[1], adapter_grads[0]), False),
+                (gate(one_sent[1], adapter_grads[0], layer_out), False),
                 (grad_down_qkv, True),
                 (inputs, True),
                 (grad_middle, False),
@@ -1182,7 +1342,7 @@
             [(width, bf16)],
         )
         grad_other = on(grad_own, "tp", CORE_SWAP)
-        grad_inputs = natural(grad_own, grad_other)
+        grad_inputs = place_rows(core_id, grad_own, grad_other, width)
 
         out_a_attn, out_b_attn, out_a_up, out_b_up, out_a_down, out_b_down = adapter_grads
         return (

time: 549 us -> 498 us (0.907)
  other arithmetic: 38.7 us -> 21.7 us
  local copies, waits for them, and re-layouts: 68.4 us -> 54.9 us
  Pallas kernels: 151 us -> 140 us
    pallas_call x8 -> x6, Pallas kernels: 44.4 us -> 23.4 us  [matmul(): pl.pallas_call(kernel, grid_spec=pltpu.PrefetchScalarGridSpec(num_scalar_...]
    pallas_call x0 -> x8, Pallas kernels: none -> 16.9 us  [the longest x1 5.59 us: back_project(): pl.pallas_call(kernel, grid_spec=pltpu.PrefetchScalarGridSpec(num_scalar_...]
    unnamed x201 -> x181, local copies, waits for them, and re-layouts: 40.5 us -> 28.5 us
    convert_element_type x5 -> x1, other arithmetic: 9.71 us -> 0.05 us  [round_low(): return lax.reduce_precision(v, 8, 7).astype(bf16)]
    ppermute x8 -> x12, waiting for transfers between devices: 39.9 us -> 48.9 us  [the longest x3 20.6 us: third(): self.last = lax.ppermute(self.back, 'fsdp', [(1, 0), (2, 3)])]
    ppermute x4 -> x3, waiting for transfers between devices: 9.32 us -> 0.73 us  [second(): self.y_one = lax.ppermute(self.one, 'ctx', SWAP_Y)]
    ppermute x4 -> x3, waiting for transfers between devices: 14.8 us -> 7.41 us  [fourth(): self.y_three = lax.ppermute(self.three, 'ctx', SWAP_Y)]
    ppermute x24 -> x29, waiting for transfers between devices: 88.8 us -> 95.7 us  [on(): return lax.ppermute(value, axis, pairs)]
  transfers between devices with their start and end apart: 56 -> 59, of which waited for: 31 -> 29; matrix products, arithmetic and copies ran while one was open for 12% -> 9% of each run, Pallas kernels for 19% -> 22%
where the time goes in v4:
time: 498 us; the launch traced here: 490 us
  waiting for transfers between devices  186 us (37%)
  Pallas kernels  140 us (28%)
  starting transfers between devices  79.8 us (16%)
  local copies, waits for them, and re-layouts  54.9 us (11%)
  other arithmetic  21.7 us (4%)
  between operations  6.52 us (1%)
    ppermute x29, waiting for transfers between devices, on(): return lax.ppermute(value, axis, pairs)  95.7 us
    ppermute x29, starting transfers between devices, on(): return lax.ppermute(value, axis, pairs)  32 us
    unnamed x181, local copies, waits for them, and re-layouts  28.5 us
    pallas_call x6, Pallas kernels, matmul(): pl.pallas_call(kernel, grid_spec=pltpu.PrefetchScalarGridSpec(num_scalar_...  23.4 us
    ppermute x3, waiting for transfers between devices, third(): self.last = lax.ppermute(self.back, 'fsdp', [(1, 0), (2, 3)])  20.6 us
    pallas_call x4, Pallas kernels, row_call(): pl.pallas_call(kernel, grid_spec=pltpu.PrefetchScalarGridSpec(num_scalar_...  17.7 us
    ppermute x3, waiting for transfers between devices, first(): lax.ppermute(part, 'fsdp', [(i, i ^ k) for i in range(4)])  15.9 us
    ppermute x3, waiting for transfers between devices, first(): self.one = lax.ppermute(part, 'fsdp', [(0, 1), (1, 0), (2, 3), (3, 2)])  13.9 us
  transfers between devices with their start and end apart: 59, of which 29 were waited for; matrix products, arithmetic and copies ran while one was open for 9% of the time, Pallas kernels for 22%

profile of v4, /device:TPU:9, one launch (start us, length us, event | category | flops | bytes accessed | tf_op | source)
XLA Modules:
  0.0 490.1 jit_solution(18339461960733721665)
XLA Ops:
  31.1 12.9 %collective-permute-done.4 = bf16[3,256,512]{2,1,0:T(8,128)(2,1)S(1)} collective-permute-done((bf16[3,256,512]{2,1,0:T(8,128)(2,1)}, bf16[3,256,512]{2,1,0:T(8,128)(2,1)S(1)}, u32[]{:S(2)}, u32[]{:S(2)}) %collective-permute-start.4) | collective-permute-done | bytes 786464 | tf_op jit(solution)/shard_map/ppermute | solution.py:817
  62.6 8.1 %collective-permute-done.8 = bf16[3,256,512]{2,1,0:T(8,128)(2,1)S(1)} collective-permute-done((bf16[3,256,512]{2,1,0:T(8,128)(2,1)S(1)}, bf16[3,256,512]{2,1,0:T(8,128)(2,1)S(1)}, u32[]{:S(2)}, u32[]{:S(2)}) %collective-permute-start.8) | collective-permute-done | bytes 786464 | tf_op jit(solution)/shard_map/ppermute | solution.py:825
  78.3 4.8 norm_wide.3.refs_1_
  88.4 12.2 %collective-permute-done.12.refs_5_ = bf16[256,512]{1,0:T(8,128)(2,1)} collective-permute-done((bf16[256,512]{1,0:T(8,128)(2,1)S(1)}, bf16[256,512]{1,0:T(8,128)(2,1)}, u32[]{:S(2)}, u32[]{:S(2)}) %collective-permute-start.12) | collective-permute-done | bytes 262176 | tf_op jit(solution)/shard_map/ppermute | solution.py:790
  115.9 11.0 %project.1.q_ref.k_ref.v_ref.fk_ref.fv_ref = bf16[768,2560]{1,0:T(8,128)(2,1)S(1)} custom-call(bf16[768,2176]{1,0:T(8,128)(2,1)S(1)} %copy-done.9, bf16[768,2176]{1,0:T(8,128)(2,1)S(1)} %copy-done.17, f32[1,1536]{1,0:T(1,128)S(1)} %broadcast_in_dim.114.refs_2_, bf16[2176,1536]{1,0:T(8,128)(2,1)S(1)} %copy-done.4), custom_call_target="tpu_custom_call" | custom-call | flops 1 | bytes 1 | tf_op jit(solution)/shard_map/project/pallas_call | solution.py:704
  138.9 10.8 %attend_forward.1 = (f32[768,512]{1,0:T(8,128)S(1)}, bf16[768,512]{1,0:T(8,128)(2,1)S(1)}, bf16[4,768,768]{2,1,0:T(8,128)(2,1)S(1)}, bf16[4,768,768]{2,1,0:T(8,128)(2,1)S(1)}) custom-call(bf16[768,2560]{1,0:T(8,128)(2,1)S(1)} %copy-done.1, bf16[768,2560]{1,0:T(8,128)(2,1)S(1)} %copy-done.1, bf16[768,2560]{1,0:T(8,128)(2,1)S(1)} %copy-done.1, ...), custom_call_target="tpu_custom_call" | custom-call | flops 1 | bytes 1 | tf_op jit(solution)/shard_map/attend_forward/pallas_call | solution.py:106
  172.2 12.5 %collective-permute-done.25 = bf16[256,2048]{1,0:T(8,128)(2,1)} collective-permute-done((bf16[256,2048]{1,0:T(8,128)(2,1)}, bf16[256,2048]{1,0:T(8,128)(2,1)}, u32[]{:S(2)}, u32[]{:S(2)}) %collective-permute-start.25) | collective-permute-done | bytes 1048608 | tf_op jit(solution)/shard_map/ppermute | solution.py:825
  195.7 13.9 %collective-permute-done.28.refs_1_ = bf16[1024,512]{1,0:T(8,128)(2,1)} collective-permute-done((bf16[1024,512]{1,0:T(8,128)(2,1)}, bf16[1024,512]{1,0:T(8,128)(2,1)}, u32[]{:S(2)}, u32[]{:S(2)}) %collective-permute-start.28) | collective-permute-done | bytes 1048608 | tf_op jit(solution)/shard_map/ppermute | solution.py:810
  227.3 12.1 %collective-permute-done.31 = bf16[1024,512]{1,0:T(8,128)(2,1)} collective-permute-done((bf16[1024,512]{1,0:T(8,128)(2,1)}, bf16[1024,512]{1,0:T(8,128)(2,1)}, u32[]{:S(2)}, u32[]{:S(2)}) %collective-permute-start.31) | collective-permute-done | bytes 1048608 | tf_op jit(solution)/shard_map/ppermute | solution.py:816
  243.0 5.1 %collective-permute-start.34 = (bf16[1024,512]{1,0:T(8,128)(2,1)}, bf16[1024,512]{1,0:T(8,128)(2,1)}, u32[]{:S(2)}, u32[]{:S(2)}) collective-permute-start(bf16[1024,512]{1,0:T(8,128)(2,1)} %collective-permute-done.32), channel_id=1, source_target_pairs={{8,0},{16,24},{9,1},{17,25},{10,2},{18,26},{11,3},{19,27},{12,4},{... | collective-permute-start | bytes 3145736 | tf_op jit(solution)/shard_map/ppermute | solution.py:825
  250.2 7.9 %collective-permute-done.21.refs_1_ = bf16[384,2176]{1,0:T(8,128)(2,1)} collective-permute-done((bf16[384,2176]{1,0:T(8,128)(2,1)}, bf16[384,2176]{1,0:T(8,128)(2,1)}, u32[]{:S(2)}, u32[]{:S(2)}) %collective-permute-start.21) | collective-permute-done | bytes 1671200 | tf_op jit(solution)/shard_map/ppermute | solution.py:968
  258.8 6.0 %after_attention.1 = (f32[384,2048]{1,0:T(8,128)S(1)}, bf16[384,2176]{1,0:T(8,128)(2,1)}) custom-call(s32[1]{0:T(128)} %bitcast.half_ref.core_ref, s32[3]{0:T(128)S(1)} %copy-done.50, bf16[384,2176]{1,0:T(8,128)(2,1)S(1)} %copy-done.23, bf16[384,2176]{1,0:T(8,128)(2,1)} %collective-permute-done.21.refs_1_, bf16[768,2048]{1,0:T(8,128)(2,1)S(1)} %copy-done.6, ...), custom_call_target="tpu_custom_call" | custom-call | flops 1 | bytes 1 | tf_op jit(solution)/shard_map/after_attention/pallas_call | solution.py:349
  285.0 12.1 %expand.1 = (bf16[768,2048]{1,0:T(8,128)(2,1)S(1)}, bf16[768,2048]{1,0:T(8,128)(2,1)S(1)}) custom-call(bf16[384,2176]{1,0:T(8,128)(2,1)} %get-tuple-element.117.own_ref.two_a, bf16[384,2176]{1,0:T(8,128)(2,1)} %collective-permute-done.30.other_ref.two_b, bf16[2176,2048]{1,0:T(8,128)(2,1)S(1)} %assemble.6.w_ref, f32[1,2048]{1,0:T(1,128)S(1)} %bitcast.82), custom_call_target="tpu_custom_call" | custom-call | flops 1 | bytes 1 | tf_op jit(solution)/shard_map/expand/pallas_call | solution.py:738
  306.3 8.6 %back_hidden.1.x_ref.gp_ref = bf16[768,2048]{1,0:T(8,128)(2,1)S(1)} custom-call(bf16[768,2176]{1,0:T(8,128)(2,1)S(1)} %pad_maximum_fusion.x_ref, bf16[2048,2176]{1,0:T(8,128)(2,1)S(1)} %assemble.7.w_ref, bf16[768,2048]{1,0:T(8,128)(2,1)S(1)} %get-tuple-element.132.s_ref), custom_call_target="tpu_custom_call" | custom-call | flops 1 | bytes 1 | tf_op jit(solution)/shard_map/back_hidden/pallas_call | solution.py:765
  314.9 5.3 %matmul.9 = bf16[384,2176]{1,0:T(8,128)(2,1)S(1)} custom-call(s32[1]{0:T(128)} %constant.159.clone.1.half_ref, bf16[768,2048]{1,0:T(8,128)(2,1)S(1)} %back_hidden.1.x_ref.gp_ref, bf16[2176,2048]{1,0:T(8,128)(2,1)S(1)} %assemble.6.w_ref), custom_call_target="tpu_custom_call" | custom-call | flops 1 | bytes 1 | tf_op jit(solution)/shard_map/matmul/pallas_call | solution.py:883
  321.0 5.5 %matmul.8.a_ref = bf16[384,2176]{1,0:T(8,128)(2,1)S(1)} custom-call(s32[1]{0:T(128)} %constant.146.clone.1.half_ref, bf16[768,2048]{1,0:T(8,128)(2,1)S(1)} %back_hidden.1.x_ref.gp_ref, bf16[2176,2048]{1,0:T(8,128)(2,1)S(1)} %assemble.6.w_ref), custom_call_target="tpu_custom_call" | custom-call | flops 1 | bytes 1 | tf_op jit(solution)/shard_map/matmul/pallas_call | solution.py:883
  327.5 4.6 matmul.11
  338.1 27.2 %collective-permute-done.40.refs_1_ = bf16[384,2176]{1,0:T(8,128)(2,1)S(1)} collective-permute-done((bf16[384,2176]{1,0:T(8,128)(2,1)S(1)}, bf16[384,2176]{1,0:T(8,128)(2,1)S(1)}, u32[]{:S(2)}, u32[]{:S(2)}) %collective-permute-start.40) | collective-permute-done | bytes 1671200 | tf_op jit(solution)/shard_map/ppermute | solution.py:968
  375.5 11.4 %attend_backward.1 = (bf16[768,512]{1,0:T(8,128)(2,1)S(1)}, bf16[768,512]{1,0:T(8,128)(2,1)S(1)}, bf16[768,512]{1,0:T(8,128)(2,1)S(1)}, bf16[2,768,512]{2,1,0:T(8,128)(2,1)S(1)}) custom-call(bf16[768,2560]{1,0:T(8,128)(2,1)S(1)} %copy-done.2, bf16[768,2560]{1,0:T(8,128)(2,1)S(1)} %copy-done.2, bf16[768,2560]{1,0:T(8,128)(2,1)S(1)} %copy-done.2, ...), custom_call_target="tpu_custom_call" | custom-call | flops 1 | bytes 1 | tf_op jit(solution)/shard_map/attend_backward/pallas_call | solution.py:181
  388.4 20.0 %collective-permute-done.41.refs_1_ = bf16[384,2176]{1,0:T(8,128)(2,1)S(1)} collective-permute-done((bf16[384,2176]{1,0:T(8,128)(2,1)S(1)}, bf16[384,2176]{1,0:T(8,128)(2,1)S(1)}, u32[]{:S(2)}, u32[]{:S(2)}) %collective-permute-start.41) | collective-permute-done | bytes 1671200 | tf_op jit(solution)/shard_map/ppermute | solution.py:968
  417.7 6.8 %collective-permute-done.45 = bf16[2,768,512]{2,1,0:T(8,128)(2,1)S(1)} collective-permute-done((bf16[2,768,512]{2,1,0:T(8,128)(2,1)S(1)}, bf16[2,768,512]{2,1,0:T(8,128)(2,1)S(1)}, u32[]{:S(2)}, u32[]{:S(2)}) %collective-permute-start.45) | collective-permute-done | bytes 1572896 | tf_op jit(solution)/shard_map/ppermute | solution.py:968
  425.9 5.6 %back_project.1 = (bf16[384,2048]{1,0:T(8,128)(2,1)S(1)}, bf16[384,2048]{1,0:T(8,128)(2,1)S(1)}) custom-call(s32[1]{0:T(128)} %bitcast.half_ref.core_ref, bf16[768,1536]{1,0:T(8,128)(2,1)S(1)} %pad_maximum_fusion.1.x_ref.gq_ref, bf16[2176,1536]{1,0:T(8,128)(2,1)S(1)} %bitcast.77), custom_call_target="tpu_custom_call" | custom-call | flops 1 | bytes 1 | tf_op jit(solution)/shard_map/back_project/pallas_call | solution.py:406
  470.4 7.7 %collective-permute-done.49.refs_1_ = bf16[384,2048]{1,0:T(8,128)(2,1)} collective-permute-done((bf16[384,2048]{1,0:T(8,128)(2,1)}, bf16[384,2048]{1,0:T(8,128)(2,1)}, u32[]{:S(2)}, u32[]{:S(2)}) %collective-permute-start.49) | collective-permute-done | bytes 1572896 | tf_op jit(solution)/shard_map/ppermute | solution.py:968
  478.1 4.7 back_first.1.own_ref
  (404 shorter events, 246.7 us)
Async XLA Ops:
  70.8 29.9 %collective-permute-start.14 = (bf16[3,256,512]{2,1,0:T(8,128)(2,1)S(1)}, bf16[3,256,512]{2,1,0:T(8,128)(2,1)S(1)}, u32[]{:S(2)}, u32[]{:S(2)}) collective-permute-start(bf16[3,256,512]{2,1,0:T(8,128)(2,1)S(1)} %broadcast_select_fusion.4.refs_5_), channel_id=1, source_target_pairs={{0,4},{4,0},{1,5},{5,1},{2,6},{6,2},{3,7},{7,3},{8,12},{12,8},{9,1... | collective-permute-start | bytes 2359304 | tf_op jit(solution)/shard_map/ppermute | solution.py:832
  76.0 24.6 %collective-permute-start.12 = (bf16[256,512]{1,0:T(8,128)(2,1)S(1)}, bf16[256,512]{1,0:T(8,128)(2,1)}, u32[]{:S(2)}, u32[]{:S(2)}) collective-permute-start(bf16[256,512]{1,0:T(8,128)(2,1)S(1)} %constant_dynamic-slice_fusion.9), channel_id=1, source_target_pairs={{0,24},{8,16},{16,8},{24,0},{1,25},{9,17},{17,9},{25,1},{2,26},{10... | collective-permute-start | bytes 786440 | tf_op jit(solution)/shard_map/ppermute | solution.py:790
  100.6 28.3 %collective-permute-start.15 = (bf16[256,2048]{1,0:T(8,128)(2,1)}, bf16[256,2048]{1,0:T(8,128)(2,1)}, u32[]{:S(2)}, u32[]{:S(2)}) collective-permute-start(bf16[256,2048]{1,0:T(8,128)(2,1)} %constant_dynamic-slice_fusion.6), channel_id=1, source_target_pairs={{0,8},{8,0},{16,24},{24,16},{1,9},{9,1},{17,25},{25,17},{2,10},{10... | collective-permute-start | bytes 3145736 | tf_op jit(solution)/shard_map/ppermute | solution.py:810
  100.6 28.3 %collective-permute-start.16 = (bf16[256,2048]{1,0:T(8,128)(2,1)}, bf16[256,2048]{1,0:T(8,128)(2,1)}, u32[]{:S(2)}, u32[]{:S(2)}) collective-permute-start(bf16[256,2048]{1,0:T(8,128)(2,1)} %constant_dynamic-slice_fusion.6), channel_id=1, source_target_pairs={{8,16},{16,8},{9,17},{17,9},{10,18},{18,10},{11,19},{19,11},{12,20... | collective-permute-start | bytes 3145736 | tf_op jit(solution)/shard_map/ppermute | solution.py:811
  104.0 24.9 %collective-permute-start.17 = (bf16[256,512]{1,0:T(8,128)(2,1)}, bf16[256,512]{1,0:T(8,128)(2,1)}, u32[]{:S(2)}, u32[]{:S(2)}) collective-permute-start(bf16[256,512]{1,0:T(8,128)(2,1)} %collective-permute-done.10.refs_1_), channel_id=1, source_target_pairs={{0,4},{4,0},{1,5},{5,1},{2,6},{6,2},{3,7},{7,3},{8,12},{12,8},{9,1... | collective-permute-start | bytes 786440 | tf_op jit(solution)/shard_map/ppermute | solution.py:795
  104.3 24.6 %collective-permute-start.18 = (bf16[256,512]{1,0:T(8,128)(2,1)}, bf16[256,512]{1,0:T(8,128)(2,1)}, u32[]{:S(2)}, u32[]{:S(2)}) collective-permute-start(bf16[256,512]{1,0:T(8,128)(2,1)} %collective-permute-done.11.refs_3_), channel_id=1, source_target_pairs={{0,4},{4,0},{1,5},{5,1},{2,6},{6,2},{3,7},{7,3},{8,12},{12,8},{9,1... | collective-permute-start | bytes 786440 | tf_op jit(solution)/shard_map/ppermute | solution.py:795
  128.9 31.9 %collective-permute-start.23 = (bf16[256,2048]{1,0:T(8,128)(2,1)}, bf16[256,2048]{1,0:T(8,128)(2,1)}, u32[]{:S(2)}, u32[]{:S(2)}) collective-permute-start(bf16[256,2048]{1,0:T(8,128)(2,1)} %collective-permute-done.15.refs_1_), channel_id=1, source_target_pairs={{8,16},{16,8},{9,17},{17,9},{10,18},{18,10},{11,19},{19,11},{12,20... | collective-permute-start | bytes 3145736 | tf_op jit(solution)/shard_map/ppermute | solution.py:817
  132.0 28.8 %collective-permute-start.24 = (bf16[256,2048]{1,0:T(8,128)(2,1)}, bf16[256,2048]{1,0:T(8,128)(2,1)}, u32[]{:S(2)}, u32[]{:S(2)}) collective-permute-start(bf16[256,2048]{1,0:T(8,128)(2,1)} %collective-permute-done.15.refs_1_), channel_id=1, source_target_pairs={{0,4},{4,0},{1,5},{5,1},{2,6},{6,2},{3,7},{7,3},{8,12},{12,8},{9,1... | collective-permute-start | bytes 3145736 | tf_op jit(solution)/shard_map/ppermute | solution.py:815
  133.3 27.5 %collective-permute-start.22 = (bf16[256,2048]{1,0:T(8,128)(2,1)}, bf16[256,2048]{1,0:T(8,128)(2,1)}, u32[]{:S(2)}, u32[]{:S(2)}) collective-permute-start(bf16[256,2048]{1,0:T(8,128)(2,1)} %collective-permute-done.16), channel_id=1, source_target_pairs={{8,0},{16,24},{9,1},{17,25},{10,2},{18,26},{11,3},{19,27},{12,4},{... | collective-permute-start | bytes 3145736 | tf_op jit(solution)/shard_map/ppermute | solution.py:816
  160.8 23.9 %collective-permute-start.25 = (bf16[256,2048]{1,0:T(8,128)(2,1)}, bf16[256,2048]{1,0:T(8,128)(2,1)}, u32[]{:S(2)}, u32[]{:S(2)}) collective-permute-start(bf16[256,2048]{1,0:T(8,128)(2,1)} %collective-permute-done.23), channel_id=1, source_target_pairs={{8,0},{16,24},{9,1},{17,25},{10,2},{18,26},{11,3},{19,27},{12,4},{... | collective-permute-start | bytes 3145736 | tf_op jit(solution)/shard_map/ppermute | solution.py:825
  165.4 24.5 %collective-permute-start.26 = (bf16[256,2048]{1,0:T(8,128)(2,1)}, bf16[256,2048]{1,0:T(8,128)(2,1)}, u32[]{:S(2)}, u32[]{:S(2)}) collective-permute-start(bf16[256,2048]{1,0:T(8,128)(2,1)} %broadcast_select_fusion.3.refs_3_), channel_id=1, source_target_pairs={{0,4},{4,0},{1,5},{5,1},{2,6},{6,2},{3,7},{7,3},{8,12},{12,8},{9,1... | collective-permute-start | bytes 3145736 | tf_op jit(solution)/shard_map/ppermute | solution.py:824
  184.7 24.9 %collective-permute-start.28 = (bf16[1024,512]{1,0:T(8,128)(2,1)}, bf16[1024,512]{1,0:T(8,128)(2,1)}, u32[]{:S(2)}, u32[]{:S(2)}) collective-permute-start(bf16[1024,512]{1,0:T(8,128)(2,1)} %constant_dynamic-slice_fusion.3), channel_id=1, source_target_pairs={{0,8},{8,0},{16,24},{24,16},{1,9},{9,1},{17,25},{25,17},{2,10},{10... | collective-permute-start | bytes 3145736 | tf_op jit(solution)/shard_map/ppermute | solution.py:810
  186.9 25.5 %collective-permute-start.29 = (bf16[1024,512]{1,0:T(8,128)(2,1)}, bf16[1024,512]{1,0:T(8,128)(2,1)}, u32[]{:S(2)}, u32[]{:S(2)}) collective-permute-start(bf16[1024,512]{1,0:T(8,128)(2,1)} %constant_dynamic-slice_fusion.3), channel_id=1, source_target_pairs={{8,16},{16,8},{9,17},{17,9},{10,18},{18,10},{11,19},{19,11},{12,20... | collective-permute-start | bytes 3145736 | tf_op jit(solution)/shard_map/ppermute | solution.py:811
  192.2 23.6 %collective-permute-start.27 = (bf16[256,2048]{1,0:T(8,128)(2,1)}, bf16[256,2048]{1,0:T(8,128)(2,1)}, u32[]{:S(2)}, u32[]{:S(2)}) collective-permute-start(bf16[256,2048]{1,0:T(8,128)(2,1)} %broadcast_select_fusion.2.refs_5_), channel_id=1, source_target_pairs={{0,4},{4,0},{1,5},{5,1},{2,6},{6,2},{3,7},{7,3},{8,12},{12,8},{9,1... | collective-permute-start | bytes 3145736 | tf_op jit(solution)/shard_map/ppermute | solution.py:832
  215.8 24.5 %collective-permute-start.32 = (bf16[1024,512]{1,0:T(8,128)(2,1)}, bf16[1024,512]{1,0:T(8,128)(2,1)}, u32[]{:S(2)}, u32[]{:S(2)}) collective-permute-start(bf16[1024,512]{1,0:T(8,128)(2,1)} %collective-permute-done.28.refs_1_), channel_id=1, source_target_pairs={{8,16},{16,8},{9,17},{17,9},{10,18},{18,10},{11,19},{19,11},{12,20... | collective-permute-start | bytes 3145736 | tf_op jit(solution)/shard_map/ppermute | solution.py:817
  222.9 35.2 %collective-permute-start.21 = (bf16[384,2176]{1,0:T(8,128)(2,1)}, bf16[384,2176]{1,0:T(8,128)(2,1)}, u32[]{:S(2)}, u32[]{:S(2)}) collective-permute-start(bf16[384,2176]{1,0:T(8,128)(2,1)} %copy-done.22), channel_id=1, source_target_pairs={{0,2},{2,0},{1,3},{3,1},{4,6},{6,4},{5,7},{7,5},{8,10},{10,8},{9,1... | collective-permute-start | bytes 5013512 | tf_op jit(solution)/shard_map/ppermute | solution.py:968
  242.7 32.2 %collective-permute-start.35 = (bf16[1024,512]{1,0:T(8,128)(2,1)}, bf16[1024,512]{1,0:T(8,128)(2,1)}, u32[]{:S(2)}, u32[]{:S(2)}) collective-permute-start(bf16[1024,512]{1,0:T(8,128)(2,1)} %broadcast_select_fusion.1.refs_3_), channel_id=1, source_target_pairs={{0,4},{4,0},{1,5},{5,1},{2,6},{6,2},{3,7},{7,3},{8,12},{12,8},{9,1... | collective-permute-start | bytes 3145736 | tf_op jit(solution)/shard_map/ppermute | solution.py:824
  243.0 31.9 %collective-permute-start.34 = (bf16[1024,512]{1,0:T(8,128)(2,1)}, bf16[1024,512]{1,0:T(8,128)(2,1)}, u32[]{:S(2)}, u32[]{:S(2)}) collective-permute-start(bf16[1024,512]{1,0:T(8,128)(2,1)} %collective-permute-done.32), channel_id=1, source_target_pairs={{8,0},{16,24},{9,1},{17,25},{10,2},{18,26},{11,3},{19,27},{12,4},{... | collective-permute-start | bytes 3145736 | tf_op jit(solution)/shard_map/ppermute | solution.py:825
  276.3 24.9 %collective-permute-start.36 = (bf16[1024,512]{1,0:T(8,128)(2,1)S(1)}, bf16[1024,512]{1,0:T(8,128)(2,1)S(1)}, u32[]{:S(2)}, u32[]{:S(2)}) collective-permute-start(bf16[1024,512]{1,0:T(8,128)(2,1)S(1)} %broadcast_select_fusion.refs_5_), channel_id=1, source_target_pairs={{0,4},{4,0},{1,5},{5,1},{2,6},{6,2},{3,7},{7,3},{8,12},{12,8},{9,1... | collective-permute-start | bytes 3145736 | tf_op jit(solution)/shard_map/ppermute | solution.py:832
  327.2 38.2 %collective-permute-start.40 = (bf16[384,2176]{1,0:T(8,128)(2,1)S(1)}, bf16[384,2176]{1,0:T(8,128)(2,1)S(1)}, u32[]{:S(2)}, u32[]{:S(2)}) collective-permute-start(bf16[384,2176]{1,0:T(8,128)(2,1)S(1)} %join.5.refs_0_), channel_id=1, source_target_pairs={{0,2},{2,0},{1,3},{3,1},{4,6},{6,4},{5,7},{7,5},{8,10},{10,8},{9,1... | collective-permute-start | bytes 5013512 | tf_op jit(solution)/shard_map/ppermute | solution.py:968
  370.2 38.1 %collective-permute-start.41 = (bf16[384,2176]{1,0:T(8,128)(2,1)S(1)}, bf16[384,2176]{1,0:T(8,128)(2,1)S(1)}, u32[]{:S(2)}, u32[]{:S(2)}) collective-permute-start(bf16[384,2176]{1,0:T(8,128)(2,1)S(1)} %join.6.refs_0_), channel_id=1, source_target_pairs={{0,2},{2,0},{1,3},{3,1},{4,6},{6,4},{5,7},{7,5},{8,10},{10,8},{9,1... | collective-permute-start | bytes 5013512 | tf_op jit(solution)/shard_map/ppermute | solution.py:968
  387.0 37.5 %collective-permute-start.45 = (bf16[2,768,512]{2,1,0:T(8,128)(2,1)S(1)}, bf16[2,768,512]{2,1,0:T(8,128)(2,1)S(1)}, u32[]{:S(2)}, u32[]{:S(2)}) collective-permute-start(bf16[2,768,512]{2,1,0:T(8,128)(2,1)S(1)} %get-tuple-element.148), channel_id=1, source_target_pairs={{4,0},{5,1},{6,2},{7,3},{12,8},{13,9},{14,10},{15,11},{20,16},{21,... | collective-permute-start | bytes 4718600 | tf_op jit(solution)/shard_map/ppermute | solution.py:968
  436.5 25.4 %collective-permute-start.42 = (bf16[384,2048]{1,0:T(8,128)(2,1)}, bf16[384,2048]{1,0:T(8,128)(2,1)}, u32[]{:S(2)}, u32[]{:S(2)}) collective-permute-start(bf16[384,2048]{1,0:T(8,128)(2,1)} %get-tuple-element.138.own_ref), channel_id=1, source_target_pairs={{0,1},{1,0},{2,3},{3,2},{4,5},{5,4},{6,7},{7,6},{8,9},{9,8},{10,11... | collective-permute-start | bytes 4718600 | tf_op jit(solution)/shard_map/ppermute | solution.py:968
  443.1 35.0 %collective-permute-start.49 = (bf16[384,2048]{1,0:T(8,128)(2,1)}, bf16[384,2048]{1,0:T(8,128)(2,1)}, u32[]{:S(2)}, u32[]{:S(2)}) collective-permute-start(bf16[384,2048]{1,0:T(8,128)(2,1)} %join.7.refs_0_), channel_id=1, source_target_pairs={{0,2},{2,0},{1,3},{3,1},{4,6},{6,4},{5,7},{7,5},{8,10},{10,8},{9,1... | collective-permute-start | bytes 4718600 | tf_op jit(solution)/shard_map/ppermute | solution.py:968
  (126 other events, 1870.3 us)

commit v5 on v4

--- a/solution.py
+++ b/solution.py
@@ -127,7 +127,7 @@
             jax.ShapeDtypeStruct((heads, tokens, far_rows), bf16),
             jax.ShapeDtypeStruct((heads, tokens, tokens), bf16),
         ],
-        compiler_params=pltpu.CompilerParams(vmem_limit_bytes=(14 if far_rows == tokens else 56) << 20),
+        compiler_params=pltpu.CompilerParams(vmem_limit_bytes=(44 if far_rows == tokens else 56) << 20),
         cost_estimate=HINT,
         name="attend_forward",
     )(qkv, qkv, qkv, far, far, far_bias, own_bias)
@@ -200,7 +200,7 @@
             pltpu.VMEM((far_rows, HD), f32),
             pltpu.VMEM((far_rows, HD), f32),
         ],
-        compiler_params=pltpu.CompilerParams(vmem_limit_bytes=(16 if far_rows == tokens else 56) << 20),
+        compiler_params=pltpu.CompilerParams(vmem_limit_bytes=(44 if far_rows == tokens else 56) << 20),
         cost_estimate=HINT,
         name="attend_backward",
     )(qkv, qkv, qkv, far, far, grad_attended, attended, probs_far, probs_own)
@@ -685,11 +685,15 @@
     tokens, wide = own.shape
     blocks = 3 + (2 if far is not None else 0)
 
+    def column(n):
+        return jnp.where(n < 3, n, n - 2)
+
     def kernel(*refs):
         bias_ref, w_ref, out_ref = refs[-3:]
 
         def write(x_ref):
-            out_ref[...] = (dot_nn(x_ref[...], w_ref[...]) + bias_ref[...]).astype(bf16)
+            at = pl.ds(pl.multiple_of(column(pl.program_id(0)) * local, local), local)
+            out_ref[...] = (dot_nn(x_ref[...], w_ref[:, at]) + bias_ref[...]).astype(bf16)
 
         if far is None:
             write(refs[0])
@@ -697,9 +701,6 @@
             pl.when(pl.program_id(0) < 3)(lambda: write(refs[0]))
             pl.when(pl.program_id(0) >= 3)(lambda: write(refs[1]))
 
-    def column(n):
-        return jnp.where(n < 3, n, n - 2)
-
     rows = [own] if far is None else [own, far]
     return pl.pallas_call(
         kernel,
@@ -707,7 +708,7 @@
         in_specs=[pl.BlockSpec((tokens, wide), lambda n: (0, 0))] * len(rows)
         + [
             pl.BlockSpec((1, local), lambda n: (0, column(n))),
-            pl.BlockSpec((wide, local), lambda n: (0, column(n))),
+            pl.BlockSpec(memory_space=pltpu.VMEM),
         ],
         out_specs=pl.BlockSpec((tokens, local), lambda n: (0, n)),
         out_shape=jax.ShapeDtypeStruct((tokens, blocks * local), bf16),
@@ -772,7 +773,7 @@
         ],
         out_specs=block,
         out_shape=jax.ShapeDtypeStruct((tokens, hidden), bf16),
-        compiler_params=pltpu.CompilerParams(vmem_limit_bytes=14 << 20),
+        compiler_params=pltpu.CompilerParams(vmem_limit_bytes=36 << 20),
         cost_estimate=HINT,
         name="back_hidden",
     )(loss, weight, slope)

time: 498 us -> 485 us (0.974)
  waiting for transfers between devices: 186 us -> 175 us
  local copies, waits for them, and re-layouts: 54.9 us -> 49.5 us
    ppermute x29, waiting for transfers between devices: 95.7 us -> 89.8 us  [on(): return lax.ppermute(value, axis, pairs)]
    unnamed x181 -> x165, local copies, waits for them, and re-layouts: 28.5 us -> 29 us
  transfers between devices with their start and end apart: 59 -> 59, of which waited for: 29 -> 29; matrix products, arithmetic and copies ran while one was open for 9% -> 7% of each run, Pallas kernels for 22% -> 23%
where the time goes in v5:
time: 485 us; the launch traced here: 477 us
  waiting for transfers between devices  175 us (36%)
  Pallas kernels  143 us (29%)
  starting transfers between devices  83 us (17%)
  local copies, waits for them, and re-layouts  49.5 us (10%)
  other arithmetic  18 us (4%)
  between operations  6.54 us (1%)
    ppermute x29, waiting for transfers between devices, on(): return lax.ppermute(value, axis, pairs)  89.8 us
    ppermute x29, starting transfers between devices, on(): return lax.ppermute(value, axis, pairs)  35.1 us
    unnamed x165, local copies, waits for them, and re-layouts  29 us
    pallas_call x6, Pallas kernels, matmul(): pl.pallas_call(kernel, grid_spec=pltpu.PrefetchScalarGridSpec(num_scalar_...  23.4 us
    pallas_call x4, Pallas kernels, row_call(): pl.pallas_call(kernel, grid_spec=pltpu.PrefetchScalarGridSpec(num_scalar_...  18.8 us
    ppermute x3, waiting for transfers between devices, third(): self.last = lax.ppermute(self.back, 'fsdp', [(1, 0), (2, 3)])  17.7 us
    ppermute x3, waiting for transfers between devices, first(): lax.ppermute(part, 'fsdp', [(i, i ^ k) for i in range(4)])  15.8 us
    ppermute x3, waiting for transfers between devices, second(): self.back = lax.ppermute(self.one, 'fsdp', [(1, 2), (2, 1)])  14.3 us
  transfers between devices with their start and end apart: 59, of which 29 were waited for; matrix products, arithmetic and copies ran while one was open for 7% of the time, Pallas kernels for 23%

profile of v5, /device:TPU:9, one launch (start us, length us, event | category | flops | bytes accessed | tf_op | source)
XLA Modules:
  0.0 477.0 jit_solution(14405397398495951389)
XLA Ops:
  31.1 12.9 %collective-permute-done.4 = bf16[3,256,512]{2,1,0:T(8,128)(2,1)S(1)} collective-permute-done((bf16[3,256,512]{2,1,0:T(8,128)(2,1)}, bf16[3,256,512]{2,1,0:T(8,128)(2,1)S(1)}, u32[]{:S(2)}, u32[]{:S(2)}) %collective-permute-start.4) | collective-permute-done | bytes 786464 | tf_op jit(solution)/shard_map/ppermute | solution.py:818
  62.6 8.1 %collective-permute-done.8 = bf16[3,256,512]{2,1,0:T(8,128)(2,1)S(1)} collective-permute-done((bf16[3,256,512]{2,1,0:T(8,128)(2,1)S(1)}, bf16[3,256,512]{2,1,0:T(8,128)(2,1)S(1)}, u32[]{:S(2)}, u32[]{:S(2)}) %collective-permute-start.8) | collective-permute-done | bytes 786464 | tf_op jit(solution)/shard_map/ppermute | solution.py:826
  78.3 4.8 %norm_wide.3.refs_1_ = bf16[768,2176]{1,0:T(8,128)(2,1)S(1)} custom-call(s32[4]{0:T(128)S(1)} %pad_add_fusion.place_ref, s32[3]{0:T(128)S(1)} %get-tuple-element.205.slot_ref, bf16[192,2048]{1,0:T(8,128)(2,1)} %collective-permute-done.refs_0_, bf16[192,2048]{1,0:T(8,128)(2,1)S(1)} %collective-permute-done.6.refs_1_, ...), custom_call_target="tpu_custom_call" | custom-call | flops 1 | bytes 1 | tf_op jit(solution)/shard_map/norm_wide/pallas_call | solution.py:302
  88.4 12.2 %collective-permute-done.12.refs_5_ = bf16[256,512]{1,0:T(8,128)(2,1)} collective-permute-done((bf16[256,512]{1,0:T(8,128)(2,1)S(1)}, bf16[256,512]{1,0:T(8,128)(2,1)}, u32[]{:S(2)}, u32[]{:S(2)}) %collective-permute-start.12) | collective-permute-done | bytes 262176 | tf_op jit(solution)/shard_map/ppermute | solution.py:791
  115.4 10.3 %project.1.q_ref.k_ref.v_ref.fk_ref.fv_ref = bf16[768,2560]{1,0:T(8,128)(2,1)S(1)} custom-call(bf16[768,2176]{1,0:T(8,128)(2,1)S(1)} %copy-done.13, bf16[768,2176]{1,0:T(8,128)(2,1)S(1)} %copy-done.22, f32[1,1536]{1,0:T(1,128)S(1)} %broadcast_in_dim.114.refs_2_, bf16[2176,1536]{1,0:T(8,128)(2,1)S(1)} %copy-done.4), custom_call_target="tpu_custom_call" | custom-call | flops 1 | bytes 1 | tf_op jit(solution)/shard_map/project/pallas_call | solution.py:705
  136.8 12.3 %attend_forward.1 = (f32[768,512]{1,0:T(8,128)S(1)}, bf16[768,512]{1,0:T(8,128)(2,1)S(1)}, bf16[4,768,768]{2,1,0:T(8,128)(2,1)}, bf16[4,768,768]{2,1,0:T(8,128)(2,1)}) custom-call(bf16[768,2560]{1,0:T(8,128)(2,1)S(1)} %copy-done.1, bf16[768,2560]{1,0:T(8,128)(2,1)S(1)} %copy-done.1, bf16[768,2560]{1,0:T(8,128)(2,1)S(1)} %copy-done.1, ...), custom_call_target="tpu_custom_call" | custom-call | flops 1 | bytes 1 | tf_op jit(solution)/shard_map/attend_forward/pallas_call | solution.py:106
  168.0 9.5 %collective-permute-done.25 = bf16[256,2048]{1,0:T(8,128)(2,1)} collective-permute-done((bf16[256,2048]{1,0:T(8,128)(2,1)}, bf16[256,2048]{1,0:T(8,128)(2,1)}, u32[]{:S(2)}, u32[]{:S(2)}) %collective-permute-start.25) | collective-permute-done | bytes 1048608 | tf_op jit(solution)/shard_map/ppermute | solution.py:826
  188.0 11.2 %collective-permute-done.28.refs_1_ = bf16[1024,512]{1,0:T(8,128)(2,1)} collective-permute-done((bf16[1024,512]{1,0:T(8,128)(2,1)}, bf16[1024,512]{1,0:T(8,128)(2,1)}, u32[]{:S(2)}, u32[]{:S(2)}) %collective-permute-start.28) | collective-permute-done | bytes 1048608 | tf_op jit(solution)/shard_map/ppermute | solution.py:811
  215.7 10.4 %collective-permute-done.31 = bf16[1024,512]{1,0:T(8,128)(2,1)} collective-permute-done((bf16[1024,512]{1,0:T(8,128)(2,1)}, bf16[1024,512]{1,0:T(8,128)(2,1)}, u32[]{:S(2)}, u32[]{:S(2)}) %collective-permute-start.31) | collective-permute-done | bytes 1048608 | tf_op jit(solution)/shard_map/ppermute | solution.py:817
  229.0 5.2 %collective-permute-start.34 = (bf16[1024,512]{1,0:T(8,128)(2,1)}, bf16[1024,512]{1,0:T(8,128)(2,1)}, u32[]{:S(2)}, u32[]{:S(2)}) collective-permute-start(bf16[1024,512]{1,0:T(8,128)(2,1)} %collective-permute-done.32), channel_id=1, source_target_pairs={{8,0},{16,24},{9,1},{17,25},{10,2},{18,26},{11,3},{19,27},{12,4},{... | collective-permute-start | bytes 3145736 | tf_op jit(solution)/shard_map/ppermute | solution.py:826
  234.5 10.4 %collective-permute-done.21.refs_1_ = bf16[384,2176]{1,0:T(8,128)(2,1)} collective-permute-done((bf16[384,2176]{1,0:T(8,128)(2,1)}, bf16[384,2176]{1,0:T(8,128)(2,1)}, u32[]{:S(2)}, u32[]{:S(2)}) %collective-permute-start.21) | collective-permute-done | bytes 1671200 | tf_op jit(solution)/shard_map/ppermute | solution.py:969
  244.9 4.8 %after_attention.1 = (f32[384,2048]{1,0:T(8,128)S(1)}, bf16[384,2176]{1,0:T(8,128)(2,1)S(1)}) custom-call(s32[1]{0:T(128)} %bitcast.half_ref.core_ref, s32[3]{0:T(128)S(1)} %get-tuple-element.206.slot_ref, bf16[384,2176]{1,0:T(8,128)(2,1)S(1)} %copy-done.31, bf16[384,2176]{1,0:T(8,128)(2,1)} %collective-permute-done.21.refs_1_, ...), custom_call_target="tpu_custom_call" | custom-call | flops 1 | bytes 1 | tf_op jit(solution)/shard_map/after_attention/pallas_call | solution.py:349
  251.4 7.0 %collective-permute-start.30 = (bf16[384,2176]{1,0:T(8,128)(2,1)S(1)}, bf16[384,2176]{1,0:T(8,128)(2,1)}, u32[]{:S(2)}, u32[]{:S(2)}) collective-permute-start(bf16[384,2176]{1,0:T(8,128)(2,1)S(1)} %get-tuple-element.117.own_ref.two_a), channel_id=1, source_target_pairs={{0,1},{1,0},{2,3},{3,2},{4,5},{5,4},{6,7},{7,6},{8,9},{9,8},{10,11... | collective-permute-start | bytes 5013512 | tf_op jit(solution)/shard_map/ppermute | solution.py:969
  270.0 11.6 %expand.1 = (bf16[768,2048]{1,0:T(8,128)(2,1)S(1)}, bf16[768,2048]{1,0:T(8,128)(2,1)S(1)}) custom-call(bf16[384,2176]{1,0:T(8,128)(2,1)S(1)} %get-tuple-element.117.own_ref.two_a, bf16[384,2176]{1,0:T(8,128)(2,1)} %collective-permute-done.30.other_ref.two_b, bf16[2176,2048]{1,0:T(8,128)(2,1)S(1)} %assemble.6.w_ref, f32[1,2048]{1,0:T(1,128)S(1)} %bitcast.78), custom_call_target="tpu_custom_call" | custom-call | flops 1 | bytes 1 | tf_op jit(solution)/shard_map/expand/pallas_call | solution.py:739
  281.6 5.1 %collective-permute-done.36.refs_6_ = bf16[1024,512]{1,0:T(8,128)(2,1)S(1)} collective-permute-done((bf16[1024,512]{1,0:T(8,128)(2,1)S(1)}, bf16[1024,512]{1,0:T(8,128)(2,1)S(1)}, u32[]{:S(2)}, u32[]{:S(2)}) %collective-permute-start.36) | collective-permute-done | bytes 1048608 | tf_op jit(solution)/shard_map/ppermute | solution.py:833
  289.4 8.6 %back_hidden.1.x_ref.gp_ref = bf16[768,2048]{1,0:T(8,128)(2,1)S(1)} custom-call(bf16[768,2176]{1,0:T(8,128)(2,1)S(1)} %pad_maximum_fusion.x_ref, bf16[2048,2176]{1,0:T(8,128)(2,1)S(1)} %assemble.7.w_ref, bf16[768,2048]{1,0:T(8,128)(2,1)S(1)} %get-tuple-element.132.s_ref), custom_call_target="tpu_custom_call" | custom-call | flops 1 | bytes 1 | tf_op jit(solution)/shard_map/back_hidden/pallas_call | solution.py:766
  298.1 5.3 %matmul.9 = bf16[384,2176]{1,0:T(8,128)(2,1)S(1)} custom-call(s32[1]{0:T(128)} %constant.159.clone.1.half_ref, bf16[768,2048]{1,0:T(8,128)(2,1)S(1)} %back_hidden.1.x_ref.gp_ref, bf16[2176,2048]{1,0:T(8,128)(2,1)S(1)} %assemble.6.w_ref), custom_call_target="tpu_custom_call" | custom-call | flops 1 | bytes 1 | tf_op jit(solution)/shard_map/matmul/pallas_call | solution.py:884
  304.3 5.5 %matmul.8.a_ref = bf16[384,2176]{1,0:T(8,128)(2,1)S(1)} custom-call(s32[1]{0:T(128)} %constant.146.clone.1.half_ref, bf16[768,2048]{1,0:T(8,128)(2,1)S(1)} %back_hidden.1.x_ref.gp_ref, bf16[2176,2048]{1,0:T(8,128)(2,1)S(1)} %assemble.6.w_ref), custom_call_target="tpu_custom_call" | custom-call | flops 1 | bytes 1 | tf_op jit(solution)/shard_map/matmul/pallas_call | solution.py:884
  323.2 25.5 %collective-permute-done.40.refs_1_ = bf16[384,2176]{1,0:T(8,128)(2,1)S(1)} collective-permute-done((bf16[384,2176]{1,0:T(8,128)(2,1)S(1)}, bf16[384,2176]{1,0:T(8,128)(2,1)S(1)}, u32[]{:S(2)}, u32[]{:S(2)}) %collective-permute-start.40) | collective-permute-done | bytes 1671200 | tf_op jit(solution)/shard_map/ppermute | solution.py:969
  360.4 13.5 %attend_backward.1 = (bf16[768,512]{1,0:T(8,128)(2,1)S(1)}, bf16[768,512]{1,0:T(8,128)(2,1)S(1)}, bf16[768,512]{1,0:T(8,128)(2,1)S(1)}, bf16[2,768,512]{2,1,0:T(8,128)(2,1)S(1)}) custom-call(bf16[768,2560]{1,0:T(8,128)(2,1)S(1)} %copy-done.2, bf16[768,2560]{1,0:T(8,128)(2,1)S(1)} %copy-done.2, bf16[768,2560]{1,0:T(8,128)(2,1)S(1)} %copy-done.2, ...), custom_call_target="tpu_custom_call" | custom-call | flops 1 | bytes 1 | tf_op jit(solution)/shard_map/attend_backward/pallas_call | solution.py:181
  375.2 18.2 %collective-permute-done.41.refs_1_ = bf16[384,2176]{1,0:T(8,128)(2,1)} collective-permute-done((bf16[384,2176]{1,0:T(8,128)(2,1)}, bf16[384,2176]{1,0:T(8,128)(2,1)}, u32[]{:S(2)}, u32[]{:S(2)}) %collective-permute-start.41) | collective-permute-done | bytes 1671200 | tf_op jit(solution)/shard_map/ppermute | solution.py:969
  395.4 5.4 %after_hidden.1 = (bf16[384,2048]{1,0:T(8,128)(2,1)}, bf16[384,128]{1,0:T(8,128)(2,1)S(1)}) custom-call(s32[1]{0:T(128)} %bitcast.half_ref.core_ref, s32[3]{0:T(128)S(1)} %get-tuple-element.206.slot_ref, bf16[384,2176]{1,0:T(8,128)(2,1)} %join.6.refs_0_, bf16[384,2176]{1,0:T(8,128)(2,1)} %collective-permute-done.41.refs_1_, f32[384,2048]{1,0:T(8,128)S(1)} %copy-done.25, ...), custom_call_target="tpu_custom_call" | custom-call | flops 1 | bytes 1 | tf_op jit(solution)/shard_map/after_hidden/pallas_call | solution.py:349
  412.8 5.6 %back_project.1 = (bf16[384,2048]{1,0:T(8,128)(2,1)S(1)}, bf16[384,2048]{1,0:T(8,128)(2,1)S(1)}) custom-call(s32[1]{0:T(128)} %bitcast.half_ref.core_ref, bf16[768,1536]{1,0:T(8,128)(2,1)S(1)} %pad_maximum_fusion.1.x_ref.gq_ref, bf16[2176,1536]{1,0:T(8,128)(2,1)S(1)} %bitcast.77), custom_call_target="tpu_custom_call" | custom-call | flops 1 | bytes 1 | tf_op jit(solution)/shard_map/back_project/pallas_call | solution.py:406
  457.1 7.8 %collective-permute-done.49.refs_1_ = bf16[384,2048]{1,0:T(8,128)(2,1)} collective-permute-done((bf16[384,2048]{1,0:T(8,128)(2,1)}, bf16[384,2048]{1,0:T(8,128)(2,1)}, u32[]{:S(2)}, u32[]{:S(2)}) %collective-permute-start.49) | collective-permute-done | bytes 1572896 | tf_op jit(solution)/shard_map/ppermute | solution.py:969
  (386 shorter events, 239.0 us)
Async XLA Ops:
  2.7 21.7 %collective-permute-start.2 = (bf16[3,256,512]{2,1,0:T(8,128)(2,1)}, bf16[3,256,512]{2,1,0:T(8,128)(2,1)}, u32[]{:S(2)}, u32[]{:S(2)}) collective-permute-start(bf16[3,256,512]{2,1,0:T(8,128)(2,1)} %constant_dynamic-slice_fusion.12), channel_id=1, source_target_pairs={{8,16},{16,8},{9,17},{17,9},{10,18},{18,10},{11,19},{19,11},{12,20... | collective-permute-start | bytes 2359304 | tf_op jit(solution)/shard_map/ppermute | solution.py:812
  9.3 21.8 %collective-permute-start = (bf16[192,2048]{1,0:T(8,128)(2,1)}, bf16[192,2048]{1,0:T(8,128)(2,1)}, u32[]{:S(2)}, u32[]{:S(2)}) collective-permute-start(bf16[192,2048]{1,0:T(8,128)(2,1)} %constant_dynamic-slice_fusion.13), channel_id=1, source_target_pairs={{0,4},{1,5},{2,6},{3,7},{8,12},{9,13},{10,14},{11,15},{16,20},{17,... | collective-permute-start | bytes 2359304 | tf_op jit(solution)/shard_map/ppermute | solution.py:969
  70.8 29.9 %collective-permute-start.14 = (bf16[3,256,512]{2,1,0:T(8,128)(2,1)S(1)}, bf16[3,256,512]{2,1,0:T(8,128)(2,1)S(1)}, u32[]{:S(2)}, u32[]{:S(2)}) collective-permute-start(bf16[3,256,512]{2,1,0:T(8,128)(2,1)S(1)} %broadcast_select_fusion.4.refs_5_), channel_id=1, source_target_pairs={{0,4},{4,0},{1,5},{5,1},{2,6},{6,2},{3,7},{7,3},{8,12},{12,8},{9,1... | collective-permute-start | bytes 2359304 | tf_op jit(solution)/shard_map/ppermute | solution.py:833
  76.0 24.6 %collective-permute-start.12 = (bf16[256,512]{1,0:T(8,128)(2,1)S(1)}, bf16[256,512]{1,0:T(8,128)(2,1)}, u32[]{:S(2)}, u32[]{:S(2)}) collective-permute-start(bf16[256,512]{1,0:T(8,128)(2,1)S(1)} %constant_dynamic-slice_fusion.9), channel_id=1, source_target_pairs={{0,24},{8,16},{16,8},{24,0},{1,25},{9,17},{17,9},{25,1},{2,26},{10... | collective-permute-start | bytes 786440 | tf_op jit(solution)/shard_map/ppermute | solution.py:791
  100.6 26.9 %collective-permute-start.15 = (bf16[256,2048]{1,0:T(8,128)(2,1)}, bf16[256,2048]{1,0:T(8,128)(2,1)}, u32[]{:S(2)}, u32[]{:S(2)}) collective-permute-start(bf16[256,2048]{1,0:T(8,128)(2,1)} %constant_dynamic-slice_fusion.6), channel_id=1, source_target_pairs={{0,8},{8,0},{16,24},{24,16},{1,9},{9,1},{17,25},{25,17},{2,10},{10... | collective-permute-start | bytes 3145736 | tf_op jit(solution)/shard_map/ppermute | solution.py:811
  100.6 26.9 %collective-permute-start.16 = (bf16[256,2048]{1,0:T(8,128)(2,1)}, bf16[256,2048]{1,0:T(8,128)(2,1)}, u32[]{:S(2)}, u32[]{:S(2)}) collective-permute-start(bf16[256,2048]{1,0:T(8,128)(2,1)} %constant_dynamic-slice_fusion.6), channel_id=1, source_target_pairs={{8,16},{16,8},{9,17},{17,9},{10,18},{18,10},{11,19},{19,11},{12,20... | collective-permute-start | bytes 3145736 | tf_op jit(solution)/shard_map/ppermute | solution.py:812
  103.6 23.9 %collective-permute-start.17 = (bf16[256,512]{1,0:T(8,128)(2,1)}, bf16[256,512]{1,0:T(8,128)(2,1)}, u32[]{:S(2)}, u32[]{:S(2)}) collective-permute-start(bf16[256,512]{1,0:T(8,128)(2,1)} %collective-permute-done.10.refs_1_), channel_id=1, source_target_pairs={{0,4},{4,0},{1,5},{5,1},{2,6},{6,2},{3,7},{7,3},{8,12},{12,8},{9,1... | collective-permute-start | bytes 786440 | tf_op jit(solution)/shard_map/ppermute | solution.py:796
  103.8 23.6 %collective-permute-start.18 = (bf16[256,512]{1,0:T(8,128)(2,1)}, bf16[256,512]{1,0:T(8,128)(2,1)}, u32[]{:S(2)}, u32[]{:S(2)}) collective-permute-start(bf16[256,512]{1,0:T(8,128)(2,1)} %collective-permute-done.11.refs_3_), channel_id=1, source_target_pairs={{0,4},{4,0},{1,5},{5,1},{2,6},{6,2},{3,7},{7,3},{8,12},{12,8},{9,1... | collective-permute-start | bytes 786440 | tf_op jit(solution)/shard_map/ppermute | solution.py:796
  105.1 22.4 %collective-permute-start.19 = (bf16[256,512]{1,0:T(8,128)(2,1)}, bf16[256,512]{1,0:T(8,128)(2,1)}, u32[]{:S(2)}, u32[]{:S(2)}) collective-permute-start(bf16[256,512]{1,0:T(8,128)(2,1)} %collective-permute-done.12.refs_5_), channel_id=1, source_target_pairs={{0,4},{4,0},{1,5},{5,1},{2,6},{6,2},{3,7},{7,3},{8,12},{12,8},{9,1... | collective-permute-start | bytes 786440 | tf_op jit(solution)/shard_map/ppermute | solution.py:796
  127.5 28.6 %collective-permute-start.23 = (bf16[256,2048]{1,0:T(8,128)(2,1)}, bf16[256,2048]{1,0:T(8,128)(2,1)}, u32[]{:S(2)}, u32[]{:S(2)}) collective-permute-start(bf16[256,2048]{1,0:T(8,128)(2,1)} %collective-permute-done.15.refs_1_), channel_id=1, source_target_pairs={{8,16},{16,8},{9,17},{17,9},{10,18},{18,10},{11,19},{19,11},{12,20... | collective-permute-start | bytes 3145736 | tf_op jit(solution)/shard_map/ppermute | solution.py:818
  130.6 25.5 %collective-permute-start.24 = (bf16[256,2048]{1,0:T(8,128)(2,1)}, bf16[256,2048]{1,0:T(8,128)(2,1)}, u32[]{:S(2)}, u32[]{:S(2)}) collective-permute-start(bf16[256,2048]{1,0:T(8,128)(2,1)} %collective-permute-done.15.refs_1_), channel_id=1, source_target_pairs={{0,4},{4,0},{1,5},{5,1},{2,6},{6,2},{3,7},{7,3},{8,12},{12,8},{9,1... | collective-permute-start | bytes 3145736 | tf_op jit(solution)/shard_map/ppermute | solution.py:816
  131.9 24.2 %collective-permute-start.22 = (bf16[256,2048]{1,0:T(8,128)(2,1)}, bf16[256,2048]{1,0:T(8,128)(2,1)}, u32[]{:S(2)}, u32[]{:S(2)}) collective-permute-start(bf16[256,2048]{1,0:T(8,128)(2,1)} %collective-permute-done.16), channel_id=1, source_target_pairs={{8,0},{16,24},{9,1},{17,25},{10,2},{18,26},{11,3},{19,27},{12,4},{... | collective-permute-start | bytes 3145736 | tf_op jit(solution)/shard_map/ppermute | solution.py:817
  177.6 21.6 %collective-permute-start.28 = (bf16[1024,512]{1,0:T(8,128)(2,1)}, bf16[1024,512]{1,0:T(8,128)(2,1)}, u32[]{:S(2)}, u32[]{:S(2)}) collective-permute-start(bf16[1024,512]{1,0:T(8,128)(2,1)} %constant_dynamic-slice_fusion.3), channel_id=1, source_target_pairs={{0,8},{8,0},{16,24},{24,16},{1,9},{9,1},{17,25},{25,17},{2,10},{10... | collective-permute-start | bytes 3145736 | tf_op jit(solution)/shard_map/ppermute | solution.py:811
  179.8 22.1 %collective-permute-start.29 = (bf16[1024,512]{1,0:T(8,128)(2,1)}, bf16[1024,512]{1,0:T(8,128)(2,1)}, u32[]{:S(2)}, u32[]{:S(2)}) collective-permute-start(bf16[1024,512]{1,0:T(8,128)(2,1)} %constant_dynamic-slice_fusion.3), channel_id=1, source_target_pairs={{8,16},{16,8},{9,17},{17,9},{10,18},{18,10},{11,19},{19,11},{12,20... | collective-permute-start | bytes 3145736 | tf_op jit(solution)/shard_map/ppermute | solution.py:812
  205.9 21.7 %collective-permute-start.32 = (bf16[1024,512]{1,0:T(8,128)(2,1)}, bf16[1024,512]{1,0:T(8,128)(2,1)}, u32[]{:S(2)}, u32[]{:S(2)}) collective-permute-start(bf16[1024,512]{1,0:T(8,128)(2,1)} %collective-permute-done.28.refs_1_), channel_id=1, source_target_pairs={{8,16},{16,8},{9,17},{17,9},{10,18},{18,10},{11,19},{19,11},{12,20... | collective-permute-start | bytes 3145736 | tf_op jit(solution)/shard_map/ppermute | solution.py:818
  212.7 32.2 %collective-permute-start.21 = (bf16[384,2176]{1,0:T(8,128)(2,1)}, bf16[384,2176]{1,0:T(8,128)(2,1)}, u32[]{:S(2)}, u32[]{:S(2)}) collective-permute-start(bf16[384,2176]{1,0:T(8,128)(2,1)} %copy-done.30), channel_id=1, source_target_pairs={{0,2},{2,0},{1,3},{3,1},{4,6},{6,4},{5,7},{7,5},{8,10},{10,8},{9,1... | collective-permute-start | bytes 5013512 | tf_op jit(solution)/shard_map/ppermute | solution.py:969
  228.9 31.7 %collective-permute-start.35 = (bf16[1024,512]{1,0:T(8,128)(2,1)S(1)}, bf16[1024,512]{1,0:T(8,128)(2,1)}, u32[]{:S(2)}, u32[]{:S(2)}) collective-permute-start(bf16[1024,512]{1,0:T(8,128)(2,1)S(1)} %broadcast_select_fusion.1.refs_3_), channel_id=1, source_target_pairs={{0,4},{4,0},{1,5},{5,1},{2,6},{6,2},{3,7},{7,3},{8,12},{12,8},{9,1... | collective-permute-start | bytes 3145736 | tf_op jit(solution)/shard_map/ppermute | solution.py:825
  229.0 31.6 %collective-permute-start.34 = (bf16[1024,512]{1,0:T(8,128)(2,1)}, bf16[1024,512]{1,0:T(8,128)(2,1)}, u32[]{:S(2)}, u32[]{:S(2)}) collective-permute-start(bf16[1024,512]{1,0:T(8,128)(2,1)} %collective-permute-done.32), channel_id=1, source_target_pairs={{8,0},{16,24},{9,1},{17,25},{10,2},{18,26},{11,3},{19,27},{12,4},{... | collective-permute-start | bytes 3145736 | tf_op jit(solution)/shard_map/ppermute | solution.py:826
  262.0 24.8 %collective-permute-start.36 = (bf16[1024,512]{1,0:T(8,128)(2,1)S(1)}, bf16[1024,512]{1,0:T(8,128)(2,1)S(1)}, u32[]{:S(2)}, u32[]{:S(2)}) collective-permute-start(bf16[1024,512]{1,0:T(8,128)(2,1)S(1)} %broadcast_select_fusion.refs_5_), channel_id=1, source_target_pairs={{0,4},{4,0},{1,5},{5,1},{2,6},{6,2},{3,7},{7,3},{8,12},{12,8},{9,1... | collective-permute-start | bytes 3145736 | tf_op jit(solution)/shard_map/ppermute | solution.py:833
  310.5 38.1 %collective-permute-start.40 = (bf16[384,2176]{1,0:T(8,128)(2,1)S(1)}, bf16[384,2176]{1,0:T(8,128)(2,1)S(1)}, u32[]{:S(2)}, u32[]{:S(2)}) collective-permute-start(bf16[384,2176]{1,0:T(8,128)(2,1)S(1)} %join.5.refs_0_), channel_id=1, source_target_pairs={{0,2},{2,0},{1,3},{3,1},{4,6},{6,4},{5,7},{7,5},{8,10},{10,8},{9,1... | collective-permute-start | bytes 5013512 | tf_op jit(solution)/shard_map/ppermute | solution.py:969
  355.1 38.4 %collective-permute-start.41 = (bf16[384,2176]{1,0:T(8,128)(2,1)}, bf16[384,2176]{1,0:T(8,128)(2,1)}, u32[]{:S(2)}, u32[]{:S(2)}) collective-permute-start(bf16[384,2176]{1,0:T(8,128)(2,1)} %join.6.refs_0_), channel_id=1, source_target_pairs={{0,2},{2,0},{1,3},{3,1},{4,6},{6,4},{5,7},{7,5},{8,10},{10,8},{9,1... | collective-permute-start | bytes 5013512 | tf_op jit(solution)/shard_map/ppermute | solution.py:969
  373.8 37.5 %collective-permute-start.45 = (bf16[2,768,512]{2,1,0:T(8,128)(2,1)S(1)}, bf16[2,768,512]{2,1,0:T(8,128)(2,1)S(1)}, u32[]{:S(2)}, u32[]{:S(2)}) collective-permute-start(bf16[2,768,512]{2,1,0:T(8,128)(2,1)S(1)} %get-tuple-element.148), channel_id=1, source_target_pairs={{4,0},{5,1},{6,2},{7,3},{12,8},{13,9},{14,10},{15,11},{20,16},{21,... | collective-permute-start | bytes 4718600 | tf_op jit(solution)/shard_map/ppermute | solution.py:969
  423.3 25.2 %collective-permute-start.42 = (bf16[384,2048]{1,0:T(8,128)(2,1)}, bf16[384,2048]{1,0:T(8,128)(2,1)}, u32[]{:S(2)}, u32[]{:S(2)}) collective-permute-start(bf16[384,2048]{1,0:T(8,128)(2,1)} %get-tuple-element.138.own_ref), channel_id=1, source_target_pairs={{0,1},{1,0},{2,3},{3,2},{4,5},{5,4},{6,7},{7,6},{8,9},{9,8},{10,11... | collective-permute-start | bytes 4718600 | tf_op jit(solution)/shard_map/ppermute | solution.py:969
  429.9 35.0 %collective-permute-start.49 = (bf16[384,2048]{1,0:T(8,128)(2,1)}, bf16[384,2048]{1,0:T(8,128)(2,1)}, u32[]{:S(2)}, u32[]{:S(2)}) collective-permute-start(bf16[384,2048]{1,0:T(8,128)(2,1)} %join.7.refs_0_), channel_id=1, source_target_pairs={{0,2},{2,0},{1,3},{3,1},{4,6},{6,4},{5,7},{7,5},{8,10},{10,8},{9,1... | collective-permute-start | bytes 4718600 | tf_op jit(solution)/shard_map/ppermute | solution.py:969
  (118 other events, 1446.1 us)

commit v6 on v5

--- a/solution.py
+++ b/solution.py
@@ -1175,7 +1175,7 @@
         two_other = on(two_own, "tp", CORE_SWAP)
 
         if pair_ctx:
-            out_ring.second(in_ring.y_three)
+            out_ring.second(branch_far)
             in_full = assemble(
                 gate(spot, out_ring.outward, out_ring.back),
                 in_ring.pieces(),

time: 485 us -> 477 us (0.984)
  the two profiles are of different devices: /device:TPU:9 before, /device:TPU:0 now
where the time goes in v6:
time: 477 us; the launch traced here: 469 us
  waiting for transfers between devices  191 us (40%)
  Pallas kernels  145 us (30%)
  starting transfers between devices  64.1 us (13%)
  local copies, waits for them, and re-layouts  47 us (10%)
  other arithmetic  14 us (3%)
  between operations  6.53 us (1%)
    ppermute x29, waiting for transfers between devices, on(): return lax.ppermute(value, axis, pairs)  89.3 us
    ppermute x3, waiting for transfers between devices, second(): self.outward = lax.ppermute(self.across, 'fsdp', [(1, 0), (2, 3)])  27.6 us
    unnamed x161, local copies, waits for them, and re-layouts  26.8 us
    ppermute x3, waiting for transfers between devices, third(): self.last = lax.ppermute(self.back, 'fsdp', [(1, 0), (2, 3)])  24.5 us
    pallas_call x6, Pallas kernels, matmul(): pl.pallas_call(kernel, grid_spec=pltpu.PrefetchScalarGridSpec(num_scalar_...  23.5 us
    ppermute x29, starting transfers between devices, on(): return lax.ppermute(value, axis, pairs)  19.8 us
    pallas_call x4, Pallas kernels, row_call(): pl.pallas_call(kernel, grid_spec=pltpu.PrefetchScalarGridSpec(num_scalar_...  19.1 us
    ppermute x3, waiting for transfers between devices, second(): self.y_one = lax.ppermute(self.one, 'ctx', SWAP_Y)  15.4 us
  transfers between devices with their start and end apart: 59, of which 28 were waited for; matrix products, arithmetic and copies ran while one was open for 7% of the time, Pallas kernels for 24%

profile of v6, /device:TPU:0, one launch (start us, length us, event | category | flops | bytes accessed | tf_op | source)
XLA Modules:
  0.0 469.1 jit_solution(17070333047083801896)
XLA Ops:
  31.1 15.4 %collective-permute-done.5.refs_2_ = bf16[3,256,512]{2,1,0:T(8,128)(2,1)S(1)} collective-permute-done((bf16[3,256,512]{2,1,0:T(8,128)(2,1)}, bf16[3,256,512]{2,1,0:T(8,128)(2,1)S(1)}, u32[]{:S(2)}, u32[]{:S(2)}) %collective-permute-start.5) | collective-permute-done | bytes 786464 | tf_op jit(solution)/shard_map/ppermute | solution.py:816
  59.4 8.7 %collective-permute-done.6.refs_1_ = bf16[192,2048]{1,0:T(8,128)(2,1)S(1)} collective-permute-done((bf16[192,2048]{1,0:T(8,128)(2,1)}, bf16[192,2048]{1,0:T(8,128)(2,1)S(1)}, u32[]{:S(2)}, u32[]{:S(2)}) %collective-permute-start.6) | collective-permute-done | bytes 786464 | tf_op jit(solution)/shard_map/ppermute | solution.py:969
  68.1 6.5 %collective-permute-done.8 = bf16[3,256,512]{2,1,0:T(8,128)(2,1)S(1)} collective-permute-done((bf16[3,256,512]{2,1,0:T(8,128)(2,1)S(1)}, bf16[3,256,512]{2,1,0:T(8,128)(2,1)S(1)}, u32[]{:S(2)}, u32[]{:S(2)}) %collective-permute-start.8) | collective-permute-done | bytes 786464 | tf_op jit(solution)/shard_map/ppermute | solution.py:826
  89.8 8.2 %collective-permute-done.11.refs_3_ = bf16[256,512]{1,0:T(8,128)(2,1)} collective-permute-done((bf16[256,512]{1,0:T(8,128)(2,1)S(1)}, bf16[256,512]{1,0:T(8,128)(2,1)}, u32[]{:S(2)}, u32[]{:S(2)}) %collective-permute-start.11) | collective-permute-done | bytes 262176 | tf_op jit(solution)/shard_map/ppermute | solution.py:791
  98.0 5.8 %collective-permute-start.15 = (bf16[256,2048]{1,0:T(8,128)(2,1)}, bf16[256,2048]{1,0:T(8,128)(2,1)}, u32[]{:S(2)}, u32[]{:S(2)}) collective-permute-start(bf16[256,2048]{1,0:T(8,128)(2,1)} %constant_dynamic-slice_fusion.6), channel_id=1, source_target_pairs={{0,8},{8,0},{16,24},{24,16},{1,9},{9,1},{17,25},{25,17},{2,10},{10... | collective-permute-start | bytes 3145736 | tf_op jit(solution)/shard_map/ppermute | solution.py:811
  118.7 10.3 %project.1.q_ref.k_ref.v_ref.fk_ref.fv_ref = bf16[768,2560]{1,0:T(8,128)(2,1)S(1)} custom-call(bf16[768,2176]{1,0:T(8,128)(2,1)S(1)} %copy-done.13, bf16[768,2176]{1,0:T(8,128)(2,1)S(1)} %copy-done.22, f32[1,1536]{1,0:T(1,128)S(1)} %broadcast_in_dim.114.refs_2_, bf16[2176,1536]{1,0:T(8,128)(2,1)S(1)} %copy-done.4), custom_call_target="tpu_custom_call" | custom-call | flops 1 | bytes 1 | tf_op jit(solution)/shard_map/project/pallas_call | solution.py:705
  138.0 12.3 %attend_forward.1 = (f32[768,512]{1,0:T(8,128)S(1)}, bf16[768,512]{1,0:T(8,128)(2,1)S(1)}, bf16[4,768,768]{2,1,0:T(8,128)(2,1)}, bf16[4,768,768]{2,1,0:T(8,128)(2,1)}) custom-call(bf16[768,2560]{1,0:T(8,128)(2,1)S(1)} %copy-done.1, bf16[768,2560]{1,0:T(8,128)(2,1)S(1)} %copy-done.1, bf16[768,2560]{1,0:T(8,128)(2,1)S(1)} %copy-done.1, ...), custom_call_target="tpu_custom_call" | custom-call | flops 1 | bytes 1 | tf_op jit(solution)/shard_map/attend_forward/pallas_call | solution.py:106
  154.8 4.9 %collective-permute-done.22 = bf16[256,2048]{1,0:T(8,128)(2,1)} collective-permute-done((bf16[256,2048]{1,0:T(8,128)(2,1)}, bf16[256,2048]{1,0:T(8,128)(2,1)}, u32[]{:S(2)}, u32[]{:S(2)}) %collective-permute-start.22) | collective-permute-done | bytes 1048608 | tf_op jit(solution)/shard_map/ppermute | solution.py:817
  169.7 15.2 %collective-permute-done.25 = bf16[256,2048]{1,0:T(8,128)(2,1)} collective-permute-done((bf16[256,2048]{1,0:T(8,128)(2,1)}, bf16[256,2048]{1,0:T(8,128)(2,1)}, u32[]{:S(2)}, u32[]{:S(2)}) %collective-permute-start.25) | collective-permute-done | bytes 1048608 | tf_op jit(solution)/shard_map/ppermute | solution.py:826
  192.1 14.8 %collective-permute-done.28.refs_1_ = bf16[1024,512]{1,0:T(8,128)(2,1)} collective-permute-done((bf16[1024,512]{1,0:T(8,128)(2,1)}, bf16[1024,512]{1,0:T(8,128)(2,1)}, u32[]{:S(2)}, u32[]{:S(2)}) %collective-permute-start.28) | collective-permute-done | bytes 1048608 | tf_op jit(solution)/shard_map/ppermute | solution.py:811
  217.1 18.4 %collective-permute-done.31 = bf16[1024,512]{1,0:T(8,128)(2,1)S(1)} collective-permute-done((bf16[1024,512]{1,0:T(8,128)(2,1)}, bf16[1024,512]{1,0:T(8,128)(2,1)S(1)}, u32[]{:S(2)}, u32[]{:S(2)}) %collective-permute-start.31) | collective-permute-done | bytes 1048608 | tf_op jit(solution)/shard_map/ppermute | solution.py:817
  240.1 5.1 %after_attention.1 = (f32[384,2048]{1,0:T(8,128)S(1)}, bf16[384,2176]{1,0:T(8,128)(2,1)S(1)}) custom-call(s32[1]{0:T(128)} %bitcast.half_ref.core_ref, s32[3]{0:T(128)S(1)} %get-tuple-element.206.slot_ref, bf16[384,2176]{1,0:T(8,128)(2,1)} %join.4.refs_0_, bf16[384,2176]{1,0:T(8,128)(2,1)} %collective-permute-done.21.refs_1_, ...), custom_call_target="tpu_custom_call" | custom-call | flops 1 | bytes 1 | tf_op jit(solution)/shard_map/after_attention/pallas_call | solution.py:349
  249.2 6.1 %collective-permute-done.35.refs_4_ = bf16[1024,512]{1,0:T(8,128)(2,1)} collective-permute-done((bf16[1024,512]{1,0:T(8,128)(2,1)S(1)}, bf16[1024,512]{1,0:T(8,128)(2,1)}, u32[]{:S(2)}, u32[]{:S(2)}) %collective-permute-start.35) | collective-permute-done | bytes 1048608 | tf_op jit(solution)/shard_map/ppermute | solution.py:825
  267.7 11.6 %expand.1 = (bf16[768,2048]{1,0:T(8,128)(2,1)S(1)}, bf16[768,2048]{1,0:T(8,128)(2,1)S(1)}) custom-call(bf16[384,2176]{1,0:T(8,128)(2,1)S(1)} %get-tuple-element.117.own_ref.two_a, bf16[384,2176]{1,0:T(8,128)(2,1)} %collective-permute-done.30.other_ref.two_b, bf16[2176,2048]{1,0:T(8,128)(2,1)S(1)} %assemble.6.w_ref, f32[1,2048]{1,0:T(1,128)S(1)} %bitcast.78), custom_call_target="tpu_custom_call" | custom-call | flops 1 | bytes 1 | tf_op jit(solution)/shard_map/expand/pallas_call | solution.py:739
  282.1 8.6 %back_hidden.1.x_ref.gp_ref = bf16[768,2048]{1,0:T(8,128)(2,1)S(1)} custom-call(bf16[768,2176]{1,0:T(8,128)(2,1)S(1)} %pad_maximum_fusion.x_ref, bf16[2048,2176]{1,0:T(8,128)(2,1)S(1)} %assemble.7.w_ref, bf16[768,2048]{1,0:T(8,128)(2,1)S(1)} %get-tuple-element.132.s_ref), custom_call_target="tpu_custom_call" | custom-call | flops 1 | bytes 1 | tf_op jit(solution)/shard_map/back_hidden/pallas_call | solution.py:766
  290.7 5.3 %matmul.9 = bf16[384,2176]{1,0:T(8,128)(2,1)S(1)} custom-call(s32[1]{0:T(128)} %constant.159.clone.1.half_ref, bf16[768,2048]{1,0:T(8,128)(2,1)S(1)} %back_hidden.1.x_ref.gp_ref, bf16[2176,2048]{1,0:T(8,128)(2,1)S(1)} %assemble.6.w_ref), custom_call_target="tpu_custom_call" | custom-call | flops 1 | bytes 1 | tf_op jit(solution)/shard_map/matmul/pallas_call | solution.py:884
  296.1 5.5 %matmul.8.a_ref = bf16[384,2176]{1,0:T(8,128)(2,1)S(1)} custom-call(s32[1]{0:T(128)} %constant.146.clone.1.half_ref, bf16[768,2048]{1,0:T(8,128)(2,1)S(1)} %back_hidden.1.x_ref.gp_ref, bf16[2176,2048]{1,0:T(8,128)(2,1)S(1)} %assemble.6.w_ref), custom_call_target="tpu_custom_call" | custom-call | flops 1 | bytes 1 | tf_op jit(solution)/shard_map/matmul/pallas_call | solution.py:884
  315.0 26.2 %collective-permute-done.40.refs_1_ = bf16[384,2176]{1,0:T(8,128)(2,1)S(1)} collective-permute-done((bf16[384,2176]{1,0:T(8,128)(2,1)S(1)}, bf16[384,2176]{1,0:T(8,128)(2,1)S(1)}, u32[]{:S(2)}, u32[]{:S(2)}) %collective-permute-start.40) | collective-permute-done | bytes 1671200 | tf_op jit(solution)/shard_map/ppermute | solution.py:969
  352.5 13.5 %attend_backward.1 = (bf16[768,512]{1,0:T(8,128)(2,1)S(1)}, bf16[768,512]{1,0:T(8,128)(2,1)S(1)}, bf16[768,512]{1,0:T(8,128)(2,1)S(1)}, bf16[2,768,512]{2,1,0:T(8,128)(2,1)S(1)}) custom-call(bf16[768,2560]{1,0:T(8,128)(2,1)S(1)} %copy-done.2, bf16[768,2560]{1,0:T(8,128)(2,1)S(1)} %copy-done.2, bf16[768,2560]{1,0:T(8,128)(2,1)S(1)} %copy-done.2, ...), custom_call_target="tpu_custom_call" | custom-call | flops 1 | bytes 1 | tf_op jit(solution)/shard_map/attend_backward/pallas_call | solution.py:181
  367.3 18.7 %collective-permute-done.41.refs_1_ = bf16[384,2176]{1,0:T(8,128)(2,1)} collective-permute-done((bf16[384,2176]{1,0:T(8,128)(2,1)}, bf16[384,2176]{1,0:T(8,128)(2,1)}, u32[]{:S(2)}, u32[]{:S(2)}) %collective-permute-start.41) | collective-permute-done | bytes 1671200 | tf_op jit(solution)/shard_map/ppermute | solution.py:969
  388.0 5.4 %after_hidden.1 = (bf16[384,2048]{1,0:T(8,128)(2,1)}, bf16[384,128]{1,0:T(8,128)(2,1)S(1)}) custom-call(s32[1]{0:T(128)} %bitcast.half_ref.core_ref, s32[3]{0:T(128)S(1)} %get-tuple-element.206.slot_ref, bf16[384,2176]{1,0:T(8,128)(2,1)} %join.6.refs_0_, bf16[384,2176]{1,0:T(8,128)(2,1)} %collective-permute-done.41.refs_1_, f32[384,2048]{1,0:T(8,128)S(1)} %copy-done.25, ...), custom_call_target="tpu_custom_call" | custom-call | flops 1 | bytes 1 | tf_op jit(solution)/shard_map/after_hidden/pallas_call | solution.py:349
  405.7 5.6 %back_project.1 = (bf16[384,2048]{1,0:T(8,128)(2,1)S(1)}, bf16[384,2048]{1,0:T(8,128)(2,1)S(1)}) custom-call(s32[1]{0:T(128)} %bitcast.half_ref.core_ref, bf16[768,1536]{1,0:T(8,128)(2,1)S(1)} %pad_maximum_fusion.1.x_ref.gq_ref, bf16[2176,1536]{1,0:T(8,128)(2,1)S(1)} %bitcast.77), custom_call_target="tpu_custom_call" | custom-call | flops 1 | bytes 1 | tf_op jit(solution)/shard_map/back_project/pallas_call | solution.py:406
  417.2 4.9 %collective-permute-done.48 = bf16[768,128]{1,0:T(8,128)(2,1)S(1)} collective-permute-done((bf16[768,128]{1,0:T(8,128)(2,1)S(1)}, bf16[768,128]{1,0:T(8,128)(2,1)S(1)}, u32[]{:S(2)}, u32[]{:S(2)}) %collective-permute-start.48) | collective-permute-done | bytes 196640 | tf_op jit(solution)/shard_map/ppermute | solution.py:969
  451.5 7.2 %collective-permute-done.49.refs_1_ = bf16[384,2048]{1,0:T(8,128)(2,1)} collective-permute-done((bf16[384,2048]{1,0:T(8,128)(2,1)}, bf16[384,2048]{1,0:T(8,128)(2,1)}, u32[]{:S(2)}, u32[]{:S(2)}) %collective-permute-start.49) | collective-permute-done | bytes 1572896 | tf_op jit(solution)/shard_map/ppermute | solution.py:969
  (381 shorter events, 218.4 us)
Async XLA Ops:
  24.3 22.2 %collective-permute-start.5 = (bf16[3,256,512]{2,1,0:T(8,128)(2,1)}, bf16[3,256,512]{2,1,0:T(8,128)(2,1)S(1)}, u32[]{:S(2)}, u32[]{:S(2)}) collective-permute-start(bf16[3,256,512]{2,1,0:T(8,128)(2,1)} %collective-permute-done.1.refs_1_), channel_id=1, source_target_pairs={{0,4},{4,0},{1,5},{5,1},{2,6},{6,2},{3,7},{7,3},{8,12},{12,8},{9,1... | collective-permute-start | bytes 2359304 | tf_op jit(solution)/shard_map/ppermute | solution.py:816
  26.1 24.8 %collective-permute-start.3 = (bf16[3,256,512]{2,1,0:T(8,128)(2,1)}, bf16[3,256,512]{2,1,0:T(8,128)(2,1)S(1)}, u32[]{:S(2)}, u32[]{:S(2)}) collective-permute-start(bf16[3,256,512]{2,1,0:T(8,128)(2,1)} %collective-permute-done.2), channel_id=1, source_target_pairs={{8,0},{16,24},{9,1},{17,25},{10,2},{18,26},{11,3},{19,27},{12,4},{... | collective-permute-start | bytes 2359304 | tf_op jit(solution)/shard_map/ppermute | solution.py:817
  52.5 22.1 %collective-permute-start.13 = (bf16[3,256,512]{2,1,0:T(8,128)(2,1)S(1)}, bf16[3,256,512]{2,1,0:T(8,128)(2,1)S(1)}, u32[]{:S(2)}, u32[]{:S(2)}) collective-permute-start(bf16[3,256,512]{2,1,0:T(8,128)(2,1)S(1)} %broadcast_select_fusion.5.refs_3_), channel_id=1, source_target_pairs={{0,4},{4,0},{1,5},{5,1},{2,6},{6,2},{3,7},{7,3},{8,12},{12,8},{9,1... | collective-permute-start | bytes 2359304 | tf_op jit(solution)/shard_map/ppermute | solution.py:825
  74.7 23.3 %collective-permute-start.14 = (bf16[3,256,512]{2,1,0:T(8,128)(2,1)S(1)}, bf16[3,256,512]{2,1,0:T(8,128)(2,1)S(1)}, u32[]{:S(2)}, u32[]{:S(2)}) collective-permute-start(bf16[3,256,512]{2,1,0:T(8,128)(2,1)S(1)} %broadcast_select_fusion.4.refs_5_), channel_id=1, source_target_pairs={{0,4},{4,0},{1,5},{5,1},{2,6},{6,2},{3,7},{7,3},{8,12},{12,8},{9,1... | collective-permute-start | bytes 2359304 | tf_op jit(solution)/shard_map/ppermute | solution.py:833
  98.0 32.9 %collective-permute-start.15 = (bf16[256,2048]{1,0:T(8,128)(2,1)}, bf16[256,2048]{1,0:T(8,128)(2,1)}, u32[]{:S(2)}, u32[]{:S(2)}) collective-permute-start(bf16[256,2048]{1,0:T(8,128)(2,1)} %constant_dynamic-slice_fusion.6), channel_id=1, source_target_pairs={{0,8},{8,0},{16,24},{24,16},{1,9},{9,1},{17,25},{25,17},{2,10},{10... | collective-permute-start | bytes 3145736 | tf_op jit(solution)/shard_map/ppermute | solution.py:811
  103.8 27.1 %collective-permute-start.16 = (bf16[256,2048]{1,0:T(8,128)(2,1)}, bf16[256,2048]{1,0:T(8,128)(2,1)}, u32[]{:S(2)}, u32[]{:S(2)}) collective-permute-start(bf16[256,2048]{1,0:T(8,128)(2,1)} %constant_dynamic-slice_fusion.6), channel_id=1, source_target_pairs={{8,16},{16,8},{9,17},{17,9},{10,18},{18,10},{11,19},{19,11},{12,20... | collective-permute-start | bytes 3145736 | tf_op jit(solution)/shard_map/ppermute | solution.py:812
  106.1 24.8 %collective-permute-start.17 = (bf16[256,512]{1,0:T(8,128)(2,1)}, bf16[256,512]{1,0:T(8,128)(2,1)}, u32[]{:S(2)}, u32[]{:S(2)}) collective-permute-start(bf16[256,512]{1,0:T(8,128)(2,1)} %collective-permute-done.10.refs_1_), channel_id=1, source_target_pairs={{0,4},{4,0},{1,5},{5,1},{2,6},{6,2},{3,7},{7,3},{8,12},{12,8},{9,1... | collective-permute-start | bytes 786440 | tf_op jit(solution)/shard_map/ppermute | solution.py:796
  106.7 24.2 %collective-permute-start.18 = (bf16[256,512]{1,0:T(8,128)(2,1)}, bf16[256,512]{1,0:T(8,128)(2,1)}, u32[]{:S(2)}, u32[]{:S(2)}) collective-permute-start(bf16[256,512]{1,0:T(8,128)(2,1)} %collective-permute-done.11.refs_3_), channel_id=1, source_target_pairs={{0,4},{4,0},{1,5},{5,1},{2,6},{6,2},{3,7},{7,3},{8,12},{12,8},{9,1... | collective-permute-start | bytes 786440 | tf_op jit(solution)/shard_map/ppermute | solution.py:796
  108.2 22.7 %collective-permute-start.19 = (bf16[256,512]{1,0:T(8,128)(2,1)}, bf16[256,512]{1,0:T(8,128)(2,1)}, u32[]{:S(2)}, u32[]{:S(2)}) collective-permute-start(bf16[256,512]{1,0:T(8,128)(2,1)} %collective-permute-done.12.refs_5_), channel_id=1, source_target_pairs={{0,4},{4,0},{1,5},{5,1},{2,6},{6,2},{3,7},{7,3},{8,12},{12,8},{9,1... | collective-permute-start | bytes 786440 | tf_op jit(solution)/shard_map/ppermute | solution.py:796
  130.9 28.8 %collective-permute-start.23 = (bf16[256,2048]{1,0:T(8,128)(2,1)}, bf16[256,2048]{1,0:T(8,128)(2,1)}, u32[]{:S(2)}, u32[]{:S(2)}) collective-permute-start(bf16[256,2048]{1,0:T(8,128)(2,1)} %collective-permute-done.15.refs_1_), channel_id=1, source_target_pairs={{8,16},{16,8},{9,17},{17,9},{10,18},{18,10},{11,19},{19,11},{12,20... | collective-permute-start | bytes 3145736 | tf_op jit(solution)/shard_map/ppermute | solution.py:818
  132.6 27.1 %collective-permute-start.24 = (bf16[256,2048]{1,0:T(8,128)(2,1)}, bf16[256,2048]{1,0:T(8,128)(2,1)}, u32[]{:S(2)}, u32[]{:S(2)}) collective-permute-start(bf16[256,2048]{1,0:T(8,128)(2,1)} %collective-permute-done.15.refs_1_), channel_id=1, source_target_pairs={{0,4},{4,0},{1,5},{5,1},{2,6},{6,2},{3,7},{7,3},{8,12},{12,8},{9,1... | collective-permute-start | bytes 3145736 | tf_op jit(solution)/shard_map/ppermute | solution.py:816
  134.1 25.6 %collective-permute-start.22 = (bf16[256,2048]{1,0:T(8,128)(2,1)}, bf16[256,2048]{1,0:T(8,128)(2,1)}, u32[]{:S(2)}, u32[]{:S(2)}) collective-permute-start(bf16[256,2048]{1,0:T(8,128)(2,1)} %collective-permute-done.16), channel_id=1, source_target_pairs={{8,0},{16,24},{9,1},{17,25},{10,2},{18,26},{11,3},{19,27},{12,4},{... | collective-permute-start | bytes 3145736 | tf_op jit(solution)/shard_map/ppermute | solution.py:817
  159.7 25.2 %collective-permute-start.25 = (bf16[256,2048]{1,0:T(8,128)(2,1)}, bf16[256,2048]{1,0:T(8,128)(2,1)}, u32[]{:S(2)}, u32[]{:S(2)}) collective-permute-start(bf16[256,2048]{1,0:T(8,128)(2,1)} %collective-permute-done.23), channel_id=1, source_target_pairs={{8,0},{16,24},{9,1},{17,25},{10,2},{18,26},{11,3},{19,27},{12,4},{... | collective-permute-start | bytes 3145736 | tf_op jit(solution)/shard_map/ppermute | solution.py:826
  163.3 23.3 %collective-permute-start.26 = (bf16[256,2048]{1,0:T(8,128)(2,1)}, bf16[256,2048]{1,0:T(8,128)(2,1)}, u32[]{:S(2)}, u32[]{:S(2)}) collective-permute-start(bf16[256,2048]{1,0:T(8,128)(2,1)} %broadcast_select_fusion.3.refs_3_), channel_id=1, source_target_pairs={{0,4},{4,0},{1,5},{5,1},{2,6},{6,2},{3,7},{7,3},{8,12},{12,8},{9,1... | collective-permute-start | bytes 3145736 | tf_op jit(solution)/shard_map/ppermute | solution.py:825
  168.1 42.5 %collective-permute-start.21 = (bf16[384,2176]{1,0:T(8,128)(2,1)}, bf16[384,2176]{1,0:T(8,128)(2,1)}, u32[]{:S(2)}, u32[]{:S(2)}) collective-permute-start(bf16[384,2176]{1,0:T(8,128)(2,1)} %join.4.refs_0_), channel_id=1, source_target_pairs={{0,2},{2,0},{1,3},{3,1},{4,6},{6,4},{5,7},{7,5},{8,10},{10,8},{9,1... | collective-permute-start | bytes 5013512 | tf_op jit(solution)/shard_map/ppermute | solution.py:969
  184.9 21.9 %collective-permute-start.29 = (bf16[1024,512]{1,0:T(8,128)(2,1)}, bf16[1024,512]{1,0:T(8,128)(2,1)}, u32[]{:S(2)}, u32[]{:S(2)}) collective-permute-start(bf16[1024,512]{1,0:T(8,128)(2,1)} %constant_dynamic-slice_fusion.3), channel_id=1, source_target_pairs={{8,16},{16,8},{9,17},{17,9},{10,18},{18,10},{11,19},{19,11},{12,20... | collective-permute-start | bytes 3145736 | tf_op jit(solution)/shard_map/ppermute | solution.py:812
  210.6 24.9 %collective-permute-start.32 = (bf16[1024,512]{1,0:T(8,128)(2,1)}, bf16[1024,512]{1,0:T(8,128)(2,1)}, u32[]{:S(2)}, u32[]{:S(2)}) collective-permute-start(bf16[1024,512]{1,0:T(8,128)(2,1)} %collective-permute-done.28.refs_1_), channel_id=1, source_target_pairs={{8,16},{16,8},{9,17},{17,9},{10,18},{18,10},{11,19},{19,11},{12,20... | collective-permute-start | bytes 3145736 | tf_op jit(solution)/shard_map/ppermute | solution.py:818
  212.2 23.3 %collective-permute-start.33 = (bf16[1024,512]{1,0:T(8,128)(2,1)}, bf16[1024,512]{1,0:T(8,128)(2,1)S(1)}, u32[]{:S(2)}, u32[]{:S(2)}) collective-permute-start(bf16[1024,512]{1,0:T(8,128)(2,1)} %collective-permute-done.28.refs_1_), channel_id=1, source_target_pairs={{0,4},{4,0},{1,5},{5,1},{2,6},{6,2},{3,7},{7,3},{8,12},{12,8},{9,1... | collective-permute-start | bytes 3145736 | tf_op jit(solution)/shard_map/ppermute | solution.py:816
  212.7 22.8 %collective-permute-start.31 = (bf16[1024,512]{1,0:T(8,128)(2,1)}, bf16[1024,512]{1,0:T(8,128)(2,1)S(1)}, u32[]{:S(2)}, u32[]{:S(2)}) collective-permute-start(bf16[1024,512]{1,0:T(8,128)(2,1)} %collective-permute-done.29), channel_id=1, source_target_pairs={{8,0},{16,24},{9,1},{17,25},{10,2},{18,26},{11,3},{19,27},{12,4},{... | collective-permute-start | bytes 3145736 | tf_op jit(solution)/shard_map/ppermute | solution.py:817
  302.3 38.9 %collective-permute-start.40 = (bf16[384,2176]{1,0:T(8,128)(2,1)S(1)}, bf16[384,2176]{1,0:T(8,128)(2,1)S(1)}, u32[]{:S(2)}, u32[]{:S(2)}) collective-permute-start(bf16[384,2176]{1,0:T(8,128)(2,1)S(1)} %join.5.refs_0_), channel_id=1, source_target_pairs={{0,2},{2,0},{1,3},{3,1},{4,6},{6,4},{5,7},{7,5},{8,10},{10,8},{9,1... | collective-permute-start | bytes 5013512 | tf_op jit(solution)/shard_map/ppermute | solution.py:969
  346.8 39.2 %collective-permute-start.41 = (bf16[384,2176]{1,0:T(8,128)(2,1)}, bf16[384,2176]{1,0:T(8,128)(2,1)}, u32[]{:S(2)}, u32[]{:S(2)}) collective-permute-start(bf16[384,2176]{1,0:T(8,128)(2,1)} %join.6.refs_0_), channel_id=1, source_target_pairs={{0,2},{2,0},{1,3},{3,1},{4,6},{6,4},{5,7},{7,5},{8,10},{10,8},{9,1... | collective-permute-start | bytes 5013512 | tf_op jit(solution)/shard_map/ppermute | solution.py:969
  365.9 38.3 %collective-permute-start.45 = (bf16[2,768,512]{2,1,0:T(8,128)(2,1)S(1)}, bf16[2,768,512]{2,1,0:T(8,128)(2,1)S(1)}, u32[]{:S(2)}, u32[]{:S(2)}) collective-permute-start(bf16[2,768,512]{2,1,0:T(8,128)(2,1)S(1)} %get-tuple-element.148), channel_id=1, source_target_pairs={{4,0},{5,1},{6,2},{7,3},{12,8},{13,9},{14,10},{15,11},{20,16},{21,... | collective-permute-start | bytes 4718600 | tf_op jit(solution)/shard_map/ppermute | solution.py:969
  415.7 27.6 %collective-permute-start.42 = (bf16[384,2048]{1,0:T(8,128)(2,1)}, bf16[384,2048]{1,0:T(8,128)(2,1)}, u32[]{:S(2)}, u32[]{:S(2)}) collective-permute-start(bf16[384,2048]{1,0:T(8,128)(2,1)} %get-tuple-element.138.own_ref), channel_id=1, source_target_pairs={{0,1},{1,0},{2,3},{3,2},{4,5},{5,4},{6,7},{7,6},{8,9},{9,8},{10,11... | collective-permute-start | bytes 4718600 | tf_op jit(solution)/shard_map/ppermute | solution.py:969
  422.8 35.9 %collective-permute-start.49 = (bf16[384,2048]{1,0:T(8,128)(2,1)}, bf16[384,2048]{1,0:T(8,128)(2,1)}, u32[]{:S(2)}, u32[]{:S(2)}) collective-permute-start(bf16[384,2048]{1,0:T(8,128)(2,1)} %join.7.refs_0_), channel_id=1, source_target_pairs={{0,2},{2,0},{1,3},{3,1},{4,6},{6,4},{5,7},{7,5},{8,10},{10,8},{9,1... | collective-permute-start | bytes 4718600 | tf_op jit(solution)/shard_map/ppermute | solution.py:969
  (115 other events, 1398.8 us)
